TPU v7x, 32 devices: a whole 2x2x4 slice. The times are simulated.
32 devices in a mesh: gx: 8 (over z, x), gy: 4 (over y, core).
Axes of the slice: x: 2, y: 2, z: 4, core: 2. Of those that a mesh axis runs over, the one named last changes fastest.
Arguments:
- ensemble: float32 [16, 512, 1024], P('gx', None, 'gy'), may hold values from -6 to 6
- obs_values: float32 [4, 128], replicated, may hold values from -6 to 6
- obs_error: float32 [4, 128], replicated, may hold values from 0.3 to 3
- tile_weight: float32 [4, 128, 8, 4], P(None, None, 'gx', 'gy'), may hold values from 0.2 to 1
- owner_device: int32 [4], replicated, may hold values from 0 to 31
- obs_cells: int32 [4, 128], replicated, may hold values from 0 to 16383
Outputs:
- analysis_ensemble: float32 [16, 512, 1024], P('gx', None, 'gy')
Inputs may be any that keep to these rules, and one draw needn't show every extreme that they name: `owner_device`: device numbers count gy fastest: the device at index i of gx and j of gy is number i times the length of gy plus j. `obs_cells`: cell c of a tile lies c // 256 cells along the first direction and c % 256 along the second from the tile's first cell; cells may repeat.
All inputs are finite; a program needn't handle non-finite values.
Results may differ from a plain program's by a relative error of at most 0.00015.
Values sent between devices are 32-bit elements; how exact they have to be, the bound alone decides.
No kernel may reach another device: no remote copies, remote signals or barrier semaphores. Data moves between devices by JAX's collectives and lax.ppermute only.
A program may use at most 64 MiB of HBM per device.

v0:
```python
import math

import jax
import jax.numpy as jnp
from jax import lax
from jax.sharding import PartitionSpec as P

EPSILON = 1e-06
PRECISE = lax.Precision.HIGHEST


def spread_2(shard, axis, root):
    mine = lax.axis_index(axis) == root
    return lax.psum(jnp.where(mine, shard, jnp.zeros_like(shard)), axis)


def analysis(prior_ens, values, errors):
    members = prior_ens.shape[1]
    average = jnp.mean(prior_ens, axis=1, keepdims=True)
    anomaly = prior_ens - average
    spread = jnp.sum(anomaly * anomaly, axis=1, keepdims=True) / (members - 1) + EPSILON
    obs_noise = errors[:, None]
    post_var = 1.0 / (1.0 / spread + 1.0 / obs_noise)
    post_mean = post_var * (average / spread + values[:, None] / obs_noise)
    increment = post_mean - average + (jnp.sqrt(post_var / spread) - 1.0) * anomaly
    return (anomaly, spread, increment)


def regression(
    state_cols,
    anomaly,
    spread,
    increment,
    weight_cols,
    obs_xpos,
    obs_ypos,
    grid_xpos,
    grid_ypos,
    radius,
):
    members = state_cols.shape[0]
    deviation = state_cols - jnp.mean(state_cols, axis=0, keepdims=True)
    covariance = jnp.dot(anomaly, deviation, precision=PRECISE) / (members - 1)
    distance = (grid_xpos[None, :] - obs_xpos[:, None]) ** 2 + (
        grid_ypos[None, :] - obs_ypos[:, None]
    ) ** 2
    tapering = 1.0 / (1.0 + distance / radius)
    gain_rows = covariance * (tapering * weight_cols) / spread
    return state_cols + jnp.dot(increment.T, gain_rows, precision=PRECISE)


def blocked_regression(
    state_cols,
    anomaly,
    spread,
    increment,
    weight_cols,
    obs_xpos,
    obs_ypos,
    grid_xpos,
    grid_ypos,
    radius,
):
    members, cell_count = state_cols.shape
    breadth = math.gcd(cell_count, 512)
    pieces = cell_count // breadth
    stacked = state_cols.reshape(members, pieces, breadth).transpose(1, 0, 2)
    row_coords = grid_xpos.reshape(pieces, breadth)
    col_coords = grid_ypos.reshape(pieces, breadth)

    def update_piece(element):
        states, rows_here, cols_here = element
        return regression(
            states,
            anomaly,
            spread,
            increment,
            weight_cols,
            obs_xpos,
            obs_ypos,
            rows_here,
            cols_here,
            radius,
        )

    updated = lax.map(update_piece, (stacked, row_coords, col_coords))
    return updated.transpose(1, 0, 2).reshape(members, cell_count)


def local(ensemble, obs_values, obs_error, tile_weight, owner_device, obs_cells):
    gx_count = lax.axis_size("gx")
    gy_count = lax.axis_size("gy")
    members = ensemble.shape[0] * gx_count
    tile_rows = ensemble.shape[1] // gx_count
    tile_cols = ensemble.shape[2]
    cell_count = tile_rows * tile_cols
    radius = float((tile_rows * gx_count // 4) ** 2)
    row_index = lax.axis_index("gx")
    col_index = lax.axis_index("gy")
    cell_ids = jnp.arange(cell_count, dtype=jnp.int32)
    grid_xpos = (row_index * tile_rows + cell_ids // tile_cols).astype(jnp.float32)
    grid_ypos = (col_index * tile_cols + cell_ids % tile_cols).astype(jnp.float32)
    batches = obs_cells.shape[0]
    upcoming = None
    tile_state = lax.all_to_all(ensemble, "gx", split_axis=1, concat_axis=0, tiled=True).reshape(
        members, cell_count
    )
    for batch in range(batches):
        observed = obs_cells[batch]
        if batch == 0:
            own_prior = jnp.take(tile_state, observed, axis=1).T
        else:
            own_prior = upcoming
        root_index = owner_device[batch]
        prior_ens = spread_2(own_prior, ("gx", "gy"), root_index)
        anomaly, spread, increment = analysis(prior_ens, obs_values[batch], obs_error[batch])
        obs_xpos = (root_index // gy_count * tile_rows + observed // tile_cols).astype(jnp.float32)
        obs_ypos = (root_index % gy_count * tile_cols + observed % tile_cols).astype(jnp.float32)
        weight_cols = tile_weight[batch, :, 0, 0][:, None]
        if batch + 1 < batches:
            following = obs_cells[batch + 1]
            picked = jnp.take(tile_state, following, axis=1)
            upcoming = regression(
                picked,
                anomaly,
                spread,
                increment,
                weight_cols,
                obs_xpos,
                obs_ypos,
                jnp.take(grid_xpos, following),
                jnp.take(grid_ypos, following),
                radius,
            ).T
        tile_state = blocked_regression(
            tile_state,
            anomaly,
            spread,
            increment,
            weight_cols,
            obs_xpos,
            obs_ypos,
            grid_xpos,
            grid_ypos,
            radius,
        )
    result = lax.all_to_all(
        tile_state.reshape(members, tile_rows, tile_cols),
        "gx",
        split_axis=0,
        concat_axis=1,
        tiled=True,
    )
    return result


def solution(mesh):
    placed = (P("gx", None, "gy"), P(), P(), P(None, None, "gx", "gy"), P(), P())
    return jax.shard_map(
        local, mesh=mesh, in_specs=placed, out_specs=P("gx", None, "gy"), check_vma=False
    )
```

profile of v0, /device:TPU:0, one launch (start us, length us, event | category | flops | bytes accessed | tf_op | source)
XLA Modules:
  0.0 399.0 jit_solution(14153259270426064827)
XLA Ops:
  0.0 3.0 copy.37
  3.0 7.3 %all-to-all-start = ((f32[2,512,256]{2,0,1:T(2,128)}), f32[2,512,256]{2,0,1:T(2,128)S(1)}, u32[]{:S(2)}, u32[]{:S(2)}) async-start(f32[2,512,256]{2,0,1:T(2,128)} %copy.37), calls=%async_computation | async-start | bytes 2097152 | tf_op jit(solution)/shard_map/all_to_all | solution.py:105
  10.3 1.5 fusion.99
  25.3 1.1 gather_fusion.9
  26.4 1.1 gather_fusion.6
  27.6 1.1 gather_fusion.8
  28.8 1.1 gather_fusion.5
  34.1 2.0 all-to-all-done
  37.1 4.6 %copy.39 = f32[16,16384]{0,1:T(8,128)} copy(f32[16,16384]{1,0:T(8,128)S(1)} %bitcast.405) | data formatting | bytes 2097152 | tf_op jit(solution)/shard_map/reshape | solution.py:105
  41.7 4.0 %gather_fusion.1 = f32[128,16]{1,0:T(8,128)S(1)} fusion(f32[16,16384]{0,1:T(8,128)} %copy.39, s32[1024]{0:T(1024)S(1)} %pad_clamp_fusion.2), kind=kCustom, calls=%fused_computation.2.clone | custom fusion | bytes 16896 | tf_op jit(solution)/shard_map/jit(_take)/gather | solution.py:122
  45.7 4.0 %gather_fusion = f32[128,16]{1,0:T(8,128)S(1)} fusion(f32[16,16384]{0,1:T(8,128)} %copy.39, s32[1024]{0:T(1024)S(1)} %pad_clamp_fusion.3), kind=kCustom, calls=%fused_computation.clone | custom fusion | bytes 16896 | tf_op jit(solution)/shard_map/jit(_take)/gather | solution.py:111
  49.9 38.8 %psum.28 = f32[128,16]{0,1:T(8,128)S(1)} all-reduce(f32[128,16]{0,1:T(8,128)S(1)} %fusion.65), channel_id=1, replica_groups=mesh['gx'=8,'gy'=4] {'gx','gy'}, use_global_device_ids=true, to_apply=%region_0.2 | all-reduce | flops 2048 | bytes 16384 | tf_op jit(solution)/shard_map/psum | solution.py:14
  89.0 35.3 %while.40 = (s32[]{:T(128)}, f32[32,16,512]{2,1,0:T(8,128)S(1)}, f32[32,16,512]{2,0,1:T(8,128)S(1)}, f32[128,16]{0,1:T(8,128)S(1)}, f32[32,512]{1,0:T(8,128)S(1)...) while((s32[]{:T(128)}, f32[32,16,512]{2,1,0:T(8,128)S(1)}, ...), condition=%wide.region_5.7_spmd, body=%wide.region_3.6_spmd.sunk | while | flops 25976832 | bytes 727177 | solution.py:86
  124.8 40.4 %psum.29 = f32[128,16]{0,1:T(8,128)S(1)} all-reduce(f32[128,16]{0,1:T(8,128)S(1)} %fusion.46), channel_id=1, replica_groups=mesh['gx'=8,'gy'=4] {'gx','gy'}, use_global_device_ids=true, to_apply=%region_7.10 | all-reduce | flops 2048 | bytes 16384 | tf_op jit(solution)/shard_map/psum | solution.py:14
  165.4 34.3 %while.41 = (s32[]{:T(128)}, f32[32,16,512]{2,1,0:T(8,128)S(1)}, f32[32,16,512]{2,1,0:T(8,128)S(1)}, f32[128,16]{0,1:T(8,128)S(1)}, f32[32,512]{1,0:T(8,128)S(1)...) while((s32[]{:T(128)}, f32[32,16,512]{2,1,0:T(8,128)S(1)}, ...), condition=%wide.region_12.15_spmd, body=%wide.region_10.14_spmd.sunk | while | flops 25976832 | bytes 694413 | solution.py:86
  199.7 4.6 %copy.46 = f32[16,32,512]{0,2,1:T(8,128)} copy(f32[16,32,512]{2,0,1:T(8,128)S(1)} %bitcast.404) | data formatting | bytes 2097152 | tf_op jit(solution)/shard_map/transpose | solution.py:87
  204.3 4.0 %gather_fusion.7 = f32[128,16]{1,0:T(8,128)S(1)} fusion(f32[16,16384]{0,1:T(8,128)} %bitcast.402, s32[1024]{0:T(1024)S(1)} %pad_clamp_fusion), kind=kCustom, calls=%fused_computation.4.clone | custom fusion | bytes 16896 | tf_op jit(solution)/shard_map/jit(_take)/gather | solution.py:122
  208.4 4.6 %copy.44 = f32[16,32,512]{0,2,1:T(8,128)} copy(f32[16,32,512]{2,0,1:T(8,128)S(1)} %bitcast.403) | data formatting | bytes 2097152 | tf_op jit(solution)/shard_map/transpose | solution.py:87
  213.1 4.0 %gather_fusion.4 = f32[128,16]{1,0:T(8,128)S(1)} fusion(f32[16,16384]{0,1:T(8,128)} %bitcast.401, s32[1024]{0:T(1024)S(1)} %pad_clamp_fusion.1), kind=kCustom, calls=%fused_computation.3.clone | custom fusion | bytes 16896 | tf_op jit(solution)/shard_map/jit(_take)/gather | solution.py:122
  217.6 39.8 %psum.30 = f32[128,16]{0,1:T(8,128)S(1)} all-reduce(f32[128,16]{0,1:T(8,128)S(1)} %fusion.44), channel_id=1, replica_groups=mesh['gx'=8,'gy'=4] {'gx','gy'}, use_global_device_ids=true, to_apply=%region_14.17 | all-reduce | flops 2048 | bytes 16384 | tf_op jit(solution)/shard_map/psum | solution.py:14
  257.6 34.3 %while.42 = (s32[]{:T(128)}, f32[32,16,512]{2,1,0:T(8,128)S(1)}, f32[32,16,512]{2,1,0:T(8,128)S(1)}, f32[128,16]{0,1:T(8,128)S(1)}, f32[32,512]{1,0:T(8,128)S(1)...) while((s32[]{:T(128)}, f32[32,16,512]{2,1,0:T(8,128)S(1)}, ...), condition=%wide.region_19.22_spmd, body=%wide.region_17.21_spmd.sunk | while | flops 25976832 | bytes 694413 | solution.py:86
  292.4 40.4 %psum.31 = f32[128,16]{0,1:T(8,128)S(1)} all-reduce(f32[128,16]{0,1:T(8,128)S(1)} %fusion.42), channel_id=1, replica_groups=mesh['gx'=8,'gy'=4] {'gx','gy'}, use_global_device_ids=true, to_apply=%region_21.24 | all-reduce | flops 2048 | bytes 16384 | tf_op jit(solution)/shard_map/psum | solution.py:14
  333.0 34.3 %while.43 = (s32[]{:T(128)}, f32[32,16,512]{2,1,0:T(8,128)S(1)}, f32[32,16,512]{2,1,0:T(8,128)S(1)}, f32[128,16]{0,1:T(8,128)S(1)}, f32[32,512]{1,0:T(8,128)S(1)...) while((s32[]{:T(128)}, f32[32,16,512]{2,1,0:T(8,128)S(1)}, ...), condition=%wide.region_26.29_spmd, body=%wide.region_24.28_spmd.sunk | while | flops 25976832 | bytes 694413 | solution.py:86
  368.1 29.8 %all_to_all.33 = f32[16,64,256]{2,1,0:T(8,128)S(1)} all-to-all(f32[16,64,256]{2,1,0:T(8,128)S(1)} %reshape_reshape.7), channel_id=1, replica_groups=mesh['gx'=8,'gy'=4] {'gx'}, dimensions={0} | all-to-all | bytes 2097152 | tf_op jit(solution)/shard_map/all_to_all | solution.py:147
  (709 shorter events, 142.6 us)
Async XLA Ops:
  3.0 33.0 %all-to-all-start = ((f32[2,512,256]{2,0,1:T(2,128)}), f32[2,512,256]{2,0,1:T(2,128)S(1)}, u32[]{:S(2)}, u32[]{:S(2)}) async-start(f32[2,512,256]{2,0,1:T(2,128)} %copy.37), calls=%async_computation | async-start | bytes 2097152 | tf_op jit(solution)/shard_map/all_to_all | solution.py:105
  31.1 57.7 %copy-start = (f32[4,128]{1,0:T(4,128)S(1)}, f32[4,128]{1,0:T(4,128)}, u32[]{:S(2)}) copy-start(f32[4,128]{1,0:T(4,128)} %param.19) | copy-start | bytes 6148
  31.1 57.7 %copy-start.1 = (f32[4,128]{1,0:T(4,128)S(1)}, f32[4,128]{1,0:T(4,128)}, u32[]{:S(2)}) copy-start(f32[4,128]{1,0:T(4,128)} %param.20) | copy-start | bytes 6148
where the time goes:
time: 400 us; the launch traced here: 399 us
  blocking collectives  189 us (47%)
  matrix products  126 us (32%)
  local copies, waits for them, and re-layouts  47.4 us (12%)
  between operations  13.1 us (3%)
  other arithmetic  7.79 us (2%)
  starting transfers between devices  7.28 us (2%)
  loops' own time  5.79 us (1%)
    psum x4, blocking collectives, spread_2(): return lax.psum(jnp.where(mine, shard, jnp.zeros_like(shard)), axis)  159 us
    dot_general x131, matrix products, regression(): covariance = jnp.dot(anomaly, deviation, precision=PRECISE) / (members - 1)  83.5 us
    dot_general x131, matrix products, regression(): return state_cols + jnp.dot(increment.T, gain_rows, precision=PRECISE)  42.9 us
    all_to_all x1, blocking collectives, local(): lax.all_to_all(tile_state.reshape(members, tile_rows, tile_cols), 'gx', s...  29.8 us
    gather x6, local copies, waits for them, and re-layouts, local(): picked = jnp.take(tile_state, following, axis=1)  12.2 us
    transpose x3, local copies, waits for them, and re-layouts, blocked_regression(): return updated.transpose(1, 0, 2).reshape(members, cell_count)  9.85 us
  transfers between devices with their start and end apart: 1, of which 1 were waited for; matrix products, arithmetic and copies ran while one was open for 3% of the time, Pallas kernels for 0%

commit v1 on v0

v1 whole, which is shorter than its diff:
```python
import functools

import jax
import jax.numpy as jnp
from jax import lax
from jax.experimental import pallas as pl
from jax.experimental.pallas import tpu as pltpu
from jax.sharding import PartitionSpec as P

EPSILON = 1e-06
CHUNKS = 1
ROWS = 8
F32 = jnp.float32
BF16 = jnp.bfloat16
VMEM = pltpu.MemorySpace.VMEM
SMEM = pltpu.MemorySpace.SMEM


def split_two(value):
    high = value.astype(BF16)
    low = (value - high.astype(F32)).astype(BF16)
    return high, low


def pairs_of(batches):
    return [(b, later) for b in range(batches) for later in range(b + 1, batches)]


def pick_body(owner_ref, cells_ref, weight_ref, ens_ref, out_ref, window, sems, *, tile_rows, gy_count):
    batches, nobs = cells_ref.shape
    held, _, cols = ens_ref.shape
    row_at = lax.axis_index("gx")
    col_at = lax.axis_index("gy")
    me = row_at * gy_count + col_at

    def fetch(b):
        first = pl.multiple_of((owner_ref[b] // gy_count) * tile_rows, tile_rows)
        return pltpu.make_async_copy(
            ens_ref.at[:, pl.ds(first, tile_rows), :], window.at[b], sems.at[b]
        )

    for b in range(batches):
        fetch(b).start()
    out_ref[...] = jnp.zeros_like(out_ref)
    for at, (b, later) in enumerate(pairs_of(batches)):
        row = held * batches + at
        out_ref[row : row + 1, :] = jnp.where(owner_ref[later] == me, weight_ref[b : b + 1, :], 0.0)
    for b in range(batches):
        fetch(b).wait()
        cell = cells_ref[b : b + 1, :]
        row_hit = (lax.broadcasted_iota(jnp.int32, (tile_rows, nobs), 0) == cell // cols).astype(F32)
        row_hit = row_hit.astype(BF16)
        row_hit = jnp.concatenate([row_hit] * 3, axis=0)
        col_hit = lax.broadcasted_iota(jnp.int32, (cols, nobs), 0) == cell % cols
        mine = owner_ref[b] % gy_count == col_at
        for m in range(held):
            values = window[b, m]
            high = values.astype(BF16)
            rest = values - high.astype(F32)
            middle, low = split_two(rest)
            stacked = jnp.concatenate([high, middle, low], axis=0)
            columns = lax.dot_general(
                stacked, row_hit, (((0,), (0,)), ((), ())), preferred_element_type=F32
            )
            picked = jnp.sum(jnp.where(col_hit, columns, 0.0), axis=0, keepdims=True)
            row = m * batches + b
            out_ref[row : row + 1, :] = jnp.where(mine, picked, 0.0)


def chain_body(
    owner_ref,
    cells_ref,
    values_ref,
    errors_ref,
    weight_ref,
    got_ref,
    a_ref,
    w_ref,
    x_ref,
    y_ref,
    prior_ref,
    *,
    tile_rows,
    tile_cols,
    held,
    gx_count,
    gy_count,
    inverse,
):
    batches, nobs = cells_ref.shape
    members = held * gx_count
    col_at = lax.axis_index("gy")
    payload = got_ref.shape[1]
    weights = jnp.zeros((payload, nobs), F32)
    for g in range(gx_count):
        part = got_ref[g * gy_count]
        for j in range(1, gy_count):
            part = part + got_ref[g * gy_count + j]
        weights = weights + part
        for m in range(held):
            for b in range(batches):
                row = m * batches + b
                prior_ref[b, held * g + m : held * g + m + 1, :] = part[row : row + 1, :]
    pair_weight = {
        pair: weights[held * batches + at : held * batches + at + 1, :]
        for at, pair in enumerate(pairs_of(batches))
    }
    rows_x, rows_y, cols_x, cols_y = [], [], [], []
    for b in range(batches):
        cell = cells_ref[b : b + 1, :]
        owner = owner_ref[b]
        ox = ((owner // gy_count) * tile_rows + cell // tile_cols).astype(F32) * inverse
        oy = ((owner % gy_count) * tile_cols + cell % tile_cols).astype(F32) * inverse
        rows_x.append(ox)
        rows_y.append(oy)
        cols_x.append(jnp.transpose(jnp.broadcast_to(ox, (nobs, nobs))))
        cols_y.append(jnp.transpose(jnp.broadcast_to(oy, (nobs, nobs))))
    for b in range(batches):
        prior = prior_ref[b]
        average = jnp.mean(prior, axis=0, keepdims=True)
        anomaly = prior - average
        spread = jnp.sum(anomaly * anomaly, axis=0, keepdims=True) / (members - 1) + EPSILON
        noise = errors_ref[b : b + 1, :]
        post_var = 1.0 / (1.0 / spread + 1.0 / noise)
        post_mean = post_var * (average / spread + values_ref[b : b + 1, :] / noise)
        increment = post_mean - average + (jnp.sqrt(post_var / spread) - 1.0) * anomaly
        for later in range(b + 1, batches):
            there = prior_ref[later]
            deviation = there - jnp.mean(there, axis=0, keepdims=True)
            scaled = anomaly * (pair_weight[b, later] / spread / (members - 1))
            covariance = lax.dot_general(
                scaled,
                deviation,
                (((0,), (0,)), ((), ())),
                precision=lax.Precision.HIGHEST,
                preferred_element_type=F32,
            )
            dx = cols_x[b] - rows_x[later]
            dy = cols_y[b] - rows_y[later]
            gain = covariance / (1.0 + (dx * dx + dy * dy))
            prior_ref[later] = there + jnp.dot(
                increment, gain, precision=lax.Precision.HIGHEST, preferred_element_type=F32
            )
        scaled = anomaly * (weight_ref[b : b + 1, :] / spread / (members - 1))
        high, low = split_two(scaled)
        stacked = jnp.concatenate([high, high, low], axis=0).astype(F32)
        wide = a_ref.shape[2]
        if wide > stacked.shape[0]:
            stacked = jnp.concatenate(
                [stacked, jnp.zeros((wide - stacked.shape[0], nobs), F32)], axis=0
            )
        a_ref[b] = jnp.transpose(stacked).astype(BF16)
        high, low = split_two(increment)
        w_ref[b, :members, :nobs] = high
        w_ref[b, :members, nobs:] = high
        w_ref[b, members:, :nobs] = low
        w_ref[b, members:, nobs:] = low
        x_ref[b] = cols_x[b]
        for piece in range(tile_cols // nobs):
            lanes = slice(piece * nobs, (piece + 1) * nobs)
            grid = lax.broadcasted_iota(jnp.int32, (nobs, nobs), 1) + (
                col_at * tile_cols + piece * nobs
            )
            away = cols_y[b] - grid.astype(F32) * inverse
            y_ref[b, :, lanes] = away * away


def update_body(state_ref, a_ref, w_ref, x_ref, y_ref, out_ref, *, first, tile_rows, inverse):
    members, rows, cols = state_ref.shape
    batches, nobs, _ = x_ref.shape
    row_at = lax.axis_index("gx") * tile_rows + first + pl.program_id(0) * rows
    out_ref[...] = state_ref[...]
    for b in range(batches):
        scaled = a_ref[b][:, : 3 * members]
        increment = w_ref[b]
        for r in range(rows):
            state = out_ref[:, r, :]
            deviation = state - jnp.mean(state, axis=0, keepdims=True)
            high, low = split_two(deviation)
            covariance = jnp.dot(
                scaled, jnp.concatenate([high, low, high], axis=0), preferred_element_type=F32
            )
            dx = x_ref[b] - (row_at + r).astype(F32) * inverse
            dx = 1.0 + dx * dx
            away = jnp.concatenate([dx] * (cols // nobs), axis=1) + y_ref[b]
            gain = covariance * pl.reciprocal(away)
            high, low = split_two(gain)
            change = jnp.dot(
                increment, jnp.concatenate([high, low], axis=0), preferred_element_type=F32
            )
            out_ref[:, r, :] = state + (change[:members] + change[members:])


def whole(array):
    return pl.BlockSpec(array.shape, lambda i: (0,) * array.ndim)


def update(state, tables, first, tile_rows, inverse):
    members, here, cols = state.shape
    rows = min(ROWS, here)
    batches, nobs = tables[0].shape[:2]
    cells = here * cols * batches * nobs
    block = pl.BlockSpec((members, rows, cols), lambda i: (0, i, 0))
    return pl.pallas_call(
        functools.partial(update_body, first=first, tile_rows=tile_rows, inverse=inverse),
        grid=(here // rows,),
        in_specs=[block] + [whole(table) for table in tables],
        out_specs=block,
        out_shape=jax.ShapeDtypeStruct(state.shape, F32),
        cost_estimate=pl.CostEstimate(
            flops=cells * members * 10, bytes_accessed=8 * state.size, transcendentals=cells
        ),
        name="update",
    )(state, *tables)


def local(ensemble, obs_values, obs_error, tile_weight, owner_device, obs_cells):
    gx_count = lax.axis_size("gx")
    gy_count = lax.axis_size("gy")
    held, all_rows, tile_cols = ensemble.shape
    members = held * gx_count
    tile_rows = all_rows // gx_count
    batches, nobs = obs_cells.shape
    inverse = 1.0 / (all_rows // 4)
    weight = tile_weight[:, :, 0, 0]
    everyone = gx_count * gy_count
    payload = held * batches + len(pairs_of(batches))
    payload = -(-payload // 8) * 8

    blocks = ensemble.reshape(held, gx_count, tile_rows, tile_cols)
    depth = tile_rows // CHUNKS
    arriving = []
    for c in range(CHUNKS):
        piece = blocks[:, :, c * depth : (c + 1) * depth].transpose(1, 0, 2, 3)
        arriving.append(lax.all_to_all(piece, "gx", split_axis=0, concat_axis=0, tiled=True))

    picked = pl.pallas_call(
        functools.partial(pick_body, tile_rows=tile_rows, gy_count=gy_count),
        in_specs=[
            pl.BlockSpec(memory_space=SMEM),
            pl.BlockSpec(memory_space=VMEM),
            pl.BlockSpec(memory_space=VMEM),
            pl.BlockSpec(memory_space=pl.ANY),
        ],
        out_specs=pl.BlockSpec(memory_space=VMEM),
        out_shape=jax.ShapeDtypeStruct((payload, nobs), F32),
        scratch_shapes=[
            pltpu.VMEM((batches, held, tile_rows, tile_cols), F32),
            pltpu.SemaphoreType.DMA((batches,)),
        ],
        name="pick",
    )(owner_device, obs_cells, weight, ensemble)
    got = lax.all_to_all(
        jnp.broadcast_to(picked[None], (everyone, payload, nobs)),
        ("gx", "gy"),
        split_axis=0,
        concat_axis=0,
        tiled=True,
    )
    wide = -(-3 * members // nobs) * nobs
    tables = pl.pallas_call(
        functools.partial(
            chain_body,
            tile_rows=tile_rows,
            tile_cols=tile_cols,
            held=held,
            gx_count=gx_count,
            gy_count=gy_count,
            inverse=inverse,
        ),
        in_specs=[pl.BlockSpec(memory_space=SMEM)] + [pl.BlockSpec(memory_space=VMEM)] * 5,
        out_specs=[pl.BlockSpec(memory_space=VMEM)] * 4,
        out_shape=[
            jax.ShapeDtypeStruct((batches, nobs, wide), BF16),
            jax.ShapeDtypeStruct((batches, 2 * members, 2 * nobs), BF16),
            jax.ShapeDtypeStruct((batches, nobs, nobs), F32),
            jax.ShapeDtypeStruct((batches, nobs, tile_cols), F32),
        ],
        scratch_shapes=[pltpu.VMEM((batches, members, nobs), F32)],
        name="chain",
    )(owner_device, obs_cells, obs_values, obs_error, weight, got)

    leaving = []
    for c in range(CHUNKS):
        state = arriving[c].reshape(members, depth, tile_cols)
        updated = update(state, tables, c * depth, tile_rows, inverse)
        sent = lax.all_to_all(
            updated.reshape(gx_count, held, depth, tile_cols),
            "gx",
            split_axis=0,
            concat_axis=0,
            tiled=True,
        )
        leaving.append(sent.transpose(1, 0, 2, 3))
    return jnp.concatenate(leaving, axis=2).reshape(ensemble.shape)


def solution(mesh):
    placed = (P("gx", None, "gy"), P(), P(), P(None, None, "gx", "gy"), P(), P())
    return jax.shard_map(
        local, mesh=mesh, in_specs=placed, out_specs=P("gx", None, "gy"), check_vma=False
    )
```

time: 400 us -> 101 us (0.25)
  blocking collectives: 189 us -> 29.5 us
  matrix products: 126 us -> 0 us
  local copies, waits for them, and re-layouts: 47.4 us -> 5.22 us
  waiting for transfers between devices: 1.97 us -> 31.9 us
  Pallas kernels: 0 us -> 23.5 us
  between operations: 13.1 us -> 0.04 us
  other arithmetic: 7.79 us -> 0 us
  loops' own time: 5.79 us -> 0 us
    psum x4 -> x0, blocking collectives: 159 us -> none  [spread_2(): return lax.psum(jnp.where(mine, shard, jnp.zeros_like(shard)), axis)]
    dot_general x262 -> x0, matrix products: 126 us -> none  [the longest x131 83.5 us: regression(): covariance = jnp.dot(anomaly, deviation, precision=PRECISE) / (members - 1)]
    all_to_all x1 -> x2, waiting for transfers between devices: 1.97 us -> 31.9 us  [the longest x1 22.4 us: local(): lax.all_to_all(piece, 'gx', split_axis=0, concat_axis=0, tiled=True)]
    pallas_call x0 -> x3, Pallas kernels: none -> 23.5 us  [the longest x1 16.3 us: update(): pl.pallas_call(functools.partial(update_body, first=first, tile_rows=tile...]
    gather x14 -> x0, local copies, waits for them, and re-layouts: 23.2 us -> none  [the longest x6 12.2 us: local(): picked = jnp.take(tile_state, following, axis=1)]
    transpose x3 -> x1, local copies, waits for them, and re-layouts: 9.85 us -> 1.06 us  [local(): leaving.append(sent.transpose(1, 0, 2, 3))]
    another operation x4 -> x0, loops' own time: 5.79 us -> none  [blocked_regression(): updated = lax.map(update_piece, (stacked, row_coords, col_coords))]
    reduce_sum x139 -> x0, other arithmetic: 4.98 us -> none  [the longest x131 4.81 us: regression(): deviation = state_cols - jnp.mean(state_cols, axis=0, keepdims=True)]
  transfers between devices with their start and end apart: 1 -> 2, of which waited for: 1 -> 2; matrix products, arithmetic and copies ran while one was open for 3% -> 1% of each run, Pallas kernels for 0% -> 4%
where the time goes in v1:
time: 101 us
  waiting for transfers between devices  31.9 us (32%)
  blocking collectives  29.5 us (29%)
  Pallas kernels  23.5 us (23%)
  starting transfers between devices  10.9 us (11%)
  local copies, waits for them, and re-layouts  5.22 us (5%)
    all_to_all x1, blocking collectives, local(): lax.all_to_all(updated.reshape(gx_count, held, depth, tile_cols), 'gx', s...  29.5 us
    all_to_all x1, waiting for transfers between devices, local(): lax.all_to_all(piece, 'gx', split_axis=0, concat_axis=0, tiled=True)  22.4 us
    pallas_call x1, Pallas kernels, update(): pl.pallas_call(functools.partial(update_body, first=first, tile_rows=tile...  16.3 us
    all_to_all x1, waiting for transfers between devices, local(): lax.all_to_all(jnp.broadcast_to(picked[None], (everyone, payload, nobs)),...  9.49 us
    all_to_all x1, starting transfers between devices, local(): lax.all_to_all(jnp.broadcast_to(picked[None], (everyone, payload, nobs)),...  7.33 us
    pallas_call x1, Pallas kernels, local(): pl.pallas_call(functools.partial(chain_body, tile_rows=tile_rows, tile_co...  3.67 us
    all_to_all x1, starting transfers between devices, local(): lax.all_to_all(piece, 'gx', split_axis=0, concat_axis=0, tiled=True)  3.56 us
    pallas_call x1, Pallas kernels, local(): pl.pallas_call(functools.partial(pick_body, tile_rows=tile_rows, gy_count...  3.52 us
  transfers between devices with their start and end apart: 2, of which 2 were waited for; matrix products, arithmetic and copies ran while one was open for 1% of the time, Pallas kernels for 4%

profile of v1, /device:TPU:0, one launch (start us, length us, event | category | flops | bytes accessed | tf_op | source)
XLA Modules:
  0.0 101.0 jit_solution(1121676355040867320)
XLA Ops:
  0.0 0.0 copy-start
  0.0 3.5 %pick.1 = f32[16,128]{1,0:T(8,128)} custom-call(s32[4]{0:T(128)} %owner_ref.3, s32[4,128]{1,0:T(4,128)} %cells_ref.3, f32[4,128]{1,0:T(4,128)} %bitcast.13, f32[2,512,256]{2,1,0:T(8,128)} %ens_ref.1), custom_call_target="tpu_custom_call" | custom-call | tf_op jit(solution)/shard_map/pick/pallas_call | solution.py:237
  3.5 1.4 %broadcast_in_dim.2 = f32[32,16,128]{2,1,0:T(8,128)} broadcast(f32[16,128]{1,0:T(8,128)} %pick.1), dimensions={1,2} | broadcast | bytes 270336 | tf_op jit(solution)/shard_map/broadcast_in_dim | solution.py:254
  4.9 7.3 %all-to-all-start.1 = ((f32[32,16,128]{2,1,0:T(8,128)}), f32[32,16,128]{2,1,0:T(8,128)S(1)}, u32[]{:S(2)}, u32[]{:S(2)}) async-start(f32[32,16,128]{2,1,0:T(8,128)} %broadcast_in_dim.2), calls=%async_computation.1 | async-start | bytes 524288 | tf_op jit(solution)/shard_map/all_to_all | solution.py:253
  12.3 0.0 copy-done
  12.3 1.1 %copy.10 = f32[2,8,64,256]{3,2,0,1:T(8,128)} copy(f32[2,8,64,256]{3,2,1,0:T(8,128)S(1)} %bitcast.9) | data formatting | bytes 2097152 | tf_op jit(solution)/shard_map/reshape | solution.py:230
  13.4 9.5 %all-to-all-done.1.got_ref = f32[32,16,128]{2,1,0:T(8,128)S(1)} async-done(((f32[32,16,128]{2,1,0:T(8,128)}), f32[32,16,128]{2,1,0:T(8,128)S(1)}, u32[]{:S(2)}, u32[]{:S(2)}) %all-to-all-start.1) | async-done | bytes 262176 | tf_op jit(solution)/shard_map/all_to_all | solution.py:253
  22.9 0.0 copy-start.2
  22.9 0.7 copy-done.2
  23.6 3.6 %all-to-all-start = ((f32[8,2,64,256]{3,2,1,0:T(8,128)}), f32[8,2,64,256]{3,2,1,0:T(8,128)S(1)}, u32[]{:S(2)}, u32[]{:S(2)}) async-start(f32[8,2,64,256]{3,2,1,0:T(8,128)} %bitcast.8), calls=%async_computation | async-start | bytes 2097152 | tf_op jit(solution)/shard_map/all_to_all | solution.py:235
  27.1 3.7 %chain.1 = (bf16[4,128,128]{2,1,0:T(8,128)(2,1)}, bf16[4,32,256]{2,1,0:T(8,128)(2,1)}, f32[4,128,128]{2,1,0:T(8,128)}, f32[4,128,256]{2,1,0:T(8,128)}) custom-call(s32[4]{0:T(128)} %owner_ref.3, s32[4,128]{1,0:T(4,128)} %cells_ref.3, f32[4,128]{1,0:T(4,128)} %values_ref.1, f32[4,128]{1,0:T(4,128)} %errors_ref.1, f32[4,128]{1,0:T(4,128)} %bitcast.14, ...), custom_call_target="tpu_custom_call" | custom-call | tf_op jit(solution)/shard_map/chain/pallas_call | solution.py:261
  30.8 22.4 %all-to-all-done = f32[8,2,64,256]{3,2,1,0:T(8,128)S(1)} async-done(((f32[8,2,64,256]{3,2,1,0:T(8,128)}), f32[8,2,64,256]{3,2,1,0:T(8,128)S(1)}, u32[]{:S(2)}, u32[]{:S(2)}) %all-to-all-start) | async-done | bytes 1048608 | tf_op jit(solution)/shard_map/all_to_all | solution.py:235
  53.2 0.0 copy-start.1
  53.2 1.0 copy-done.1
  54.1 16.3 %update.1 = f32[16,64,256]{2,1,0:T(8,128)} custom-call(f32[16,64,256]{2,1,0:T(8,128)} %bitcast.11, bf16[4,128,128]{2,1,0:T(8,128)(2,1)} %get-tuple-element.9.a_ref, bf16[4,32,256]{2,1,0:T(8,128)(2,1)} %get-tuple-element.10.w_ref, f32[4,128,128]{2,1,0:T(8,128)} %get-tuple-element.11.x_ref, f32[4,128,256]{2,1,0:T(8,128)} %get-tuple-element.12.y_ref), custom_call_target="tpu_custom_call" | custom-call | flops 1342177280 | bytes 2097152 | tf_op jit(solution)/shard_map/update/pallas_call | solution.py:204
  70.4 29.5 %all_to_all.15 = f32[8,2,64,256]{3,2,1,0:T(8,128)S(1)} all-to-all(f32[8,2,64,256]{3,2,1,0:T(8,128)} %bitcast.12), channel_id=1, replica_groups=mesh['gx'=8,'gy'=4] {'gx'}, dimensions={0} | all-to-all | bytes 2097152 | tf_op jit(solution)/shard_map/all_to_all | solution.py:287
  99.9 1.1 %copy.8 = f32[2,8,64,256]{3,2,1,0:T(8,128)} copy(f32[2,8,64,256]{3,2,0,1:T(8,128)S(1)} %bitcast.10) | data formatting | bytes 2097152 | tf_op jit(solution)/shard_map/transpose | solution.py:294
Async XLA Ops:
  0.0 12.3 %copy-start = (f32[2,512,256]{2,1,0:T(8,128)S(1)}, f32[2,512,256]{2,1,0:T(8,128)}, u32[]{:S(2)}) copy-start(f32[2,512,256]{2,1,0:T(8,128)} %ens_ref.1) | copy-start | bytes 3145732
  4.9 17.9 %all-to-all-start.1 = ((f32[32,16,128]{2,1,0:T(8,128)}), f32[32,16,128]{2,1,0:T(8,128)S(1)}, u32[]{:S(2)}, u32[]{:S(2)}) async-start(f32[32,16,128]{2,1,0:T(8,128)} %broadcast_in_dim.2), calls=%async_computation.1 | async-start | bytes 524288 | tf_op jit(solution)/shard_map/all_to_all | solution.py:253
  22.9 0.7 copy-start.2
  23.6 29.6 %all-to-all-start = ((f32[8,2,64,256]{3,2,1,0:T(8,128)}), f32[8,2,64,256]{3,2,1,0:T(8,128)S(1)}, u32[]{:S(2)}, u32[]{:S(2)}) async-start(f32[8,2,64,256]{3,2,1,0:T(8,128)} %bitcast.8), calls=%async_computation | async-start | bytes 2097152 | tf_op jit(solution)/shard_map/all_to_all | solution.py:235
  53.2 1.0 copy-start.1

commit v2 on v1

v2 whole, which is shorter than its diff:
```python
import functools

import jax
import jax.numpy as jnp
from jax import lax
from jax.experimental import pallas as pl
from jax.experimental.pallas import tpu as pltpu
from jax.sharding import PartitionSpec as P


EPSILON = 1e-06
FIRST_EIGHTHS = 4
ROWS = 8
F32 = jnp.float32
BF16 = jnp.bfloat16
VMEM = pltpu.MemorySpace.VMEM
SMEM = pltpu.MemorySpace.SMEM


def split_two(value):
    high = value.astype(BF16)
    low = (value - high.astype(F32)).astype(BF16)
    return high, low


def pairs_of(batches):
    return [(b, later) for b in range(batches) for later in range(b + 1, batches)]


def pick_body(
    owner_ref,
    cells_ref,
    weight_ref,
    ens_ref,
    out_ref,
    blocks_ref,
    window,
    in_sems,
    out_sems,
    *,
    tile_rows,
    gx_count,
    gy_count,
):
    batches, nobs = cells_ref.shape
    held, _, cols = ens_ref.shape
    row_at = lax.axis_index("gx")
    col_at = lax.axis_index("gy")
    me = row_at * gy_count + col_at

    def fetch(tile):
        rows = pl.ds(tile * tile_rows, tile_rows)
        return pltpu.make_async_copy(ens_ref.at[:, rows, :], window.at[tile], in_sems.at[tile])

    def put(tile):
        return pltpu.make_async_copy(window.at[tile], blocks_ref.at[tile], out_sems.at[tile])

    for tile in range(gx_count):
        fetch(tile).start()
    out_ref[...] = jnp.zeros_like(out_ref)
    for at, (b, later) in enumerate(pairs_of(batches)):
        row = held * batches + at
        out_ref[row : row + 1, :] = jnp.where(owner_ref[later] == me, weight_ref[b : b + 1, :], 0.0)
    for tile in range(gx_count):
        fetch(tile).wait()
        put(tile).start()
    for b in range(batches):
        owner_row = owner_ref[b] // gy_count
        cell = cells_ref[b : b + 1, :]
        row_hit = (lax.broadcasted_iota(jnp.int32, (tile_rows, nobs), 0) == cell // cols).astype(F32)
        row_hit = row_hit.astype(BF16)
        row_hit = jnp.concatenate([row_hit] * 3, axis=0)
        col_hit = lax.broadcasted_iota(jnp.int32, (cols, nobs), 0) == cell % cols
        mine = owner_ref[b] % gy_count == col_at
        for m in range(held):
            values = window[owner_row, m]
            high = values.astype(BF16)
            rest = values - high.astype(F32)
            middle, low = split_two(rest)
            stacked = jnp.concatenate([high, middle, low], axis=0)
            columns = lax.dot_general(
                stacked, row_hit, (((0,), (0,)), ((), ())), preferred_element_type=F32
            )
            picked = jnp.sum(jnp.where(col_hit, columns, 0.0), axis=0, keepdims=True)
            row = m * batches + b
            out_ref[row : row + 1, :] = jnp.where(mine, picked, 0.0)
    for tile in range(gx_count):
        put(tile).wait()


def observed_at(owner_ref, cells_ref, b, tile_rows, tile_cols, gy_count, inverse):
    nobs = cells_ref.shape[1]
    cell = cells_ref[b : b + 1, :]
    owner = owner_ref[b]
    ox = ((owner // gy_count) * tile_rows + cell // tile_cols).astype(F32) * inverse
    oy = ((owner % gy_count) * tile_cols + cell % tile_cols).astype(F32) * inverse
    down_x = jnp.transpose(jnp.broadcast_to(ox, (nobs, nobs)))
    down_y = jnp.transpose(jnp.broadcast_to(oy, (nobs, nobs)))
    return ox, oy, down_x, down_y


def tables_body(
    owner_ref, cells_ref, x_ref, y_ref, *, tile_rows, tile_cols, gy_count, inverse
):
    batches, nobs = cells_ref.shape
    left = lax.axis_index("gy") * tile_cols
    for b in range(batches):
        _, _, down_x, down_y = observed_at(
            owner_ref, cells_ref, b, tile_rows, tile_cols, gy_count, inverse
        )
        x_ref[b] = down_x
        for piece in range(tile_cols // nobs):
            lanes = slice(piece * nobs, (piece + 1) * nobs)
            grid = lax.broadcasted_iota(jnp.int32, (nobs, nobs), 1) + (left + piece * nobs)
            away = down_y - grid.astype(F32) * inverse
            y_ref[b, :, lanes] = away * away


def chain_body(
    owner_ref,
    cells_ref,
    values_ref,
    errors_ref,
    weight_ref,
    got_ref,
    a_ref,
    w_ref,
    prior_ref,
    *,
    tile_rows,
    tile_cols,
    held,
    gy_count,
    offsets,
    inverse,
):
    batches, nobs = cells_ref.shape
    members = held * len(offsets)
    weights = jnp.zeros(got_ref.shape[1:], F32)
    row_at = lax.axis_index("gx")
    for slot, offset in enumerate(offsets):
        part = got_ref[slot]
        weights = weights + part
        source = held * (row_at ^ offset)
        for m in range(held):
            for b in range(batches):
                row = m * batches + b
                prior_ref[b, pl.ds(source + m, 1), :] = part[row : row + 1, :]
    pair_weight = {
        pair: weights[held * batches + at : held * batches + at + 1, :]
        for at, pair in enumerate(pairs_of(batches))
    }
    places = [
        observed_at(owner_ref, cells_ref, b, tile_rows, tile_cols, gy_count, inverse)
        for b in range(batches)
    ]
    for b in range(batches):
        prior = prior_ref[b]
        average = jnp.mean(prior, axis=0, keepdims=True)
        anomaly = prior - average
        spread = jnp.sum(anomaly * anomaly, axis=0, keepdims=True) / (members - 1) + EPSILON
        noise = errors_ref[b : b + 1, :]
        post_var = 1.0 / (1.0 / spread + 1.0 / noise)
        post_mean = post_var * (average / spread + values_ref[b : b + 1, :] / noise)
        increment = post_mean - average + (jnp.sqrt(post_var / spread) - 1.0) * anomaly
        for later in range(b + 1, batches):
            there = prior_ref[later]
            deviation = there - jnp.mean(there, axis=0, keepdims=True)
            scaled = anomaly * (pair_weight[b, later] / spread / (members - 1))
            covariance = lax.dot_general(
                scaled,
                deviation,
                (((0,), (0,)), ((), ())),
                precision=lax.Precision.HIGHEST,
                preferred_element_type=F32,
            )
            dx = places[b][2] - places[later][0]
            dy = places[b][3] - places[later][1]
            gain = covariance / (1.0 + (dx * dx + dy * dy))
            prior_ref[later] = there + jnp.dot(
                increment, gain, precision=lax.Precision.HIGHEST, preferred_element_type=F32
            )
        scaled = anomaly * (weight_ref[b : b + 1, :] / spread / (members - 1))
        high, low = split_two(scaled)
        stacked = jnp.concatenate([high, high, low], axis=0).astype(F32)
        wide = a_ref.shape[2]
        if wide > stacked.shape[0]:
            stacked = jnp.concatenate(
                [stacked, jnp.zeros((wide - stacked.shape[0], nobs), F32)], axis=0
            )
        a_ref[b] = jnp.transpose(stacked).astype(BF16)
        high, low = split_two(increment)
        w_ref[b, :members, :nobs] = high
        w_ref[b, :members, nobs:] = high
        w_ref[b, members:, :nobs] = low
        w_ref[b, members:, nobs:] = low


def update_body(
    state_ref, a_ref, w_ref, x_ref, y_ref, *refs, first, tile_rows, held, inverse, spread_out
):
    members, rows, cols = state_ref.shape
    batches, nobs, _ = x_ref.shape
    row_at = lax.axis_index("gx")
    top = row_at * tile_rows + first + pl.program_id(0) * rows
    states = [state_ref[:, r, :] for r in range(rows)]
    for b in range(batches):
        scaled = a_ref[b][:, : 3 * members]
        increment = w_ref[b]
        for r in range(rows):
            state = states[r]
            deviation = state - jnp.mean(state, axis=0, keepdims=True)
            high, low = split_two(deviation)
            covariance = jnp.dot(
                scaled, jnp.concatenate([high, low, high], axis=0), preferred_element_type=F32
            )
            dx = x_ref[b] - (top + r).astype(F32) * inverse
            dx = 1.0 + dx * dx
            away = jnp.concatenate([dx] * (cols // nobs), axis=1) + y_ref[b]
            gain = covariance * pl.reciprocal(away)
            high, low = split_two(gain)
            change = jnp.dot(
                increment, jnp.concatenate([high, low], axis=0), preferred_element_type=F32
            )
            states[r] = state + (change[:members] + change[members:])
    if spread_out:
        outs, whole_ref = refs[:-1], refs[-1]
    else:
        outs, whole_ref = (), refs[0]
    for r in range(rows):
        whole_ref[:, r, :] = states[r]
    for slot, out_ref in enumerate(outs):
        out_ref[...] = whole_ref[pl.ds(held * (row_at ^ slot), held)]


def share(picked, gx_count, gy_count):
    got = picked[None]
    offsets = [0]

    def gather(got, step):
        other = lax.ppermute(got, "gx", [(i, i ^ step) for i in range(gx_count)])
        return jnp.concatenate([got, other], axis=0)

    steps = [1 << bit for bit in range(gx_count.bit_length() - 1)]
    far = steps[-1:]
    for step in far:
        got = gather(got, step)
        offsets = offsets + [offset ^ step for offset in offsets]
    others = [
        lax.ppermute(got, "gy", [(i, i ^ step) for i in range(gy_count)])
        for step in range(1, gy_count)
    ]
    for other in others:
        got = got + other
    for step in steps[:-1]:
        got = gather(got, step)
        offsets = offsets + [offset ^ step for offset in offsets]
    return got, offsets


def whole(array):
    return pl.BlockSpec(array.shape, lambda i: (0,) * array.ndim)


def update(state, tables, first, depth, tile_rows, inverse, gx_count, spread_out):
    members, _, cols = state.shape
    rows = ROWS
    held = members // gx_count
    batches, nobs = tables[0].shape[:2]
    cells = depth * cols * batches * nobs
    start = first // rows
    if spread_out:
        out_specs = [pl.BlockSpec((held, rows, cols), lambda i: (0, i, 0))] * gx_count
        out_shape = [jax.ShapeDtypeStruct((held, depth, cols), F32)] * gx_count
        scratch = [pltpu.VMEM((members, rows, cols), F32)]
    else:
        out_specs = pl.BlockSpec((members, rows, cols), lambda i: (0, i, 0))
        out_shape = jax.ShapeDtypeStruct((members, depth, cols), F32)
        scratch = []
    return pl.pallas_call(
        functools.partial(
            update_body,
            first=first,
            tile_rows=tile_rows,
            inverse=inverse,
            held=held,
            spread_out=spread_out,
        ),
        grid=(depth // rows,),
        in_specs=[
            pl.BlockSpec((members, rows, cols), lambda i: (0, start + i, 0)),
            whole(tables[0]),
            whole(tables[1]),
            whole(tables[2]),
            whole(tables[3]),
        ],
        out_specs=out_specs,
        out_shape=out_shape,
        scratch_shapes=scratch,
        cost_estimate=pl.CostEstimate(
            flops=cells * members * 10,
            bytes_accessed=8 * members * depth * cols,
            transcendentals=cells,
        ),
        name="update",
    )(state, *tables)


def assemble_body(whole_ref, *refs, first, tile_rows, here):
    pieces, out_ref, sems = refs[:-2], refs[-2], refs[-1]
    row_at = lax.axis_index("gx")
    copies = []
    for tile in range(whole_ref.shape[0]):
        rows = pl.ds(tile * tile_rows, first)
        copies.append(
            pltpu.make_async_copy(whole_ref.at[tile], out_ref.at[:, rows, :], sems.at[tile])
        )
    for slot, piece in enumerate(pieces):
        start = pl.multiple_of((row_at ^ slot) * tile_rows + first, here)
        rows = pl.ds(start, tile_rows - first)
        copies.append(
            pltpu.make_async_copy(
                piece, out_ref.at[:, rows, :], sems.at[whole_ref.shape[0] + slot]
            )
        )
    for copy in copies:
        copy.start()
    for copy in copies:
        copy.wait()


def local(ensemble, obs_values, obs_error, tile_weight, owner_device, obs_cells):
    gx_count = lax.axis_size("gx")
    gy_count = lax.axis_size("gy")
    held, all_rows, tile_cols = ensemble.shape
    members = held * gx_count
    tile_rows = all_rows // gx_count
    batches, nobs = obs_cells.shape
    inverse = 1.0 / (all_rows // 4)
    weight = tile_weight[:, :, 0, 0]
    payload = held * batches + len(pairs_of(batches))
    payload = -(-payload // 8) * 8
    in_smem = pl.BlockSpec(memory_space=SMEM)
    in_vmem = pl.BlockSpec(memory_space=VMEM)
    anywhere = pl.BlockSpec(memory_space=pl.ANY)
    geometry = dict(tile_rows=tile_rows, tile_cols=tile_cols, gy_count=gy_count, inverse=inverse)

    picked, blocks = pl.pallas_call(
        functools.partial(pick_body, tile_rows=tile_rows, gx_count=gx_count, gy_count=gy_count),
        in_specs=[in_smem, in_vmem, in_vmem, anywhere],
        out_specs=[in_vmem, anywhere],
        out_shape=[
            jax.ShapeDtypeStruct((payload, nobs), F32),
            jax.ShapeDtypeStruct((gx_count, held, tile_rows, tile_cols), F32),
        ],
        scratch_shapes=[
            pltpu.VMEM((gx_count, held, tile_rows, tile_cols), F32),
            pltpu.SemaphoreType.DMA((gx_count,)),
            pltpu.SemaphoreType.DMA((gx_count,)),
        ],
        name="pick",
    )(owner_device, obs_cells, weight, ensemble)
    state = lax.all_to_all(blocks, "gx", split_axis=0, concat_axis=0, tiled=True)
    state = state.reshape(members, tile_rows, tile_cols)
    places = pl.pallas_call(
        functools.partial(tables_body, **geometry),
        in_specs=[in_smem, in_vmem],
        out_specs=[in_vmem] * 2,
        out_shape=[
            jax.ShapeDtypeStruct((batches, nobs, nobs), F32),
            jax.ShapeDtypeStruct((batches, nobs, tile_cols), F32),
        ],
        name="tables",
    )(owner_device, obs_cells)
    got, offsets = share(picked, gx_count, gy_count)
    wide = -(-3 * members // nobs) * nobs
    factors = pl.pallas_call(
        functools.partial(chain_body, held=held, offsets=offsets, **geometry),
        in_specs=[in_smem] + [in_vmem] * 5,
        out_specs=[in_vmem] * 2,
        out_shape=[
            jax.ShapeDtypeStruct((batches, nobs, wide), BF16),
            jax.ShapeDtypeStruct((batches, 2 * members, 2 * nobs), BF16),
        ],
        scratch_shapes=[pltpu.VMEM((batches, members, nobs), F32)],
        name="chain",
    )(owner_device, obs_cells, obs_values, obs_error, weight, got)
    tables = [*factors, *places]

    first = tile_rows * FIRST_EIGHTHS // 8
    rest = tile_rows - first
    upper = update(state, tables, 0, first, tile_rows, inverse, gx_count, False)
    upper = lax.all_to_all(
        upper.reshape(gx_count, held, first, tile_cols),
        "gx",
        split_axis=0,
        concat_axis=0,
        tiled=True,
    )
    lower = update(state, tables, first, rest, tile_rows, inverse, gx_count, True)
    lower = [
        piece
        if slot == 0
        else lax.ppermute(piece, "gx", [(i, i ^ slot) for i in range(gx_count)])
        for slot, piece in enumerate(lower)
    ]
    return pl.pallas_call(
        functools.partial(assemble_body, first=first, tile_rows=tile_rows, here=ROWS),
        in_specs=[in_vmem] * (1 + gx_count),
        out_specs=anywhere,
        out_shape=jax.ShapeDtypeStruct(ensemble.shape, F32),
        scratch_shapes=[pltpu.SemaphoreType.DMA((2 * gx_count,))],
        name="assemble",
    )(upper, *lower)


def solution(mesh):
    placed = (P("gx", None, "gy"), P(), P(), P(None, None, "gx", "gy"), P(), P())
    return jax.shard_map(
        local, mesh=mesh, in_specs=placed, out_specs=P("gx", None, "gy"), check_vma=False
    )
```

time: 101 us -> 95.6 us (0.947)
  blocking collectives: 29.5 us -> 0 us
  starting transfers between devices: 10.9 us -> 28.7 us
  waiting for transfers between devices: 31.9 us -> 36.4 us
  Pallas kernels: 23.5 us -> 27.3 us
  local copies, waits for them, and re-layouts: 5.22 us -> 1.84 us
    ppermute x0 -> x13, waiting for transfers between devices: none -> 36.4 us  [the longest x3 27.6 us: gather(): other = lax.ppermute(got, 'gx', [(i, i ^ step) for i in range(gx_count)])]
    all_to_all x2, waiting for transfers between devices: 31.9 us -> 0.01 us  [the longest x1 0.01 us: local(): lax.all_to_all(upper.reshape(gx_count, held, first, tile_cols), 'gx', spl...]
    all_to_all x1 -> x0, blocking collectives: 29.5 us -> none  [local(): lax.all_to_all(updated.reshape(gx_count, held, depth, tile_cols), 'gx', s...]
    ppermute x0 -> x13, starting transfers between devices: none -> 17.9 us  [the longest x7 11.7 us: local(): lax.ppermute(piece, 'gx', [(i, i ^ slot) for i in range(gx_count)])]
    pallas_call x2 -> x4, Pallas kernels: 7.19 us -> 10.8 us  [the longest x1 3.4 us: local(): pl.pallas_call(functools.partial(pick_body, tile_rows=tile_rows, gx_count...]
    broadcast_in_dim x1 -> x0, local copies, waits for them, and re-layouts: 1.41 us -> none  [local(): jnp.broadcast_to(picked[None], (everyone, payload, nobs))]
    reshape x1 -> x0, local copies, waits for them, and re-layouts: 1.07 us -> none  [local(): blocks = ensemble.reshape(held, gx_count, tile_rows, tile_cols)]
    transpose x1 -> x0, local copies, waits for them, and re-layouts: 1.06 us -> none  [local(): leaving.append(sent.transpose(1, 0, 2, 3))]
  transfers between devices with their start and end apart: 2 -> 15, of which waited for: 2 -> 7; matrix products, arithmetic and copies ran while one was open for 1% -> 1% of each run, Pallas kernels for 4% -> 14%
where the time goes in v2:
time: 95.6 us; the launch traced here: 95.1 us
  waiting for transfers between devices  36.4 us (38%)
  starting transfers between devices  28.7 us (30%)
  Pallas kernels  27.3 us (29%)
  local copies, waits for them, and re-layouts  1.84 us (2%)
    ppermute x3, waiting for transfers between devices, gather(): other = lax.ppermute(got, 'gx', [(i, i ^ step) for i in range(gx_count)])  27.6 us
    pallas_call x2, Pallas kernels, update(): pl.pallas_call(functools.partial(update_body, first=first, tile_rows=tile...  16.5 us
    ppermute x7, starting transfers between devices, local(): lax.ppermute(piece, 'gx', [(i, i ^ slot) for i in range(gx_count)])  11.7 us
    all_to_all x1, starting transfers between devices, local(): lax.all_to_all(blocks, 'gx', split_axis=0, concat_axis=0, tiled=True)  7.29 us
    ppermute x7, waiting for transfers between devices, local(): lax.ppermute(piece, 'gx', [(i, i ^ slot) for i in range(gx_count)])  5.96 us
    ppermute x3, starting transfers between devices, gather(): other = lax.ppermute(got, 'gx', [(i, i ^ step) for i in range(gx_count)])  4.34 us
    all_to_all x1, starting transfers between devices, local(): lax.all_to_all(upper.reshape(gx_count, held, first, tile_cols), 'gx', spl...  3.6 us
    pallas_call x1, Pallas kernels, local(): pl.pallas_call(functools.partial(pick_body, tile_rows=tile_rows, gx_count...  3.4 us
  transfers between devices with their start and end apart: 15, of which 7 were waited for; matrix products, arithmetic and copies ran while one was open for 1% of the time, Pallas kernels for 14%

profile of v2, /device:TPU:0, one launch (start us, length us, event | category | flops | bytes accessed | tf_op | source)
XLA Modules:
  0.0 95.1 jit_solution(3562401739556444583)
XLA Ops:
  0.0 3.4 %pick.1 = (f32[16,128]{1,0:T(8,128)}, f32[8,2,64,256]{3,2,1,0:T(8,128)}) custom-call(s32[4]{0:T(128)} %owner_ref.5, s32[4,128]{1,0:T(4,128)} %cells_ref.5, f32[4,128]{1,0:T(4,128)} %bitcast.10, f32[2,512,256]{2,1,0:T(8,128)} %ens_ref.1), custom_call_target="tpu_custom_call" | custom-call | tf_op jit(solution)/shard_map/pick/pallas_call | solution.py:348
  3.4 7.3 %all-to-all-start = ((f32[8,2,64,256]{3,2,1,0:T(8,128)}), f32[8,2,64,256]{3,2,1,0:T(8,128)S(1)}, u32[]{:S(2)}, u32[]{:S(2)}) async-start(f32[8,2,64,256]{3,2,1,0:T(8,128)} %get-tuple-element.19), calls=%async_computation | async-start | bytes 2097152 | tf_op jit(solution)/shard_map/all_to_all | solution.py:363
  10.7 2.9 %collective-permute-start = (f32[1,16,128]{2,1,0:T(8,128)S(1)}, f32[1,16,128]{2,1,0:T(8,128)S(1)}, u32[]{:S(2)}, u32[]{:S(2)}) collective-permute-start(f32[1,16,128]{2,1,0:T(8,128)S(1)} %bitcast.7), channel_id=1, source_target_pairs={{0,16},{4,20},{8,24},{12,28},{16,0},{20,4},{24,8},{28,12},{1,17},{... | collective-permute-start | bytes 24584 | tf_op jit(solution)/shard_map/ppermute | solution.py:241
  13.6 23.2 %collective-permute-done = f32[1,16,128]{2,1,0:T(8,128)S(1)} collective-permute-done((f32[1,16,128]{2,1,0:T(8,128)S(1)}, f32[1,16,128]{2,1,0:T(8,128)S(1)}, u32[]{:S(2)}, u32[]{:S(2)}) %collective-permute-start) | collective-permute-done | bytes 8224 | tf_op jit(solution)/shard_map/ppermute | solution.py:241
  36.8 1.5 %collective-permute-start.2 = (f32[2,16,128]{2,1,0:T(8,128)S(1)}, f32[2,16,128]{2,1,0:T(8,128)S(1)}, u32[]{:S(2)}, u32[]{:S(2)}) collective-permute-start(f32[2,16,128]{2,1,0:T(8,128)S(1)} %pad_maximum_fusion.2), channel_id=1, source_target_pairs={{0,2},{1,3},{2,0},{3,1},{4,6},{5,7},{6,4},{7,5},{8,10},{9,11},{10,... | collective-permute-start | bytes 49160 | tf_op jit(solution)/shard_map/ppermute | solution.py:250
  38.7 1.9 %collective-permute-done.2 = f32[2,16,128]{2,1,0:T(8,128)S(1)} collective-permute-done((f32[2,16,128]{2,1,0:T(8,128)S(1)}, f32[2,16,128]{2,1,0:T(8,128)S(1)}, u32[]{:S(2)}, u32[]{:S(2)}) %collective-permute-start.2) | collective-permute-done | bytes 16416 | tf_op jit(solution)/shard_map/ppermute | solution.py:250
  40.6 0.9 collective-permute-done.3
  41.5 1.4 %collective-permute-start.4 = (f32[2,16,128]{2,1,0:T(8,128)S(1)}, f32[2,16,128]{2,1,0:T(8,128)S(1)}, u32[]{:S(2)}, u32[]{:S(2)}) collective-permute-start(f32[2,16,128]{2,1,0:T(8,128)S(1)} %add_add_fusion), channel_id=1, source_target_pairs={{0,4},{4,0},{8,12},{12,8},{16,20},{20,16},{24,28},{28,24},{1,5},{5... | collective-permute-start | bytes 49160 | tf_op jit(solution)/shard_map/ppermute | solution.py:241
  42.9 2.3 %collective-permute-done.4 = f32[2,16,128]{2,1,0:T(8,128)S(1)} collective-permute-done((f32[2,16,128]{2,1,0:T(8,128)S(1)}, f32[2,16,128]{2,1,0:T(8,128)S(1)}, u32[]{:S(2)}, u32[]{:S(2)}) %collective-permute-start.4) | collective-permute-done | bytes 16416 | tf_op jit(solution)/shard_map/ppermute | solution.py:241
  45.3 1.8 %tables.1 = (f32[4,128,128]{2,1,0:T(8,128)}, f32[4,128,256]{2,1,0:T(8,128)}) custom-call(s32[4]{0:T(128)} %owner_ref.5, s32[4,128]{1,0:T(4,128)} %cells_ref.5), custom_call_target="tpu_custom_call" | custom-call | tf_op jit(solution)/shard_map/tables/pallas_call | solution.py:365
  47.1 2.1 %collective-permute-done.5 = f32[4,16,128]{2,1,0:T(8,128)S(1)} collective-permute-done((f32[4,16,128]{2,1,0:T(8,128)S(1)}, f32[4,16,128]{2,1,0:T(8,128)S(1)}, u32[]{:S(2)}, u32[]{:S(2)}) %collective-permute-start.5) | collective-permute-done | bytes 32800 | tf_op jit(solution)/shard_map/ppermute | solution.py:241
  49.8 3.3 %chain.1 = (bf16[4,128,128]{2,1,0:T(8,128)(2,1)}, bf16[4,32,256]{2,1,0:T(8,128)(2,1)}) custom-call(s32[4]{0:T(128)} %owner_ref.5, s32[4,128]{1,0:T(4,128)} %cells_ref.5, f32[4,128]{1,0:T(4,128)} %values_ref.1, f32[4,128]{1,0:T(4,128)} %errors_ref.1, f32[4,128]{1,0:T(4,128)} %bitcast.11, f32[8,16,128]{2,1,0:T(8,128)} %pad_maximum_fusion.got_ref), custom_call_target="tpu_custom_call" | custom-call | tf_op jit(solution)/shard_map/chain/pallas_call | solution.py:377
  53.2 1.0 %copy-done.1 = f32[8,2,64,256]{3,2,1,0:T(8,128)} copy-done((f32[8,2,64,256]{3,2,1,0:T(8,128)}, f32[8,2,64,256]{3,2,1,0:T(8,128)S(1)}, u32[]{:S(2)}) %copy-start.1) | copy-done | bytes 1048600
  54.1 8.2 %update.2 = f32[16,32,256]{2,1,0:T(8,128)} custom-call(f32[16,64,256]{2,1,0:T(8,128)} %bitcast.4, bf16[4,128,128]{2,1,0:T(8,128)(2,1)} %get-tuple-element.21.a_ref, bf16[4,32,256]{2,1,0:T(8,128)(2,1)} %get-tuple-element.22.w_ref, f32[4,128,128]{2,1,0:T(8,128)} %get-tuple-element.23.x_ref, f32[4,128,256]{2,1,0:T(8,128)} %get-tuple-element.24.y_ref), custom_call_target="tpu_custom_call" | custom-call | flops 671088640 | bytes 1048576 | tf_op jit(solution)/shard_map/update/pallas_call | solution.py:280
  62.3 3.6 %all-to-all-start.1 = ((f32[8,2,32,256]{3,2,1,0:T(8,128)}), f32[8,2,32,256]{3,2,1,0:T(8,128)S(1)}, u32[]{:S(2)}, u32[]{:S(2)}) async-start(f32[8,2,32,256]{3,2,1,0:T(8,128)} %bitcast.6), calls=%async_computation.1 | async-start | bytes 1048576 | tf_op jit(solution)/shard_map/all_to_all | solution.py:393
  65.9 8.3 %update.3 = (f32[2,32,256]{2,1,0:T(8,128)}, f32[2,32,256]{2,1,0:T(8,128)}, f32[2,32,256]{2,1,0:T(8,128)}, f32[2,32,256]{2,1,0:T(8,128)}, f32[2,32,256]{2,1,0:T(8...) custom-call(f32[16,64,256]{2,1,0:T(8,128)} %bitcast.5, ...), custom_call_target="tpu_custom_call" | custom-call | flops 671088640 | bytes 1048576 | tf_op jit(solution)/shard_map/update/pallas_call | solution.py:280
  74.2 3.9 %collective-permute-start.10 = (f32[2,32,256]{2,1,0:T(8,128)}, f32[2,32,256]{2,1,0:T(8,128)S(1)}, u32[]{:S(2)}, u32[]{:S(2)}) collective-permute-start(f32[2,32,256]{2,1,0:T(8,128)} %get-tuple-element.30), channel_id=1, source_target_pairs={{0,20},{4,16},{8,28},{12,24},{16,4},{20,0},{24,12},{28,8},{1,21},{... | collective-permute-start | bytes 196616 | tf_op jit(solution)/shard_map/ppermute | solution.py:404
  78.1 1.5 %collective-permute-start.11 = (f32[2,32,256]{2,1,0:T(8,128)}, f32[2,32,256]{2,1,0:T(8,128)S(1)}, u32[]{:S(2)}, u32[]{:S(2)}) collective-permute-start(f32[2,32,256]{2,1,0:T(8,128)} %get-tuple-element.31), channel_id=1, source_target_pairs={{0,24},{4,28},{8,16},{12,20},{16,8},{20,12},{24,0},{28,4},{1,25},{... | collective-permute-start | bytes 196616 | tf_op jit(solution)/shard_map/ppermute | solution.py:404
  79.6 2.4 %collective-permute-start.12 = (f32[2,32,256]{2,1,0:T(8,128)}, f32[2,32,256]{2,1,0:T(8,128)S(1)}, u32[]{:S(2)}, u32[]{:S(2)}) collective-permute-start(f32[2,32,256]{2,1,0:T(8,128)} %get-tuple-element.32), channel_id=1, source_target_pairs={{0,28},{4,24},{8,20},{12,16},{16,12},{20,8},{24,4},{28,0},{1,29},{... | collective-permute-start | bytes 196616 | tf_op jit(solution)/shard_map/ppermute | solution.py:404
  81.9 1.5 %collective-permute-start.6 = (f32[2,32,256]{2,1,0:T(8,128)}, f32[2,32,256]{2,1,0:T(8,128)S(1)}, u32[]{:S(2)}, u32[]{:S(2)}) collective-permute-start(f32[2,32,256]{2,1,0:T(8,128)} %get-tuple-element.26), channel_id=1, source_target_pairs={{0,4},{4,0},{8,12},{12,8},{16,20},{20,16},{24,28},{28,24},{1,5},{5... | collective-permute-start | bytes 196616 | tf_op jit(solution)/shard_map/ppermute | solution.py:404
  83.4 2.4 %collective-permute-done.10.refs_5_ = f32[2,32,256]{2,1,0:T(8,128)S(1)} collective-permute-done((f32[2,32,256]{2,1,0:T(8,128)}, f32[2,32,256]{2,1,0:T(8,128)S(1)}, u32[]{:S(2)}, u32[]{:S(2)}) %collective-permute-start.10) | collective-permute-done | bytes 65568 | tf_op jit(solution)/shard_map/ppermute | solution.py:404
  85.8 2.5 %collective-permute-start.9 = (f32[2,32,256]{2,1,0:T(8,128)}, f32[2,32,256]{2,1,0:T(8,128)S(1)}, u32[]{:S(2)}, u32[]{:S(2)}) collective-permute-start(f32[2,32,256]{2,1,0:T(8,128)} %get-tuple-element.29), channel_id=1, source_target_pairs={{0,16},{4,20},{8,24},{12,28},{16,0},{20,4},{24,8},{28,12},{1,17},{... | collective-permute-start | bytes 196616 | tf_op jit(solution)/shard_map/ppermute | solution.py:404
  88.4 3.5 %collective-permute-done.8.refs_3_ = f32[2,32,256]{2,1,0:T(8,128)S(1)} collective-permute-done((f32[2,32,256]{2,1,0:T(8,128)}, f32[2,32,256]{2,1,0:T(8,128)S(1)}, u32[]{:S(2)}, u32[]{:S(2)}) %collective-permute-start.8) | collective-permute-done | bytes 65568 | tf_op jit(solution)/shard_map/ppermute | solution.py:404
  92.8 2.3 %assemble.1 = f32[2,512,256]{2,1,0:T(8,128)} custom-call(f32[8,2,32,256]{3,2,1,0:T(8,128)} %copy-done, f32[2,32,256]{2,1,0:T(8,128)} %get-tuple-element.25.refs_0_, f32[2,32,256]{2,1,0:T(8,128)} %copy-done.5, f32[2,32,256]{2,1,0:T(8,128)} %copy-done.6, f32[2,32,256]{2,1,0:T(8,128)} %copy-done.7, f32[2,32,256]{2,1,0:T(8,128)} %copy-done.8, ...), custom_call_target="tpu_custom_call" | custom-call | tf_op jit(solution)/shard_map/assemble/pallas_call | solution.py:407
  (36 shorter events, 1.9 us)
Async XLA Ops:
  3.4 7.3 %copy-start.9 = (f32[16,128]{1,0:T(8,128)S(1)}, f32[16,128]{1,0:T(8,128)}, u32[]{:S(2)}) copy-start(f32[16,128]{1,0:T(8,128)} %get-tuple-element.20) | copy-start | bytes 24580
  3.4 49.7 %all-to-all-start = ((f32[8,2,64,256]{3,2,1,0:T(8,128)}), f32[8,2,64,256]{3,2,1,0:T(8,128)S(1)}, u32[]{:S(2)}, u32[]{:S(2)}) async-start(f32[8,2,64,256]{3,2,1,0:T(8,128)} %get-tuple-element.19), calls=%async_computation | async-start | bytes 2097152 | tf_op jit(solution)/shard_map/all_to_all | solution.py:363
  10.7 26.1 %collective-permute-start = (f32[1,16,128]{2,1,0:T(8,128)S(1)}, f32[1,16,128]{2,1,0:T(8,128)S(1)}, u32[]{:S(2)}, u32[]{:S(2)}) collective-permute-start(f32[1,16,128]{2,1,0:T(8,128)S(1)} %bitcast.7), channel_id=1, source_target_pairs={{0,16},{4,20},{8,24},{12,28},{16,0},{20,4},{24,8},{28,12},{1,17},{... | collective-permute-start | bytes 24584 | tf_op jit(solution)/shard_map/ppermute | solution.py:241
  36.8 1.9 %collective-permute-start.1 = (f32[2,16,128]{2,1,0:T(8,128)S(1)}, f32[2,16,128]{2,1,0:T(8,128)S(1)}, u32[]{:S(2)}, u32[]{:S(2)}) collective-permute-start(f32[2,16,128]{2,1,0:T(8,128)S(1)} %pad_maximum_fusion.2), channel_id=1, source_target_pairs={{0,1},{1,0},{2,3},{3,2},{4,5},{5,4},{6,7},{7,6},{8,9},{9,8},{10,11... | collective-permute-start | bytes 49160 | tf_op jit(solution)/shard_map/ppermute | solution.py:250
  36.8 3.7 %collective-permute-start.2 = (f32[2,16,128]{2,1,0:T(8,128)S(1)}, f32[2,16,128]{2,1,0:T(8,128)S(1)}, u32[]{:S(2)}, u32[]{:S(2)}) collective-permute-start(f32[2,16,128]{2,1,0:T(8,128)S(1)} %pad_maximum_fusion.2), channel_id=1, source_target_pairs={{0,2},{1,3},{2,0},{3,1},{4,6},{5,7},{6,4},{7,5},{8,10},{9,11},{10,... | collective-permute-start | bytes 49160 | tf_op jit(solution)/shard_map/ppermute | solution.py:250
  38.4 3.2 %collective-permute-start.3 = (f32[2,16,128]{2,1,0:T(8,128)S(1)}, f32[2,16,128]{2,1,0:T(8,128)S(1)}, u32[]{:S(2)}, u32[]{:S(2)}) collective-permute-start(f32[2,16,128]{2,1,0:T(8,128)S(1)} %pad_maximum_fusion.2), channel_id=1, source_target_pairs={{0,3},{1,2},{2,1},{3,0},{4,7},{5,6},{6,5},{7,4},{8,11},{9,10},{10,... | collective-permute-start | bytes 49160 | tf_op jit(solution)/shard_map/ppermute | solution.py:250
  41.5 3.7 %collective-permute-start.4 = (f32[2,16,128]{2,1,0:T(8,128)S(1)}, f32[2,16,128]{2,1,0:T(8,128)S(1)}, u32[]{:S(2)}, u32[]{:S(2)}) collective-permute-start(f32[2,16,128]{2,1,0:T(8,128)S(1)} %add_add_fusion), channel_id=1, source_target_pairs={{0,4},{4,0},{8,12},{12,8},{16,20},{20,16},{24,28},{28,24},{1,5},{5... | collective-permute-start | bytes 49160 | tf_op jit(solution)/shard_map/ppermute | solution.py:241
  45.3 3.9 %collective-permute-start.5 = (f32[4,16,128]{2,1,0:T(8,128)S(1)}, f32[4,16,128]{2,1,0:T(8,128)S(1)}, u32[]{:S(2)}, u32[]{:S(2)}) collective-permute-start(f32[4,16,128]{2,1,0:T(8,128)S(1)} %pad_maximum_fusion.1), channel_id=1, source_target_pairs={{0,8},{4,12},{8,0},{12,4},{16,24},{20,28},{24,16},{28,20},{1,9},{5... | collective-permute-start | bytes 98312 | tf_op jit(solution)/shard_map/ppermute | solution.py:241
  53.2 1.0 %copy-start.1 = (f32[8,2,64,256]{3,2,1,0:T(8,128)}, f32[8,2,64,256]{3,2,1,0:T(8,128)S(1)}, u32[]{:S(2)}) copy-start(f32[8,2,64,256]{3,2,1,0:T(8,128)S(1)} %all-to-all-done) | copy-start | bytes 3145732
  62.3 29.6 %all-to-all-start.1 = ((f32[8,2,32,256]{3,2,1,0:T(8,128)}), f32[8,2,32,256]{3,2,1,0:T(8,128)S(1)}, u32[]{:S(2)}, u32[]{:S(2)}) async-start(f32[8,2,32,256]{3,2,1,0:T(8,128)} %bitcast.6), calls=%async_computation.1 | async-start | bytes 1048576 | tf_op jit(solution)/shard_map/all_to_all | solution.py:393
  74.2 11.6 %collective-permute-start.10 = (f32[2,32,256]{2,1,0:T(8,128)}, f32[2,32,256]{2,1,0:T(8,128)S(1)}, u32[]{:S(2)}, u32[]{:S(2)}) collective-permute-start(f32[2,32,256]{2,1,0:T(8,128)} %get-tuple-element.30), channel_id=1, source_target_pairs={{0,20},{4,16},{8,28},{12,24},{16,4},{20,0},{24,12},{28,8},{1,21},{... | collective-permute-start | bytes 196616 | tf_op jit(solution)/shard_map/ppermute | solution.py:404
  78.1 7.7 %collective-permute-start.11 = (f32[2,32,256]{2,1,0:T(8,128)}, f32[2,32,256]{2,1,0:T(8,128)S(1)}, u32[]{:S(2)}, u32[]{:S(2)}) collective-permute-start(f32[2,32,256]{2,1,0:T(8,128)} %get-tuple-element.31), channel_id=1, source_target_pairs={{0,24},{4,28},{8,16},{12,20},{16,8},{20,12},{24,0},{28,4},{1,25},{... | collective-permute-start | bytes 196616 | tf_op jit(solution)/shard_map/ppermute | solution.py:404
  79.6 8.7 %collective-permute-start.12 = (f32[2,32,256]{2,1,0:T(8,128)}, f32[2,32,256]{2,1,0:T(8,128)S(1)}, u32[]{:S(2)}, u32[]{:S(2)}) collective-permute-start(f32[2,32,256]{2,1,0:T(8,128)} %get-tuple-element.32), channel_id=1, source_target_pairs={{0,28},{4,24},{8,20},{12,16},{16,12},{20,8},{24,4},{28,0},{1,29},{... | collective-permute-start | bytes 196616 | tf_op jit(solution)/shard_map/ppermute | solution.py:404
  81.9 6.4 %collective-permute-start.6 = (f32[2,32,256]{2,1,0:T(8,128)}, f32[2,32,256]{2,1,0:T(8,128)S(1)}, u32[]{:S(2)}, u32[]{:S(2)}) collective-permute-start(f32[2,32,256]{2,1,0:T(8,128)} %get-tuple-element.26), channel_id=1, source_target_pairs={{0,4},{4,0},{8,12},{12,8},{16,20},{20,16},{24,28},{28,24},{1,5},{5... | collective-permute-start | bytes 196616 | tf_op jit(solution)/shard_map/ppermute | solution.py:404
  83.4 4.9 %collective-permute-start.7 = (f32[2,32,256]{2,1,0:T(8,128)}, f32[2,32,256]{2,1,0:T(8,128)S(1)}, u32[]{:S(2)}, u32[]{:S(2)}) collective-permute-start(f32[2,32,256]{2,1,0:T(8,128)} %get-tuple-element.27), channel_id=1, source_target_pairs={{0,8},{4,12},{8,0},{12,4},{16,24},{20,28},{24,16},{28,20},{1,9},{5... | collective-permute-start | bytes 196616 | tf_op jit(solution)/shard_map/ppermute | solution.py:404
  85.8 6.1 %copy-start.2 = (f32[2,32,256]{2,1,0:T(8,128)}, f32[2,32,256]{2,1,0:T(8,128)S(1)}, u32[]{:S(2)}) copy-start(f32[2,32,256]{2,1,0:T(8,128)S(1)} %collective-permute-done.10.refs_5_) | copy-start | bytes 196612
  85.8 6.1 %collective-permute-start.8 = (f32[2,32,256]{2,1,0:T(8,128)}, f32[2,32,256]{2,1,0:T(8,128)S(1)}, u32[]{:S(2)}, u32[]{:S(2)}) collective-permute-start(f32[2,32,256]{2,1,0:T(8,128)} %get-tuple-element.28), channel_id=1, source_target_pairs={{0,12},{4,8},{8,4},{12,0},{16,28},{20,24},{24,20},{28,16},{1,13},{... | collective-permute-start | bytes 196616 | tf_op jit(solution)/shard_map/ppermute | solution.py:404
  85.8 6.1 %copy-start.3 = (f32[2,32,256]{2,1,0:T(8,128)}, f32[2,32,256]{2,1,0:T(8,128)S(1)}, u32[]{:S(2)}) copy-start(f32[2,32,256]{2,1,0:T(8,128)S(1)} %collective-permute-done.11.refs_6_) | copy-start | bytes 196612
  85.8 6.1 %collective-permute-start.9 = (f32[2,32,256]{2,1,0:T(8,128)}, f32[2,32,256]{2,1,0:T(8,128)S(1)}, u32[]{:S(2)}, u32[]{:S(2)}) collective-permute-start(f32[2,32,256]{2,1,0:T(8,128)} %get-tuple-element.29), channel_id=1, source_target_pairs={{0,16},{4,20},{8,24},{12,28},{16,0},{20,4},{24,8},{28,12},{1,17},{... | collective-permute-start | bytes 196616 | tf_op jit(solution)/shard_map/ppermute | solution.py:404
  88.3 3.6 %copy-start.4 = (f32[2,32,256]{2,1,0:T(8,128)}, f32[2,32,256]{2,1,0:T(8,128)S(1)}, u32[]{:S(2)}) copy-start(f32[2,32,256]{2,1,0:T(8,128)S(1)} %collective-permute-done.12.refs_7_) | copy-start | bytes 196612
  88.3 3.6 %copy-start.5 = (f32[2,32,256]{2,1,0:T(8,128)}, f32[2,32,256]{2,1,0:T(8,128)S(1)}, u32[]{:S(2)}) copy-start(f32[2,32,256]{2,1,0:T(8,128)S(1)} %collective-permute-done.6.refs_1_) | copy-start | bytes 196612
  88.3 3.6 %copy-start.6 = (f32[2,32,256]{2,1,0:T(8,128)}, f32[2,32,256]{2,1,0:T(8,128)S(1)}, u32[]{:S(2)}) copy-start(f32[2,32,256]{2,1,0:T(8,128)S(1)} %collective-permute-done.7.refs_2_) | copy-start | bytes 196612
  91.9 0.7 copy-start.8
  91.9 0.9 copy-start
  (1 other events, 0.6 us)

commit v3 on v2

--- a/solution.py
+++ b/solution.py
@@ -9,7 +9,8 @@
 
 
 EPSILON = 1e-06
-FIRST_EIGHTHS = 4
+FIRST_EIGHTHS = 3
+LIGHT = pltpu.CompilerParams(vmem_limit_bytes=16 << 20)
 ROWS = 8
 F32 = jnp.float32
 BF16 = jnp.bfloat16
@@ -302,6 +303,7 @@
             bytes_accessed=8 * members * depth * cols,
             transcendentals=cells,
         ),
+        compiler_params=LIGHT,
         name="update",
     )(state, *tables)
 
@@ -370,6 +372,7 @@
             jax.ShapeDtypeStruct((batches, nobs, nobs), F32),
             jax.ShapeDtypeStruct((batches, nobs, tile_cols), F32),
         ],
+        compiler_params=LIGHT,
         name="tables",
     )(owner_device, obs_cells)
     got, offsets = share(picked, gx_count, gy_count)
@@ -383,6 +386,7 @@
             jax.ShapeDtypeStruct((batches, 2 * members, 2 * nobs), BF16),
         ],
         scratch_shapes=[pltpu.VMEM((batches, members, nobs), F32)],
+        compiler_params=LIGHT,
         name="chain",
     )(owner_device, obs_cells, obs_values, obs_error, weight, got)
     tables = [*factors, *places]
@@ -397,19 +401,18 @@
         concat_axis=0,
         tiled=True,
     )
-    lower = update(state, tables, first, rest, tile_rows, inverse, gx_count, True)
-    lower = [
-        piece
-        if slot == 0
-        else lax.ppermute(piece, "gx", [(i, i ^ slot) for i in range(gx_count)])
-        for slot, piece in enumerate(lower)
-    ]
+    lower = [*update(state, tables, first, rest, tile_rows, inverse, gx_count, True)]
+    for slot in range(1, gx_count):
+        lower[slot] = lax.ppermute(
+            lower[slot], "gx", [(i, i ^ slot) for i in range(gx_count)]
+        )
     return pl.pallas_call(
         functools.partial(assemble_body, first=first, tile_rows=tile_rows, here=ROWS),
         in_specs=[in_vmem] * (1 + gx_count),
         out_specs=anywhere,
         out_shape=jax.ShapeDtypeStruct(ensemble.shape, F32),
         scratch_shapes=[pltpu.SemaphoreType.DMA((2 * gx_count,))],
+        compiler_params=LIGHT,
         name="assemble",
     )(upper, *lower)
 

time: 95.6 us -> 89.4 us (0.935)
  Pallas kernels: 27.3 us -> 20.9 us
  starting transfers between devices: 28.7 us -> 31.8 us
  local copies, waits for them, and re-layouts: 1.84 us -> 0.03 us
    pallas_call x2, Pallas kernels: 16.5 us -> 13.3 us  [update(): pl.pallas_call(functools.partial(update_body, first=first, tile_rows=tile...]
    ppermute x7, starting transfers between devices: 11.7 us -> 14.6 us  [local(): lax.ppermute(lower[slot], 'gx', [(i, i ^ slot) for i in range(gx_count)])]
    unnamed x20 -> x12, local copies, waits for them, and re-layouts: 1.84 us -> 0.03 us
    ppermute x7, waiting for transfers between devices: 5.96 us -> 4.75 us  [local(): lax.ppermute(lower[slot], 'gx', [(i, i ^ slot) for i in range(gx_count)])]
    pallas_call x1, Pallas kernels: 2.28 us -> 1.09 us  [local(): pl.pallas_call(functools.partial(assemble_body, first=first, tile_rows=ti...]
    pallas_call x1, Pallas kernels: 1.8 us -> 0.76 us  [local(): pl.pallas_call(functools.partial(tables_body, **geometry), in_specs=[in_s...]
    pallas_call x1, Pallas kernels: 3.34 us -> 2.32 us  [local(): pl.pallas_call(functools.partial(chain_body, held=held, offsets=offsets,...]
    ppermute x3, waiting for transfers between devices: 27.6 us -> 28.6 us  [gather(): other = lax.ppermute(got, 'gx', [(i, i ^ step) for i in range(gx_count)])]
  transfers between devices with their start and end apart: 15 -> 15, of which waited for: 7 -> 7; matrix products, arithmetic and copies ran while one was open for 1% -> 0% of each run, Pallas kernels for 14% -> 12%
where the time goes in v3:
time: 89.4 us; the launch traced here: 89 us
  waiting for transfers between devices  36.2 us (40%)
  starting transfers between devices  31.8 us (36%)
  Pallas kernels  20.9 us (23%)
    ppermute x3, waiting for transfers between devices, gather(): other = lax.ppermute(got, 'gx', [(i, i ^ step) for i in range(gx_count)])  28.6 us
    ppermute x7, starting transfers between devices, local(): lax.ppermute(lower[slot], 'gx', [(i, i ^ slot) for i in range(gx_count)])  14.6 us
    pallas_call x2, Pallas kernels, update(): pl.pallas_call(functools.partial(update_body, first=first, tile_rows=tile...  13.3 us
    all_to_all x1, starting transfers between devices, local(): lax.all_to_all(blocks, 'gx', split_axis=0, concat_axis=0, tiled=True)  7.29 us
    ppermute x7, waiting for transfers between devices, local(): lax.ppermute(lower[slot], 'gx', [(i, i ^ slot) for i in range(gx_count)])  4.75 us
    ppermute x3, starting transfers between devices, gather(): other = lax.ppermute(got, 'gx', [(i, i ^ step) for i in range(gx_count)])  4.41 us
    all_to_all x1, starting transfers between devices, local(): lax.all_to_all(upper.reshape(gx_count, held, first, tile_cols), 'gx', spl...  3.6 us
    pallas_call x1, Pallas kernels, local(): pl.pallas_call(functools.partial(pick_body, tile_rows=tile_rows, gx_count...  3.4 us
  transfers between devices with their start and end apart: 15, of which 7 were waited for; matrix products, arithmetic and copies ran while one was open for 0% of the time, Pallas kernels for 12%

profile of v3, /device:TPU:0, one launch (start us, length us, event | category | flops | bytes accessed | tf_op | source)
XLA Modules:
  0.0 89.0 jit_solution(7390771135072622327)
XLA Ops:
  0.0 3.4 %pick.1 = (f32[16,128]{1,0:T(8,128)}, f32[8,2,64,256]{3,2,1,0:T(8,128)}) custom-call(s32[4]{0:T(128)} %owner_ref.5, s32[4,128]{1,0:T(4,128)} %cells_ref.5, f32[4,128]{1,0:T(4,128)} %bitcast.6, f32[2,512,256]{2,1,0:T(8,128)} %ens_ref.1), custom_call_target="tpu_custom_call" | custom-call | tf_op jit(solution)/shard_map/pick/pallas_call | solution.py:350
  3.4 7.3 %all-to-all-start = ((f32[8,2,64,256]{3,2,1,0:T(8,128)}), f32[8,2,64,256]{3,2,1,0:T(8,128)S(1)}, u32[]{:S(2)}, u32[]{:S(2)}) async-start(f32[8,2,64,256]{3,2,1,0:T(8,128)} %get-tuple-element.19), calls=%async_computation | async-start | bytes 2097152 | tf_op jit(solution)/shard_map/all_to_all | solution.py:365
  10.7 2.9 %collective-permute-start = (f32[1,16,128]{2,1,0:T(8,128)S(1)}, f32[1,16,128]{2,1,0:T(8,128)S(1)}, u32[]{:S(2)}, u32[]{:S(2)}) collective-permute-start(f32[1,16,128]{2,1,0:T(8,128)S(1)} %bitcast.8), channel_id=1, source_target_pairs={{0,16},{4,20},{8,24},{12,28},{16,0},{20,4},{24,8},{28,12},{1,17},{... | collective-permute-start | bytes 24584 | tf_op jit(solution)/shard_map/ppermute | solution.py:242
  13.6 23.2 %collective-permute-done = f32[1,16,128]{2,1,0:T(8,128)S(1)} collective-permute-done((f32[1,16,128]{2,1,0:T(8,128)S(1)}, f32[1,16,128]{2,1,0:T(8,128)S(1)}, u32[]{:S(2)}, u32[]{:S(2)}) %collective-permute-start) | collective-permute-done | bytes 8224 | tf_op jit(solution)/shard_map/ppermute | solution.py:242
  36.8 1.5 %collective-permute-start.2 = (f32[2,16,128]{2,1,0:T(8,128)S(1)}, f32[2,16,128]{2,1,0:T(8,128)S(1)}, u32[]{:S(2)}, u32[]{:S(2)}) collective-permute-start(f32[2,16,128]{2,1,0:T(8,128)S(1)} %pad_maximum_fusion.2), channel_id=1, source_target_pairs={{0,2},{1,3},{2,0},{3,1},{4,6},{5,7},{6,4},{7,5},{8,10},{9,11},{10,... | collective-permute-start | bytes 49160 | tf_op jit(solution)/shard_map/ppermute | solution.py:251
  38.7 1.9 %collective-permute-done.2 = f32[2,16,128]{2,1,0:T(8,128)S(1)} collective-permute-done((f32[2,16,128]{2,1,0:T(8,128)S(1)}, f32[2,16,128]{2,1,0:T(8,128)S(1)}, u32[]{:S(2)}, u32[]{:S(2)}) %collective-permute-start.2) | collective-permute-done | bytes 16416 | tf_op jit(solution)/shard_map/ppermute | solution.py:251
  40.6 0.9 %collective-permute-done.3 = f32[2,16,128]{2,1,0:T(8,128)S(1)} collective-permute-done((f32[2,16,128]{2,1,0:T(8,128)S(1)}, f32[2,16,128]{2,1,0:T(8,128)S(1)}, u32[]{:S(2)}, u32[]{:S(2)}) %collective-permute-start.3) | collective-permute-done | bytes 16416 | tf_op jit(solution)/shard_map/ppermute | solution.py:251
  41.5 1.5 %collective-permute-start.4 = (f32[2,16,128]{2,1,0:T(8,128)S(1)}, f32[2,16,128]{2,1,0:T(8,128)S(1)}, u32[]{:S(2)}, u32[]{:S(2)}) collective-permute-start(f32[2,16,128]{2,1,0:T(8,128)S(1)} %add_add_fusion), channel_id=1, source_target_pairs={{0,4},{4,0},{8,12},{12,8},{16,20},{20,16},{24,28},{28,24},{1,5},{5... | collective-permute-start | bytes 49160 | tf_op jit(solution)/shard_map/ppermute | solution.py:242
  43.0 2.3 %collective-permute-done.4 = f32[2,16,128]{2,1,0:T(8,128)S(1)} collective-permute-done((f32[2,16,128]{2,1,0:T(8,128)S(1)}, f32[2,16,128]{2,1,0:T(8,128)S(1)}, u32[]{:S(2)}, u32[]{:S(2)}) %collective-permute-start.4) | collective-permute-done | bytes 16416 | tf_op jit(solution)/shard_map/ppermute | solution.py:242
  45.4 0.8 tables.1
  46.2 3.1 %collective-permute-done.5 = f32[4,16,128]{2,1,0:T(8,128)S(1)} collective-permute-done((f32[4,16,128]{2,1,0:T(8,128)S(1)}, f32[4,16,128]{2,1,0:T(8,128)S(1)}, u32[]{:S(2)}, u32[]{:S(2)}) %collective-permute-start.5) | collective-permute-done | bytes 32800 | tf_op jit(solution)/shard_map/ppermute | solution.py:242
  49.3 2.3 %chain.1 = (bf16[4,128,128]{2,1,0:T(8,128)(2,1)S(1)}, bf16[4,32,256]{2,1,0:T(8,128)(2,1)S(1)}) custom-call(s32[4]{0:T(128)S(1)} %copy-done.2, s32[4,128]{1,0:T(4,128)S(1)} %copy-done, f32[4,128]{1,0:T(4,128)S(1)} %copy-done.3, f32[4,128]{1,0:T(4,128)S(1)} %copy-done.4, f32[4,128]{1,0:T(4,128)S(1)} %bitcast.7, f32[8,16,128]{2,1,0:T(8,128)S(1)} %pad_maximum_fusion.got_ref), custom_call_target="tpu_custom_call" | custom-call | tf_op jit(solution)/shard_map/chain/pallas_call | solution.py:380
  51.6 5.3 %update.2 = f32[16,24,256]{2,1,0:T(8,128)} custom-call(f32[16,64,256]{2,1,0:T(8,128)S(1)} %bitcast.4, bf16[4,128,128]{2,1,0:T(8,128)(2,1)S(1)} %get-tuple-element.21.a_ref, bf16[4,32,256]{2,1,0:T(8,128)(2,1)S(1)} %get-tuple-element.22.w_ref, f32[4,128,128]{2,1,0:T(8,128)S(1)} %get-tuple-element.23.x_ref, f32[4,128,256]{2,1,0:T(8,128)S(1)} %get-tuple-element.24.y_ref), custom_call_target="tpu_custom_call" | custom-call | flops 503316480 | bytes 786432 | tf_op jit(solution)/shard_map/update/pallas_call | solution.py:281
  57.0 3.6 %all-to-all-start.1 = ((f32[8,2,24,256]{3,2,1,0:T(8,128)}), f32[8,2,24,256]{3,2,1,0:T(8,128)S(1)}, u32[]{:S(2)}, u32[]{:S(2)}) async-start(f32[8,2,24,256]{3,2,1,0:T(8,128)} %bitcast.3), calls=%async_computation.1 | async-start | bytes 786432 | tf_op jit(solution)/shard_map/all_to_all | solution.py:397
  60.6 8.0 %update.3 = (f32[2,40,256]{2,1,0:T(8,128)S(1)}, f32[2,40,256]{2,1,0:T(8,128)S(1)}, f32[2,40,256]{2,1,0:T(8,128)S(1)}, f32[2,40,256]{2,1,0:T(8,128)S(1)}, f32[2,4...) custom-call(f32[16,64,256]{2,1,0:T(8,128)S(1)} %bitcast.5, ...), custom_call_target="tpu_custom_call" | custom-call | flops 838860800 | bytes 1310720 | tf_op jit(solution)/shard_map/update/pallas_call | solution.py:281
  68.6 3.9 %collective-permute-start.10 = (f32[2,40,256]{2,1,0:T(8,128)S(1)}, f32[2,40,256]{2,1,0:T(8,128)S(1)}, u32[]{:S(2)}, u32[]{:S(2)}) collective-permute-start(f32[2,40,256]{2,1,0:T(8,128)S(1)} %get-tuple-element.30), channel_id=1, source_target_pairs={{0,20},{4,16},{8,28},{12,24},{16,4},{20,0},{24,12},{28,8},{1,21},{... | collective-permute-start | bytes 245768 | tf_op jit(solution)/shard_map/ppermute | solution.py:406
  72.5 1.5 %collective-permute-start.11 = (f32[2,40,256]{2,1,0:T(8,128)S(1)}, f32[2,40,256]{2,1,0:T(8,128)S(1)}, u32[]{:S(2)}, u32[]{:S(2)}) collective-permute-start(f32[2,40,256]{2,1,0:T(8,128)S(1)} %get-tuple-element.31), channel_id=1, source_target_pairs={{0,24},{4,28},{8,16},{12,20},{16,8},{20,12},{24,0},{28,4},{1,25},{... | collective-permute-start | bytes 245768 | tf_op jit(solution)/shard_map/ppermute | solution.py:406
  73.9 2.4 %collective-permute-start.12 = (f32[2,40,256]{2,1,0:T(8,128)S(1)}, f32[2,40,256]{2,1,0:T(8,128)S(1)}, u32[]{:S(2)}, u32[]{:S(2)}) collective-permute-start(f32[2,40,256]{2,1,0:T(8,128)S(1)} %get-tuple-element.32), channel_id=1, source_target_pairs={{0,28},{4,24},{8,20},{12,16},{16,12},{20,8},{24,4},{28,0},{1,29},{... | collective-permute-start | bytes 245768 | tf_op jit(solution)/shard_map/ppermute | solution.py:406
  76.3 1.5 %collective-permute-start.6 = (f32[2,40,256]{2,1,0:T(8,128)S(1)}, f32[2,40,256]{2,1,0:T(8,128)S(1)}, u32[]{:S(2)}, u32[]{:S(2)}) collective-permute-start(f32[2,40,256]{2,1,0:T(8,128)S(1)} %get-tuple-element.26), channel_id=1, source_target_pairs={{0,4},{4,0},{8,12},{12,8},{16,20},{20,16},{24,28},{28,24},{1,5},{5... | collective-permute-start | bytes 245768 | tf_op jit(solution)/shard_map/ppermute | solution.py:406
  77.8 1.5 %collective-permute-done.10.refs_5_ = f32[2,40,256]{2,1,0:T(8,128)S(1)} collective-permute-done((f32[2,40,256]{2,1,0:T(8,128)S(1)}, f32[2,40,256]{2,1,0:T(8,128)S(1)}, u32[]{:S(2)}, u32[]{:S(2)}) %collective-permute-start.10) | collective-permute-done | bytes 81952 | tf_op jit(solution)/shard_map/ppermute | solution.py:406
  79.2 0.6 collective-permute-start.8
  79.8 4.9 %collective-permute-start.9 = (f32[2,40,256]{2,1,0:T(8,128)S(1)}, f32[2,40,256]{2,1,0:T(8,128)S(1)}, u32[]{:S(2)}, u32[]{:S(2)}) collective-permute-start(f32[2,40,256]{2,1,0:T(8,128)S(1)} %get-tuple-element.29), channel_id=1, source_target_pairs={{0,16},{4,20},{8,24},{12,28},{16,0},{20,4},{24,8},{28,12},{1,17},{... | collective-permute-start | bytes 245768 | tf_op jit(solution)/shard_map/ppermute | solution.py:406
  84.7 3.3 %collective-permute-done.9.refs_4_ = f32[2,40,256]{2,1,0:T(8,128)S(1)} collective-permute-done((f32[2,40,256]{2,1,0:T(8,128)S(1)}, f32[2,40,256]{2,1,0:T(8,128)S(1)}, u32[]{:S(2)}, u32[]{:S(2)}) %collective-permute-start.9) | collective-permute-done | bytes 81952 | tf_op jit(solution)/shard_map/ppermute | solution.py:406
  87.9 1.1 %assemble.1 = f32[2,512,256]{2,1,0:T(8,128)} custom-call(f32[8,2,24,256]{3,2,1,0:T(8,128)S(1)} %all-to-all-done.1.whole_ref, f32[2,40,256]{2,1,0:T(8,128)S(1)} %get-tuple-element.25.refs_0_, f32[2,40,256]{2,1,0:T(8,128)S(1)} %collective-permute-done.6.refs_1_, f32[2,40,256]{2,1,0:T(8,128)S(1)} %collective-permute-done.7.refs_2_, ...), custom_call_target="tpu_custom_call" | custom-call | tf_op jit(solution)/shard_map/assemble/pallas_call | solution.py:409
  (28 shorter events, 0.4 us)
Async XLA Ops:
  3.4 7.3 %copy-start.5 = (f32[16,128]{1,0:T(8,128)S(1)}, f32[16,128]{1,0:T(8,128)}, u32[]{:S(2)}) copy-start(f32[16,128]{1,0:T(8,128)} %get-tuple-element.20) | copy-start | bytes 24580
  3.4 48.2 %all-to-all-start = ((f32[8,2,64,256]{3,2,1,0:T(8,128)}), f32[8,2,64,256]{3,2,1,0:T(8,128)S(1)}, u32[]{:S(2)}, u32[]{:S(2)}) async-start(f32[8,2,64,256]{3,2,1,0:T(8,128)} %get-tuple-element.19), calls=%async_computation | async-start | bytes 2097152 | tf_op jit(solution)/shard_map/all_to_all | solution.py:365
  10.7 26.1 %collective-permute-start = (f32[1,16,128]{2,1,0:T(8,128)S(1)}, f32[1,16,128]{2,1,0:T(8,128)S(1)}, u32[]{:S(2)}, u32[]{:S(2)}) collective-permute-start(f32[1,16,128]{2,1,0:T(8,128)S(1)} %bitcast.8), channel_id=1, source_target_pairs={{0,16},{4,20},{8,24},{12,28},{16,0},{20,4},{24,8},{28,12},{1,17},{... | collective-permute-start | bytes 24584 | tf_op jit(solution)/shard_map/ppermute | solution.py:242
  36.8 1.9 %collective-permute-start.1 = (f32[2,16,128]{2,1,0:T(8,128)S(1)}, f32[2,16,128]{2,1,0:T(8,128)S(1)}, u32[]{:S(2)}, u32[]{:S(2)}) collective-permute-start(f32[2,16,128]{2,1,0:T(8,128)S(1)} %pad_maximum_fusion.2), channel_id=1, source_target_pairs={{0,1},{1,0},{2,3},{3,2},{4,5},{5,4},{6,7},{7,6},{8,9},{9,8},{10,11... | collective-permute-start | bytes 49160 | tf_op jit(solution)/shard_map/ppermute | solution.py:251
  36.8 3.7 %collective-permute-start.2 = (f32[2,16,128]{2,1,0:T(8,128)S(1)}, f32[2,16,128]{2,1,0:T(8,128)S(1)}, u32[]{:S(2)}, u32[]{:S(2)}) collective-permute-start(f32[2,16,128]{2,1,0:T(8,128)S(1)} %pad_maximum_fusion.2), channel_id=1, source_target_pairs={{0,2},{1,3},{2,0},{3,1},{4,6},{5,7},{6,4},{7,5},{8,10},{9,11},{10,... | collective-permute-start | bytes 49160 | tf_op jit(solution)/shard_map/ppermute | solution.py:251
  38.4 3.2 %collective-permute-start.3 = (f32[2,16,128]{2,1,0:T(8,128)S(1)}, f32[2,16,128]{2,1,0:T(8,128)S(1)}, u32[]{:S(2)}, u32[]{:S(2)}) collective-permute-start(f32[2,16,128]{2,1,0:T(8,128)S(1)} %pad_maximum_fusion.2), channel_id=1, source_target_pairs={{0,3},{1,2},{2,1},{3,0},{4,7},{5,6},{6,5},{7,4},{8,11},{9,10},{10,... | collective-permute-start | bytes 49160 | tf_op jit(solution)/shard_map/ppermute | solution.py:251
  41.5 3.8 %copy-start = (s32[4,128]{1,0:T(4,128)S(1)}, s32[4,128]{1,0:T(4,128)}, u32[]{:S(2)}) copy-start(s32[4,128]{1,0:T(4,128)} %cells_ref.5) | copy-start | bytes 6148
  41.5 3.8 %copy-start.2 = (s32[4]{0:T(128)S(1)}, s32[4]{0:T(128)}, u32[]{:S(2)}) copy-start(s32[4]{0:T(128)} %owner_ref.5) | copy-start | bytes 52
  41.5 3.8 %collective-permute-start.4 = (f32[2,16,128]{2,1,0:T(8,128)S(1)}, f32[2,16,128]{2,1,0:T(8,128)S(1)}, u32[]{:S(2)}, u32[]{:S(2)}) collective-permute-start(f32[2,16,128]{2,1,0:T(8,128)S(1)} %add_add_fusion), channel_id=1, source_target_pairs={{0,4},{4,0},{8,12},{12,8},{16,20},{20,16},{24,28},{28,24},{1,5},{5... | collective-permute-start | bytes 49160 | tf_op jit(solution)/shard_map/ppermute | solution.py:242
  45.4 3.9 %collective-permute-start.5 = (f32[4,16,128]{2,1,0:T(8,128)S(1)}, f32[4,16,128]{2,1,0:T(8,128)S(1)}, u32[]{:S(2)}, u32[]{:S(2)}) collective-permute-start(f32[4,16,128]{2,1,0:T(8,128)S(1)} %pad_maximum_fusion.1), channel_id=1, source_target_pairs={{0,8},{4,12},{8,0},{12,4},{16,24},{20,28},{24,16},{28,20},{1,9},{5... | collective-permute-start | bytes 98312 | tf_op jit(solution)/shard_map/ppermute | solution.py:242
  46.1 3.1 %copy-start.1 = (f32[4,128,1,1]{1,3,2,0:T(1,128)S(1)}, f32[4,128,1,1]{1,3,2,0:T(1,128)}, u32[]{:S(2)}) copy-start(f32[4,128,1,1]{1,3,2,0:T(1,128)} %param.9) | copy-start | bytes 6148
  46.1 3.1 %copy-start.3 = (f32[4,128]{1,0:T(4,128)S(1)}, f32[4,128]{1,0:T(4,128)}, u32[]{:S(2)}) copy-start(f32[4,128]{1,0:T(4,128)} %values_ref.1) | copy-start | bytes 6148
  46.2 3.1 %copy-start.4 = (f32[4,128]{1,0:T(4,128)S(1)}, f32[4,128]{1,0:T(4,128)}, u32[]{:S(2)}) copy-start(f32[4,128]{1,0:T(4,128)} %errors_ref.1) | copy-start | bytes 6148
  57.0 31.0 %all-to-all-start.1 = ((f32[8,2,24,256]{3,2,1,0:T(8,128)}), f32[8,2,24,256]{3,2,1,0:T(8,128)S(1)}, u32[]{:S(2)}, u32[]{:S(2)}) async-start(f32[8,2,24,256]{3,2,1,0:T(8,128)} %bitcast.3), calls=%async_computation.1 | async-start | bytes 786432 | tf_op jit(solution)/shard_map/all_to_all | solution.py:397
  68.6 10.7 %collective-permute-start.10 = (f32[2,40,256]{2,1,0:T(8,128)S(1)}, f32[2,40,256]{2,1,0:T(8,128)S(1)}, u32[]{:S(2)}, u32[]{:S(2)}) collective-permute-start(f32[2,40,256]{2,1,0:T(8,128)S(1)} %get-tuple-element.30), channel_id=1, source_target_pairs={{0,20},{4,16},{8,28},{12,24},{16,4},{20,0},{24,12},{28,8},{1,21},{... | collective-permute-start | bytes 245768 | tf_op jit(solution)/shard_map/ppermute | solution.py:406
  72.5 7.3 %collective-permute-start.11 = (f32[2,40,256]{2,1,0:T(8,128)S(1)}, f32[2,40,256]{2,1,0:T(8,128)S(1)}, u32[]{:S(2)}, u32[]{:S(2)}) collective-permute-start(f32[2,40,256]{2,1,0:T(8,128)S(1)} %get-tuple-element.31), channel_id=1, source_target_pairs={{0,24},{4,28},{8,16},{12,20},{16,8},{20,12},{24,0},{28,4},{1,25},{... | collective-permute-start | bytes 245768 | tf_op jit(solution)/shard_map/ppermute | solution.py:406
  73.9 10.7 %collective-permute-start.12 = (f32[2,40,256]{2,1,0:T(8,128)S(1)}, f32[2,40,256]{2,1,0:T(8,128)S(1)}, u32[]{:S(2)}, u32[]{:S(2)}) collective-permute-start(f32[2,40,256]{2,1,0:T(8,128)S(1)} %get-tuple-element.32), channel_id=1, source_target_pairs={{0,28},{4,24},{8,20},{12,16},{16,12},{20,8},{24,4},{28,0},{1,29},{... | collective-permute-start | bytes 245768 | tf_op jit(solution)/shard_map/ppermute | solution.py:406
  76.3 8.4 %collective-permute-start.6 = (f32[2,40,256]{2,1,0:T(8,128)S(1)}, f32[2,40,256]{2,1,0:T(8,128)S(1)}, u32[]{:S(2)}, u32[]{:S(2)}) collective-permute-start(f32[2,40,256]{2,1,0:T(8,128)S(1)} %get-tuple-element.26), channel_id=1, source_target_pairs={{0,4},{4,0},{8,12},{12,8},{16,20},{20,16},{24,28},{28,24},{1,5},{5... | collective-permute-start | bytes 245768 | tf_op jit(solution)/shard_map/ppermute | solution.py:406
  77.8 6.9 %collective-permute-start.7 = (f32[2,40,256]{2,1,0:T(8,128)S(1)}, f32[2,40,256]{2,1,0:T(8,128)S(1)}, u32[]{:S(2)}, u32[]{:S(2)}) collective-permute-start(f32[2,40,256]{2,1,0:T(8,128)S(1)} %get-tuple-element.27), channel_id=1, source_target_pairs={{0,8},{4,12},{8,0},{12,4},{16,24},{20,28},{24,16},{28,20},{1,9},{5... | collective-permute-start | bytes 245768 | tf_op jit(solution)/shard_map/ppermute | solution.py:406
  79.2 5.4 %collective-permute-start.8 = (f32[2,40,256]{2,1,0:T(8,128)S(1)}, f32[2,40,256]{2,1,0:T(8,128)S(1)}, u32[]{:S(2)}, u32[]{:S(2)}) collective-permute-start(f32[2,40,256]{2,1,0:T(8,128)S(1)} %get-tuple-element.28), channel_id=1, source_target_pairs={{0,12},{4,8},{8,4},{12,0},{16,28},{20,24},{24,20},{28,16},{1,13},{... | collective-permute-start | bytes 245768 | tf_op jit(solution)/shard_map/ppermute | solution.py:406
  79.8 8.2 %collective-permute-start.9 = (f32[2,40,256]{2,1,0:T(8,128)S(1)}, f32[2,40,256]{2,1,0:T(8,128)S(1)}, u32[]{:S(2)}, u32[]{:S(2)}) collective-permute-start(f32[2,40,256]{2,1,0:T(8,128)S(1)} %get-tuple-element.29), channel_id=1, source_target_pairs={{0,16},{4,20},{8,24},{12,28},{16,0},{20,4},{24,8},{28,12},{1,17},{... | collective-permute-start | bytes 245768 | tf_op jit(solution)/shard_map/ppermute | solution.py:406

commit v4 on v3

--- a/solution.py
+++ b/solution.py
@@ -29,20 +29,20 @@
 
 
 def pick_body(
-    owner_ref,
-    cells_ref,
-    weight_ref,
+    owner_in,
+    cells_in,
+    weight_in,
     ens_ref,
     out_ref,
     blocks_ref,
-    window,
-    in_sems,
-    out_sems,
-    *,
+    *refs,
     tile_rows,
+    first,
     gx_count,
     gy_count,
 ):
+    pieces = refs[:gx_count]
+    window, owner_ref, cells_ref, weight_ref, in_sems, out_sems, small_sems = refs[gx_count:]
     batches, nobs = cells_ref.shape
     held, _, cols = ens_ref.shape
     row_at = lax.axis_index("gx")
@@ -53,25 +53,45 @@
         rows = pl.ds(tile * tile_rows, tile_rows)
         return pltpu.make_async_copy(ens_ref.at[:, rows, :], window.at[tile], in_sems.at[tile])
 
-    def put(tile):
-        return pltpu.make_async_copy(window.at[tile], blocks_ref.at[tile], out_sems.at[tile])
-
+    def puts(slot):
+        upper = window.at[slot, :, pl.ds(0, first), :]
+        lower = window.at[row_at ^ slot, :, pl.ds(first, tile_rows - first), :]
+        return (
+            pltpu.make_async_copy(upper, blocks_ref.at[slot], out_sems.at[slot]),
+            pltpu.make_async_copy(lower, pieces[slot], out_sems.at[gx_count + slot]),
+        )
+
+    small = [
+        pltpu.make_async_copy(source, target, small_sems.at[at])
+        for at, (source, target) in enumerate(
+            [(owner_in, owner_ref), (cells_in, cells_ref), (weight_in, weight_ref)]
+        )
+    ]
+    for copy in small:
+        copy.start()
     for tile in range(gx_count):
         fetch(tile).start()
     out_ref[...] = jnp.zeros_like(out_ref)
+    for copy in small:
+        copy.wait()
     for at, (b, later) in enumerate(pairs_of(batches)):
         row = held * batches + at
         out_ref[row : row + 1, :] = jnp.where(owner_ref[later] == me, weight_ref[b : b + 1, :], 0.0)
-    for tile in range(gx_count):
-        fetch(tile).wait()
-        put(tile).start()
+    hits = []
     for b in range(batches):
-        owner_row = owner_ref[b] // gy_count
         cell = cells_ref[b : b + 1, :]
         row_hit = (lax.broadcasted_iota(jnp.int32, (tile_rows, nobs), 0) == cell // cols).astype(F32)
         row_hit = row_hit.astype(BF16)
-        row_hit = jnp.concatenate([row_hit] * 3, axis=0)
         col_hit = lax.broadcasted_iota(jnp.int32, (cols, nobs), 0) == cell % cols
+        hits.append((jnp.concatenate([row_hit] * 3, axis=0), col_hit))
+    for tile in range(gx_count):
+        fetch(tile).wait()
+    for slot in range(gx_count):
+        for copy in puts(slot):
+            copy.start()
+    for b in range(batches):
+        row_hit, col_hit = hits[b]
+        owner_row = owner_ref[b] // gy_count
         mine = owner_ref[b] % gy_count == col_at
         for m in range(held):
             values = window[owner_row, m]
@@ -85,8 +105,9 @@
             picked = jnp.sum(jnp.where(col_hit, columns, 0.0), axis=0, keepdims=True)
             row = m * batches + b
             out_ref[row : row + 1, :] = jnp.where(mine, picked, 0.0)
-    for tile in range(gx_count):
-        put(tile).wait()
+    for slot in range(gx_count):
+        for copy in puts(slot):
+            copy.wait()
 
 
 def observed_at(owner_ref, cells_ref, b, tile_rows, tile_cols, gy_count, inverse):
@@ -124,6 +145,7 @@
     errors_ref,
     weight_ref,
     got_ref,
+    other_ref,
     a_ref,
     w_ref,
     prior_ref,
@@ -139,8 +161,9 @@
     members = held * len(offsets)
     weights = jnp.zeros(got_ref.shape[1:], F32)
     row_at = lax.axis_index("gx")
+    half = got_ref.shape[0]
     for slot, offset in enumerate(offsets):
-        part = got_ref[slot]
+        part = got_ref[slot] if slot < half else other_ref[slot - half]
         weights = weights + part
         source = held * (row_at ^ offset)
         for m in range(held):
@@ -197,14 +220,20 @@
         w_ref[b, members:, nobs:] = low
 
 
-def update_body(
-    state_ref, a_ref, w_ref, x_ref, y_ref, *refs, first, tile_rows, held, inverse, spread_out
-):
-    members, rows, cols = state_ref.shape
+def update_body(a_ref, w_ref, x_ref, y_ref, *refs, first, tile_rows, parts, inverse):
+    sources, targets = refs[:parts], refs[parts : 2 * parts]
+    held, rows, cols = sources[0].shape
+    members = held * parts
     batches, nobs, _ = x_ref.shape
     row_at = lax.axis_index("gx")
     top = row_at * tile_rows + first + pl.program_id(0) * rows
-    states = [state_ref[:, r, :] for r in range(rows)]
+    if parts == 1:
+        from_ref, to_ref = sources[0], targets[0]
+    else:
+        from_ref = to_ref = refs[-1]
+        for slot, source in enumerate(sources):
+            from_ref[pl.ds(held * (row_at ^ slot), held)] = source[...]
+    states = [from_ref[:, r, :] for r in range(rows)]
     for b in range(batches):
         scaled = a_ref[b][:, : 3 * members]
         increment = w_ref[b]
@@ -224,80 +253,53 @@
                 increment, jnp.concatenate([high, low], axis=0), preferred_element_type=F32
             )
             states[r] = state + (change[:members] + change[members:])
-    if spread_out:
-        outs, whole_ref = refs[:-1], refs[-1]
-    else:
-        outs, whole_ref = (), refs[0]
     for r in range(rows):
-        whole_ref[:, r, :] = states[r]
-    for slot, out_ref in enumerate(outs):
-        out_ref[...] = whole_ref[pl.ds(held * (row_at ^ slot), held)]
+        to_ref[:, r, :] = states[r]
+    if parts > 1:
+        for slot, target in enumerate(targets):
+            target[...] = to_ref[pl.ds(held * (row_at ^ slot), held)]
 
 
 def share(picked, gx_count, gy_count):
-    got = picked[None]
+    def swap(array, axis, count, step):
+        return lax.ppermute(array, axis, [(i, i ^ step) for i in range(count)])
+
+    got = [picked[None]]
     offsets = [0]
-
-    def gather(got, step):
-        other = lax.ppermute(got, "gx", [(i, i ^ step) for i in range(gx_count)])
-        return jnp.concatenate([got, other], axis=0)
-
-    steps = [1 << bit for bit in range(gx_count.bit_length() - 1)]
-    far = steps[-1:]
-    for step in far:
-        got = gather(got, step)
-        offsets = offsets + [offset ^ step for offset in offsets]
-    others = [
-        lax.ppermute(got, "gy", [(i, i ^ step) for i in range(gy_count)])
-        for step in range(1, gy_count)
-    ]
+    for step in range(2, gx_count, 2):
+        got.append(swap(picked[None], "gx", gx_count, step))
+        offsets.append(step)
+    got = jnp.concatenate(got, axis=0)
+    others = []
+    for step in range(1, gy_count):
+        others.append(swap(got, "gy", gy_count, step))
     for other in others:
         got = got + other
-    for step in steps[:-1]:
-        got = gather(got, step)
-        offsets = offsets + [offset ^ step for offset in offsets]
-    return got, offsets
+    other = swap(got, "gx", gx_count, 1)
+    return (got, other), offsets + [offset ^ 1 for offset in offsets]
 
 
 def whole(array):
     return pl.BlockSpec(array.shape, lambda i: (0,) * array.ndim)
 
 
-def update(state, tables, first, depth, tile_rows, inverse, gx_count, spread_out):
-    members, _, cols = state.shape
+def update(sources, tables, first, tile_rows, inverse):
+    parts = len(sources)
+    held, depth, cols = sources[0].shape
+    members = held * parts
     rows = ROWS
-    held = members // gx_count
     batches, nobs = tables[0].shape[:2]
     cells = depth * cols * batches * nobs
-    start = first // rows
-    if spread_out:
-        out_specs = [pl.BlockSpec((held, rows, cols), lambda i: (0, i, 0))] * gx_count
-        out_shape = [jax.ShapeDtypeStruct((held, depth, cols), F32)] * gx_count
-        scratch = [pltpu.VMEM((members, rows, cols), F32)]
-    else:
-        out_specs = pl.BlockSpec((members, rows, cols), lambda i: (0, i, 0))
-        out_shape = jax.ShapeDtypeStruct((members, depth, cols), F32)
-        scratch = []
+    blocks = [pl.BlockSpec((held, rows, cols), lambda i: (0, i, 0))] * parts
     return pl.pallas_call(
         functools.partial(
-            update_body,
-            first=first,
-            tile_rows=tile_rows,
-            inverse=inverse,
-            held=held,
-            spread_out=spread_out,
+            update_body, first=first, tile_rows=tile_rows, parts=parts, inverse=inverse
         ),
         grid=(depth // rows,),
-        in_specs=[
-            pl.BlockSpec((members, rows, cols), lambda i: (0, start + i, 0)),
-            whole(tables[0]),
-            whole(tables[1]),
-            whole(tables[2]),
-            whole(tables[3]),
-        ],
-        out_specs=out_specs,
-        out_shape=out_shape,
-        scratch_shapes=scratch,
+        in_specs=[whole(table) for table in tables] + blocks,
+        out_specs=blocks,
+        out_shape=[jax.ShapeDtypeStruct((held, depth, cols), F32)] * parts,
+        scratch_shapes=[pltpu.VMEM((members, rows, cols), F32)] if parts > 1 else [],
         cost_estimate=pl.CostEstimate(
             flops=cells * members * 10,
             bytes_accessed=8 * members * depth * cols,
@@ -305,7 +307,7 @@
         ),
         compiler_params=LIGHT,
         name="update",
-    )(state, *tables)
+    )(*tables, *sources)
 
 
 def assemble_body(whole_ref, *refs, first, tile_rows, here):
@@ -344,26 +346,36 @@
     payload = -(-payload // 8) * 8
     in_smem = pl.BlockSpec(memory_space=SMEM)
     in_vmem = pl.BlockSpec(memory_space=VMEM)
-    anywhere = pl.BlockSpec(memory_space=pl.ANY)
+    in_hbm = pl.BlockSpec(memory_space=pltpu.MemorySpace.HBM)
     geometry = dict(tile_rows=tile_rows, tile_cols=tile_cols, gy_count=gy_count, inverse=inverse)
 
-    picked, blocks = pl.pallas_call(
-        functools.partial(pick_body, tile_rows=tile_rows, gx_count=gx_count, gy_count=gy_count),
-        in_specs=[in_smem, in_vmem, in_vmem, anywhere],
-        out_specs=[in_vmem, anywhere],
+    first = tile_rows * FIRST_EIGHTHS // 8
+    rest = tile_rows - first
+    picked, blocks, *pieces = pl.pallas_call(
+        functools.partial(
+            pick_body, tile_rows=tile_rows, first=first, gx_count=gx_count, gy_count=gy_count
+        ),
+        in_specs=[in_hbm] * 4,
+        out_specs=[in_vmem] + [in_hbm] * (1 + gx_count),
         out_shape=[
             jax.ShapeDtypeStruct((payload, nobs), F32),
-            jax.ShapeDtypeStruct((gx_count, held, tile_rows, tile_cols), F32),
-        ],
+            jax.ShapeDtypeStruct((gx_count, held, first, tile_cols), F32),
+        ]
+        + [jax.ShapeDtypeStruct((held, rest, tile_cols), F32)] * gx_count,
         scratch_shapes=[
             pltpu.VMEM((gx_count, held, tile_rows, tile_cols), F32),
+            pltpu.SMEM((batches,), jnp.int32),
+            pltpu.VMEM((batches, nobs), jnp.int32),
+            pltpu.VMEM((batches, nobs), F32),
             pltpu.SemaphoreType.DMA((gx_count,)),
-            pltpu.SemaphoreType.DMA((gx_count,)),
+            pltpu.SemaphoreType.DMA((2 * gx_count,)),
+            pltpu.SemaphoreType.DMA((3,)),
         ],
         name="pick",
     )(owner_device, obs_cells, weight, ensemble)
     state = lax.all_to_all(blocks, "gx", split_axis=0, concat_axis=0, tiled=True)
-    state = state.reshape(members, tile_rows, tile_cols)
+    for slot in range(1, gx_count):
+        pieces[slot] = lax.ppermute(pieces[slot], "gx", [(i, i ^ slot) for i in range(gx_count)])
     places = pl.pallas_call(
         functools.partial(tables_body, **geometry),
         in_specs=[in_smem, in_vmem],
@@ -377,9 +389,9 @@
     )(owner_device, obs_cells)
     got, offsets = share(picked, gx_count, gy_count)
     wide = -(-3 * members // nobs) * nobs
-    factors = pl.pallas_call(
+    chain = pl.pallas_call(
         functools.partial(chain_body, held=held, offsets=offsets, **geometry),
-        in_specs=[in_smem] + [in_vmem] * 5,
+        in_specs=[in_smem] + [in_vmem] * 6,
         out_specs=[in_vmem] * 2,
         out_shape=[
             jax.ShapeDtypeStruct((batches, nobs, wide), BF16),
@@ -388,12 +400,11 @@
         scratch_shapes=[pltpu.VMEM((batches, members, nobs), F32)],
         compiler_params=LIGHT,
         name="chain",
-    )(owner_device, obs_cells, obs_values, obs_error, weight, got)
+    )
+    factors = chain(owner_device, obs_cells, obs_values, obs_error, weight, *got)
     tables = [*factors, *places]
 
-    first = tile_rows * FIRST_EIGHTHS // 8
-    rest = tile_rows - first
-    upper = update(state, tables, 0, first, tile_rows, inverse, gx_count, False)
+    (upper,) = update([state.reshape(members, first, tile_cols)], tables, 0, tile_rows, inverse)
     upper = lax.all_to_all(
         upper.reshape(gx_count, held, first, tile_cols),
         "gx",
@@ -401,7 +412,7 @@
         concat_axis=0,
         tiled=True,
     )
-    lower = [*update(state, tables, first, rest, tile_rows, inverse, gx_count, True)]
+    lower = [*update(pieces, tables, first, tile_rows, inverse)]
     for slot in range(1, gx_count):
         lower[slot] = lax.ppermute(
             lower[slot], "gx", [(i, i ^ slot) for i in range(gx_count)]
@@ -409,7 +420,7 @@
     return pl.pallas_call(
         functools.partial(assemble_body, first=first, tile_rows=tile_rows, here=ROWS),
         in_specs=[in_vmem] * (1 + gx_count),
-        out_specs=anywhere,
+        out_specs=in_hbm,
         out_shape=jax.ShapeDtypeStruct(ensemble.shape, F32),
         scratch_shapes=[pltpu.SemaphoreType.DMA((2 * gx_count,))],
         compiler_params=LIGHT,

time: 89.4 us -> 95.1 us (1.064)
  starting transfers between devices: 31.8 us -> 44.9 us
  waiting for transfers between devices: 36.2 us -> 27.7 us
    ppermute x6 -> x14, starting transfers between devices: 6.27 us -> 22.3 us  [the longest x7 14.1 us: local(): lax.ppermute(pieces[slot], 'gx', [(i, i ^ slot) for i in range(gx_count)])]
    ppermute x6 -> x14, waiting for transfers between devices: 31.4 us -> 21.5 us  [the longest x7 12.3 us: swap(): return lax.ppermute(array, axis, [(i, i ^ step) for i in range(count)])]
    ppermute x7, starting transfers between devices: 14.6 us -> 11.5 us  [local(): lax.ppermute(lower[slot], 'gx', [(i, i ^ slot) for i in range(gx_count)])]
    ppermute x7, waiting for transfers between devices: 4.75 us -> 6.15 us  [local(): lax.ppermute(lower[slot], 'gx', [(i, i ^ slot) for i in range(gx_count)])]
  transfers between devices with their start and end apart: 15 -> 23, of which waited for: 7 -> 9; matrix products, arithmetic and copies ran while one was open for 0% -> 0% of each run, Pallas kernels for 12% -> 12%
where the time goes in v4:
time: 95.1 us; the launch traced here: 94 us
  starting transfers between devices  44.9 us (47%)
  waiting for transfers between devices  27.7 us (29%)
  Pallas kernels  21.2 us (22%)
    ppermute x7, starting transfers between devices, local(): lax.ppermute(pieces[slot], 'gx', [(i, i ^ slot) for i in range(gx_count)])  14.1 us
    pallas_call x2, Pallas kernels, update(): pl.pallas_call(functools.partial(update_body, first=first, tile_rows=tile...  13.6 us
    ppermute x7, waiting for transfers between devices, swap(): return lax.ppermute(array, axis, [(i, i ^ step) for i in range(count)])  12.3 us
    ppermute x7, starting transfers between devices, local(): lax.ppermute(lower[slot], 'gx', [(i, i ^ slot) for i in range(gx_count)])  11.5 us
    ppermute x7, waiting for transfers between devices, local(): lax.ppermute(pieces[slot], 'gx', [(i, i ^ slot) for i in range(gx_count)])  9.18 us
    ppermute x7, starting transfers between devices, swap(): return lax.ppermute(array, axis, [(i, i ^ step) for i in range(count)])  8.19 us
    all_to_all x1, starting transfers between devices, local(): lax.all_to_all(blocks, 'gx', split_axis=0, concat_axis=0, tiled=True)  7.29 us
    ppermute x7, waiting for transfers between devices, local(): lax.ppermute(lower[slot], 'gx', [(i, i ^ slot) for i in range(gx_count)])  6.15 us
  transfers between devices with their start and end apart: 23, of which 9 were waited for; matrix products, arithmetic and copies ran while one was open for 0% of the time, Pallas kernels for 12%

profile of v4, /device:TPU:0, one launch (start us, length us, event | category | flops | bytes accessed | tf_op | source)
XLA Modules:
  0.0 94.0 jit_solution(15068453404570842853)
XLA Ops:
  0.0 3.4 %pick.1 = (f32[16,128]{1,0:T(8,128)}, f32[8,2,24,256]{3,2,1,0:T(8,128)}, f32[2,40,256]{2,1,0:T(8,128)}, f32[2,40,256]{2,1,0:T(8,128)}, f32[2,40,256]{2,1,0:T(8,1...) custom-call(s32[4]{0:T(128)} %owner_ref.3, ...), custom_call_target="tpu_custom_call" | custom-call | tf_op jit(solution)/shard_map/pick/pallas_call | solution.py:354
  3.4 7.3 %all-to-all-start = ((f32[8,2,24,256]{3,2,1,0:T(8,128)}), f32[8,2,24,256]{3,2,1,0:T(8,128)S(1)}, u32[]{:S(2)}, u32[]{:S(2)}) async-start(f32[8,2,24,256]{3,2,1,0:T(8,128)} %get-tuple-element.32), calls=%async_computation | async-start | bytes 786432 | tf_op jit(solution)/shard_map/all_to_all | solution.py:376
  10.7 3.8 %collective-permute-start.2 = (f32[1,16,128]{2,1,0:T(8,128)S(1)}, f32[1,16,128]{2,1,0:T(8,128)S(1)}, u32[]{:S(2)}, u32[]{:S(2)}) collective-permute-start(f32[1,16,128]{2,1,0:T(8,128)S(1)} %bitcast.7), channel_id=1, source_target_pairs={{0,24},{4,28},{8,16},{12,20},{16,8},{20,12},{24,0},{28,4},{1,25},{... | collective-permute-start | bytes 24584 | tf_op jit(solution)/shard_map/ppermute | solution.py:265
  15.2 6.4 %collective-permute-done.2 = f32[1,16,128]{2,1,0:T(8,128)S(1)} collective-permute-done((f32[1,16,128]{2,1,0:T(8,128)S(1)}, f32[1,16,128]{2,1,0:T(8,128)S(1)}, u32[]{:S(2)}, u32[]{:S(2)}) %collective-permute-start.2) | collective-permute-done | bytes 8224 | tf_op jit(solution)/shard_map/ppermute | solution.py:265
  21.6 1.5 %collective-permute-done.1 = f32[1,16,128]{2,1,0:T(8,128)S(1)} collective-permute-done((f32[1,16,128]{2,1,0:T(8,128)S(1)}, f32[1,16,128]{2,1,0:T(8,128)S(1)}, u32[]{:S(2)}, u32[]{:S(2)}) %collective-permute-start.1) | collective-permute-done | bytes 8224 | tf_op jit(solution)/shard_map/ppermute | solution.py:265
  23.1 1.6 %collective-permute-start.4 = (f32[4,16,128]{2,1,0:T(8,128)S(1)}, f32[4,16,128]{2,1,0:T(8,128)S(1)}, u32[]{:S(2)}, u32[]{:S(2)}) collective-permute-start(f32[4,16,128]{2,1,0:T(8,128)S(1)} %pad_maximum_fusion), channel_id=1, source_target_pairs={{0,2},{1,3},{2,0},{3,1},{4,6},{5,7},{6,4},{7,5},{8,10},{9,11},{10,... | collective-permute-start | bytes 98312 | tf_op jit(solution)/shard_map/ppermute | solution.py:265
  25.3 1.8 %collective-permute-done.4 = f32[4,16,128]{2,1,0:T(8,128)S(1)} collective-permute-done((f32[4,16,128]{2,1,0:T(8,128)S(1)}, f32[4,16,128]{2,1,0:T(8,128)S(1)}, u32[]{:S(2)}, u32[]{:S(2)}) %collective-permute-start.4) | collective-permute-done | bytes 32800 | tf_op jit(solution)/shard_map/ppermute | solution.py:265
  28.1 1.5 %collective-permute-start.6 = (f32[4,16,128]{2,1,0:T(8,128)S(1)}, f32[4,16,128]{2,1,0:T(8,128)S(1)}, u32[]{:S(2)}, u32[]{:S(2)}) collective-permute-start(f32[4,16,128]{2,1,0:T(8,128)S(1)} %add_add_fusion.got_ref), channel_id=1, source_target_pairs={{0,4},{4,0},{8,12},{12,8},{16,20},{20,16},{24,28},{28,24},{1,5},{5... | collective-permute-start | bytes 98312 | tf_op jit(solution)/shard_map/ppermute | solution.py:265
  30.4 1.7 %collective-permute-done.6.other_ref = f32[4,16,128]{2,1,0:T(8,128)S(1)} collective-permute-done((f32[4,16,128]{2,1,0:T(8,128)S(1)}, f32[4,16,128]{2,1,0:T(8,128)S(1)}, u32[]{:S(2)}, u32[]{:S(2)}) %collective-permute-start.6) | collective-permute-done | bytes 32800 | tf_op jit(solution)/shard_map/ppermute | solution.py:265
  32.1 2.3 %chain.1 = (bf16[4,128,128]{2,1,0:T(8,128)(2,1)S(1)}, bf16[4,32,256]{2,1,0:T(8,128)(2,1)S(1)}) custom-call(s32[4]{0:T(128)S(1)} %copy-done.2, s32[4,128]{1,0:T(4,128)S(1)} %copy-done, f32[4,128]{1,0:T(4,128)S(1)} %copy-done.3, f32[4,128]{1,0:T(4,128)S(1)} %copy-done.4, f32[4,128]{1,0:T(4,128)S(1)} %bitcast.6, f32[4,16,128]{2,1,0:T(8,128)S(1)} %add_add_fusion.got_ref, ...), custom_call_target="tpu_custom_call" | custom-call | tf_op jit(solution)/shard_map/chain/pallas_call | solution.py:404
  34.4 5.3 %update.2 = f32[16,24,256]{2,1,0:T(8,128)} custom-call(bf16[4,128,128]{2,1,0:T(8,128)(2,1)S(1)} %get-tuple-element.28.a_ref, bf16[4,32,256]{2,1,0:T(8,128)(2,1)S(1)} %get-tuple-element.29.w_ref, f32[4,128,128]{2,1,0:T(8,128)S(1)} %get-tuple-element.30.x_ref, f32[4,128,256]{2,1,0:T(8,128)S(1)} %get-tuple-element.31.y_ref, f32[16,24,256]{2,1,0:T(8,128)S(1)} %bitcast.4), custom_call_target="tpu_custom_call" | custom-call | flops 503316480 | bytes 786432 | tf_op jit(solution)/shard_map/update/pallas_call | solution.py:294
  39.8 3.8 %all-to-all-start.1 = ((f32[8,2,24,256]{3,2,1,0:T(8,128)}), f32[8,2,24,256]{3,2,1,0:T(8,128)S(1)}, u32[]{:S(2)}, u32[]{:S(2)}) async-start(f32[8,2,24,256]{3,2,1,0:T(8,128)} %bitcast.3), calls=%async_computation.1 | async-start | bytes 786432 | tf_op jit(solution)/shard_map/all_to_all | solution.py:408
  43.6 2.0 %collective-permute-start.7 = (f32[2,40,256]{2,1,0:T(8,128)S(1)}, f32[2,40,256]{2,1,0:T(8,128)S(1)}, u32[]{:S(2)}, u32[]{:S(2)}) collective-permute-start(f32[2,40,256]{2,1,0:T(8,128)S(1)} %copy-done.13), channel_id=1, source_target_pairs={{0,4},{4,0},{8,12},{12,8},{16,20},{20,16},{24,28},{28,24},{1,5},{5... | collective-permute-start | bytes 245768 | tf_op jit(solution)/shard_map/ppermute | solution.py:378
  47.2 2.8 %collective-permute-start.10 = (f32[2,40,256]{2,1,0:T(8,128)S(1)}, f32[2,40,256]{2,1,0:T(8,128)S(1)}, u32[]{:S(2)}, u32[]{:S(2)}) collective-permute-start(f32[2,40,256]{2,1,0:T(8,128)S(1)} %copy-done.10), channel_id=1, source_target_pairs={{0,16},{4,20},{8,24},{12,28},{16,0},{20,4},{24,8},{28,12},{1,17},{... | collective-permute-start | bytes 245768 | tf_op jit(solution)/shard_map/ppermute | solution.py:378
  51.5 3.3 %collective-permute-start.12 = (f32[2,40,256]{2,1,0:T(8,128)S(1)}, f32[2,40,256]{2,1,0:T(8,128)S(1)}, u32[]{:S(2)}, u32[]{:S(2)}) collective-permute-start(f32[2,40,256]{2,1,0:T(8,128)S(1)} %copy-done.8), channel_id=1, source_target_pairs={{0,24},{4,28},{8,16},{12,20},{16,8},{20,12},{24,0},{28,4},{1,25},{... | collective-permute-start | bytes 245768 | tf_op jit(solution)/shard_map/ppermute | solution.py:378
  54.8 3.0 %collective-permute-start.13 = (f32[2,40,256]{2,1,0:T(8,128)S(1)}, f32[2,40,256]{2,1,0:T(8,128)S(1)}, u32[]{:S(2)}, u32[]{:S(2)}) collective-permute-start(f32[2,40,256]{2,1,0:T(8,128)S(1)} %copy-done.7), channel_id=1, source_target_pairs={{0,28},{4,24},{8,20},{12,16},{16,12},{20,8},{24,4},{28,0},{1,29},{... | collective-permute-start | bytes 245768 | tf_op jit(solution)/shard_map/ppermute | solution.py:378
  57.8 6.7 %collective-permute-done.10.refs_4_ = f32[2,40,256]{2,1,0:T(8,128)S(1)} collective-permute-done((f32[2,40,256]{2,1,0:T(8,128)S(1)}, f32[2,40,256]{2,1,0:T(8,128)S(1)}, u32[]{:S(2)}, u32[]{:S(2)}) %collective-permute-start.10) | collective-permute-done | bytes 81952 | tf_op jit(solution)/shard_map/ppermute | solution.py:378
  64.5 2.5 %collective-permute-done.11.refs_5_ = f32[2,40,256]{2,1,0:T(8,128)S(1)} collective-permute-done((f32[2,40,256]{2,1,0:T(8,128)S(1)}, f32[2,40,256]{2,1,0:T(8,128)S(1)}, u32[]{:S(2)}, u32[]{:S(2)}) %collective-permute-start.11) | collective-permute-done | bytes 81952 | tf_op jit(solution)/shard_map/ppermute | solution.py:378
  67.0 8.3 %update.3 = (f32[2,40,256]{2,1,0:T(8,128)S(1)}, f32[2,40,256]{2,1,0:T(8,128)S(1)}, f32[2,40,256]{2,1,0:T(8,128)S(1)}, f32[2,40,256]{2,1,0:T(8,128)S(1)}, f32[2,4...) custom-call(bf16[4,128,128]{2,1,0:T(8,128)(2,1)S(1)} %get-tuple-element.2, ...), custom_call_target="tpu_custom_call" | custom-call | flops 838860800 | bytes 1310720 | tf_op jit(solution)/shard_map/update/pallas_call | solution.py:294
  76.0 2.3 %collective-permute-start.15 = (f32[2,40,256]{2,1,0:T(8,128)S(1)}, f32[2,40,256]{2,1,0:T(8,128)S(1)}, u32[]{:S(2)}, u32[]{:S(2)}) collective-permute-start(f32[2,40,256]{2,1,0:T(8,128)S(1)} %get-tuple-element.43), channel_id=1, source_target_pairs={{0,8},{4,12},{8,0},{12,4},{16,24},{20,28},{24,16},{28,20},{1,9},{5... | collective-permute-start | bytes 245768 | tf_op jit(solution)/shard_map/ppermute | solution.py:417
  79.1 2.1 %collective-permute-start.17 = (f32[2,40,256]{2,1,0:T(8,128)S(1)}, f32[2,40,256]{2,1,0:T(8,128)S(1)}, u32[]{:S(2)}, u32[]{:S(2)}) collective-permute-start(f32[2,40,256]{2,1,0:T(8,128)S(1)} %get-tuple-element.45), channel_id=1, source_target_pairs={{0,16},{4,20},{8,24},{12,28},{16,0},{20,4},{24,8},{28,12},{1,17},{... | collective-permute-start | bytes 245768 | tf_op jit(solution)/shard_map/ppermute | solution.py:417
  83.5 3.2 %collective-permute-start.20 = (f32[2,40,256]{2,1,0:T(8,128)S(1)}, f32[2,40,256]{2,1,0:T(8,128)S(1)}, u32[]{:S(2)}, u32[]{:S(2)}) collective-permute-start(f32[2,40,256]{2,1,0:T(8,128)S(1)} %get-tuple-element.48), channel_id=1, source_target_pairs={{0,28},{4,24},{8,20},{12,16},{16,12},{20,8},{24,4},{28,0},{1,29},{... | collective-permute-start | bytes 245768 | tf_op jit(solution)/shard_map/ppermute | solution.py:417
  86.7 4.4 %collective-permute-done.17.refs_4_ = f32[2,40,256]{2,1,0:T(8,128)S(1)} collective-permute-done((f32[2,40,256]{2,1,0:T(8,128)S(1)}, f32[2,40,256]{2,1,0:T(8,128)S(1)}, u32[]{:S(2)}, u32[]{:S(2)}) %collective-permute-start.17) | collective-permute-done | bytes 81952 | tf_op jit(solution)/shard_map/ppermute | solution.py:417
  91.1 1.8 %collective-permute-done.18.refs_5_ = f32[2,40,256]{2,1,0:T(8,128)S(1)} collective-permute-done((f32[2,40,256]{2,1,0:T(8,128)S(1)}, f32[2,40,256]{2,1,0:T(8,128)S(1)}, u32[]{:S(2)}, u32[]{:S(2)}) %collective-permute-start.18) | collective-permute-done | bytes 81952 | tf_op jit(solution)/shard_map/ppermute | solution.py:417
  (58 shorter events, 11.1 us)
Async XLA Ops:
  3.4 31.0 %all-to-all-start = ((f32[8,2,24,256]{3,2,1,0:T(8,128)}), f32[8,2,24,256]{3,2,1,0:T(8,128)S(1)}, u32[]{:S(2)}, u32[]{:S(2)}) async-start(f32[8,2,24,256]{3,2,1,0:T(8,128)} %get-tuple-element.32), calls=%async_computation | async-start | bytes 786432 | tf_op jit(solution)/shard_map/all_to_all | solution.py:376
  10.7 10.9 %collective-permute-start.2 = (f32[1,16,128]{2,1,0:T(8,128)S(1)}, f32[1,16,128]{2,1,0:T(8,128)S(1)}, u32[]{:S(2)}, u32[]{:S(2)}) collective-permute-start(f32[1,16,128]{2,1,0:T(8,128)S(1)} %bitcast.7), channel_id=1, source_target_pairs={{0,24},{4,28},{8,16},{12,20},{16,8},{20,12},{24,0},{28,4},{1,25},{... | collective-permute-start | bytes 24584 | tf_op jit(solution)/shard_map/ppermute | solution.py:265
  14.6 8.6 %collective-permute-start.1 = (f32[1,16,128]{2,1,0:T(8,128)S(1)}, f32[1,16,128]{2,1,0:T(8,128)S(1)}, u32[]{:S(2)}, u32[]{:S(2)}) collective-permute-start(f32[1,16,128]{2,1,0:T(8,128)S(1)} %bitcast.8), channel_id=1, source_target_pairs={{0,16},{4,20},{8,24},{12,28},{16,0},{20,4},{24,8},{28,12},{1,17},{... | collective-permute-start | bytes 24584 | tf_op jit(solution)/shard_map/ppermute | solution.py:265
  14.6 8.6 %collective-permute-start = (f32[1,16,128]{2,1,0:T(8,128)S(1)}, f32[1,16,128]{2,1,0:T(8,128)S(1)}, u32[]{:S(2)}, u32[]{:S(2)}) collective-permute-start(f32[1,16,128]{2,1,0:T(8,128)S(1)} %bitcast.9), channel_id=1, source_target_pairs={{0,8},{4,12},{8,0},{12,4},{16,24},{20,28},{24,16},{28,20},{1,9},{5... | collective-permute-start | bytes 24584 | tf_op jit(solution)/shard_map/ppermute | solution.py:265
  23.1 4.0 %collective-permute-start.4 = (f32[4,16,128]{2,1,0:T(8,128)S(1)}, f32[4,16,128]{2,1,0:T(8,128)S(1)}, u32[]{:S(2)}, u32[]{:S(2)}) collective-permute-start(f32[4,16,128]{2,1,0:T(8,128)S(1)} %pad_maximum_fusion), channel_id=1, source_target_pairs={{0,2},{1,3},{2,0},{3,1},{4,6},{5,7},{6,4},{7,5},{8,10},{9,11},{10,... | collective-permute-start | bytes 98312 | tf_op jit(solution)/shard_map/ppermute | solution.py:265
  24.7 3.3 %collective-permute-start.5 = (f32[4,16,128]{2,1,0:T(8,128)S(1)}, f32[4,16,128]{2,1,0:T(8,128)S(1)}, u32[]{:S(2)}, u32[]{:S(2)}) collective-permute-start(f32[4,16,128]{2,1,0:T(8,128)S(1)} %pad_maximum_fusion), channel_id=1, source_target_pairs={{0,3},{1,2},{2,1},{3,0},{4,7},{5,6},{6,5},{7,4},{8,11},{9,10},{10,... | collective-permute-start | bytes 98312 | tf_op jit(solution)/shard_map/ppermute | solution.py:265
  24.7 3.3 %collective-permute-start.3 = (f32[4,16,128]{2,1,0:T(8,128)S(1)}, f32[4,16,128]{2,1,0:T(8,128)S(1)}, u32[]{:S(2)}, u32[]{:S(2)}) collective-permute-start(f32[4,16,128]{2,1,0:T(8,128)S(1)} %pad_maximum_fusion), channel_id=1, source_target_pairs={{0,1},{1,0},{2,3},{3,2},{4,5},{5,4},{6,7},{7,6},{8,9},{9,8},{10,11... | collective-permute-start | bytes 98312 | tf_op jit(solution)/shard_map/ppermute | solution.py:265
  28.1 4.0 %collective-permute-start.6 = (f32[4,16,128]{2,1,0:T(8,128)S(1)}, f32[4,16,128]{2,1,0:T(8,128)S(1)}, u32[]{:S(2)}, u32[]{:S(2)}) collective-permute-start(f32[4,16,128]{2,1,0:T(8,128)S(1)} %add_add_fusion.got_ref), channel_id=1, source_target_pairs={{0,4},{4,0},{8,12},{12,8},{16,20},{20,16},{24,28},{28,24},{1,5},{5... | collective-permute-start | bytes 98312 | tf_op jit(solution)/shard_map/ppermute | solution.py:265
  39.8 27.2 %copy-start.5 = (f32[2,40,256]{2,1,0:T(8,128)S(1)}, f32[2,40,256]{2,1,0:T(8,128)}, u32[]{:S(2)}) copy-start(f32[2,40,256]{2,1,0:T(8,128)} %get-tuple-element.33.refs_0_) | copy-start | bytes 245764
  39.8 53.1 %all-to-all-start.1 = ((f32[8,2,24,256]{3,2,1,0:T(8,128)}), f32[8,2,24,256]{3,2,1,0:T(8,128)S(1)}, u32[]{:S(2)}, u32[]{:S(2)}) async-start(f32[8,2,24,256]{3,2,1,0:T(8,128)} %bitcast.3), calls=%async_computation.1 | async-start | bytes 786432 | tf_op jit(solution)/shard_map/all_to_all | solution.py:408
  43.6 7.9 %collective-permute-start.7 = (f32[2,40,256]{2,1,0:T(8,128)S(1)}, f32[2,40,256]{2,1,0:T(8,128)S(1)}, u32[]{:S(2)}, u32[]{:S(2)}) collective-permute-start(f32[2,40,256]{2,1,0:T(8,128)S(1)} %copy-done.13), channel_id=1, source_target_pairs={{0,4},{4,0},{8,12},{12,8},{16,20},{20,16},{24,28},{28,24},{1,5},{5... | collective-permute-start | bytes 245768 | tf_op jit(solution)/shard_map/ppermute | solution.py:378
  45.6 9.1 %collective-permute-start.8 = (f32[2,40,256]{2,1,0:T(8,128)S(1)}, f32[2,40,256]{2,1,0:T(8,128)S(1)}, u32[]{:S(2)}, u32[]{:S(2)}) collective-permute-start(f32[2,40,256]{2,1,0:T(8,128)S(1)} %copy-done.12), channel_id=1, source_target_pairs={{0,8},{4,12},{8,0},{12,4},{16,24},{20,28},{24,16},{28,20},{1,9},{5... | collective-permute-start | bytes 245768 | tf_op jit(solution)/shard_map/ppermute | solution.py:378
  47.1 10.7 %collective-permute-start.9 = (f32[2,40,256]{2,1,0:T(8,128)S(1)}, f32[2,40,256]{2,1,0:T(8,128)S(1)}, u32[]{:S(2)}, u32[]{:S(2)}) collective-permute-start(f32[2,40,256]{2,1,0:T(8,128)S(1)} %copy-done.11), channel_id=1, source_target_pairs={{0,12},{4,8},{8,4},{12,0},{16,28},{20,24},{24,20},{28,16},{1,13},{... | collective-permute-start | bytes 245768 | tf_op jit(solution)/shard_map/ppermute | solution.py:378
  47.2 17.3 %collective-permute-start.10 = (f32[2,40,256]{2,1,0:T(8,128)S(1)}, f32[2,40,256]{2,1,0:T(8,128)S(1)}, u32[]{:S(2)}, u32[]{:S(2)}) collective-permute-start(f32[2,40,256]{2,1,0:T(8,128)S(1)} %copy-done.10), channel_id=1, source_target_pairs={{0,16},{4,20},{8,24},{12,28},{16,0},{20,4},{24,8},{28,12},{1,17},{... | collective-permute-start | bytes 245768 | tf_op jit(solution)/shard_map/ppermute | solution.py:378
  50.0 16.9 %collective-permute-start.11 = (f32[2,40,256]{2,1,0:T(8,128)S(1)}, f32[2,40,256]{2,1,0:T(8,128)S(1)}, u32[]{:S(2)}, u32[]{:S(2)}) collective-permute-start(f32[2,40,256]{2,1,0:T(8,128)S(1)} %copy-done.9), channel_id=1, source_target_pairs={{0,20},{4,16},{8,28},{12,24},{16,4},{20,0},{24,12},{28,8},{1,21},{... | collective-permute-start | bytes 245768 | tf_op jit(solution)/shard_map/ppermute | solution.py:378
  51.5 15.5 %collective-permute-start.12 = (f32[2,40,256]{2,1,0:T(8,128)S(1)}, f32[2,40,256]{2,1,0:T(8,128)S(1)}, u32[]{:S(2)}, u32[]{:S(2)}) collective-permute-start(f32[2,40,256]{2,1,0:T(8,128)S(1)} %copy-done.8), channel_id=1, source_target_pairs={{0,24},{4,28},{8,16},{12,20},{16,8},{20,12},{24,0},{28,4},{1,25},{... | collective-permute-start | bytes 245768 | tf_op jit(solution)/shard_map/ppermute | solution.py:378
  54.8 12.2 %collective-permute-start.13 = (f32[2,40,256]{2,1,0:T(8,128)S(1)}, f32[2,40,256]{2,1,0:T(8,128)S(1)}, u32[]{:S(2)}, u32[]{:S(2)}) collective-permute-start(f32[2,40,256]{2,1,0:T(8,128)S(1)} %copy-done.7), channel_id=1, source_target_pairs={{0,28},{4,24},{8,20},{12,16},{16,12},{20,8},{24,4},{28,0},{1,29},{... | collective-permute-start | bytes 245768 | tf_op jit(solution)/shard_map/ppermute | solution.py:378
  75.3 6.8 %collective-permute-start.14 = (f32[2,40,256]{2,1,0:T(8,128)S(1)}, f32[2,40,256]{2,1,0:T(8,128)S(1)}, u32[]{:S(2)}, u32[]{:S(2)}) collective-permute-start(f32[2,40,256]{2,1,0:T(8,128)S(1)} %get-tuple-element.42), channel_id=1, source_target_pairs={{0,4},{4,0},{8,12},{12,8},{16,20},{20,16},{24,28},{28,24},{1,5},{5... | collective-permute-start | bytes 245768 | tf_op jit(solution)/shard_map/ppermute | solution.py:417
  76.0 7.6 %collective-permute-start.15 = (f32[2,40,256]{2,1,0:T(8,128)S(1)}, f32[2,40,256]{2,1,0:T(8,128)S(1)}, u32[]{:S(2)}, u32[]{:S(2)}) collective-permute-start(f32[2,40,256]{2,1,0:T(8,128)S(1)} %get-tuple-element.43), channel_id=1, source_target_pairs={{0,8},{4,12},{8,0},{12,4},{16,24},{20,28},{24,16},{28,20},{1,9},{5... | collective-permute-start | bytes 245768 | tf_op jit(solution)/shard_map/ppermute | solution.py:417
  78.2 8.5 %collective-permute-start.16 = (f32[2,40,256]{2,1,0:T(8,128)S(1)}, f32[2,40,256]{2,1,0:T(8,128)S(1)}, u32[]{:S(2)}, u32[]{:S(2)}) collective-permute-start(f32[2,40,256]{2,1,0:T(8,128)S(1)} %get-tuple-element.44), channel_id=1, source_target_pairs={{0,12},{4,8},{8,4},{12,0},{16,28},{20,24},{24,20},{28,16},{1,13},{... | collective-permute-start | bytes 245768 | tf_op jit(solution)/shard_map/ppermute | solution.py:417
  79.1 12.0 %collective-permute-start.17 = (f32[2,40,256]{2,1,0:T(8,128)S(1)}, f32[2,40,256]{2,1,0:T(8,128)S(1)}, u32[]{:S(2)}, u32[]{:S(2)}) collective-permute-start(f32[2,40,256]{2,1,0:T(8,128)S(1)} %get-tuple-element.45), channel_id=1, source_target_pairs={{0,16},{4,20},{8,24},{12,28},{16,0},{20,4},{24,8},{28,12},{1,17},{... | collective-permute-start | bytes 245768 | tf_op jit(solution)/shard_map/ppermute | solution.py:417
  81.2 11.7 %collective-permute-start.18 = (f32[2,40,256]{2,1,0:T(8,128)S(1)}, f32[2,40,256]{2,1,0:T(8,128)S(1)}, u32[]{:S(2)}, u32[]{:S(2)}) collective-permute-start(f32[2,40,256]{2,1,0:T(8,128)S(1)} %get-tuple-element.46), channel_id=1, source_target_pairs={{0,20},{4,16},{8,28},{12,24},{16,4},{20,0},{24,12},{28,8},{1,21},{... | collective-permute-start | bytes 245768 | tf_op jit(solution)/shard_map/ppermute | solution.py:417
  82.1 10.8 %collective-permute-start.19 = (f32[2,40,256]{2,1,0:T(8,128)S(1)}, f32[2,40,256]{2,1,0:T(8,128)S(1)}, u32[]{:S(2)}, u32[]{:S(2)}) collective-permute-start(f32[2,40,256]{2,1,0:T(8,128)S(1)} %get-tuple-element.47), channel_id=1, source_target_pairs={{0,24},{4,28},{8,16},{12,20},{16,8},{20,12},{24,0},{28,4},{1,25},{... | collective-permute-start | bytes 245768 | tf_op jit(solution)/shard_map/ppermute | solution.py:417
  83.5 9.4 %collective-permute-start.20 = (f32[2,40,256]{2,1,0:T(8,128)S(1)}, f32[2,40,256]{2,1,0:T(8,128)S(1)}, u32[]{:S(2)}, u32[]{:S(2)}) collective-permute-start(f32[2,40,256]{2,1,0:T(8,128)S(1)} %get-tuple-element.48), channel_id=1, source_target_pairs={{0,28},{4,24},{8,20},{12,16},{16,12},{20,8},{24,4},{28,0},{1,29},{... | collective-permute-start | bytes 245768 | tf_op jit(solution)/shard_map/ppermute | solution.py:417
  (13 other events, 93.7 us)

commit v5 on v4

--- a/solution.py
+++ b/solution.py
@@ -33,7 +33,6 @@
     cells_in,
     weight_in,
     ens_ref,
-    out_ref,
     blocks_ref,
     *refs,
     tile_rows,
@@ -42,7 +41,9 @@
     gy_count,
 ):
     pieces = refs[:gx_count]
-    window, owner_ref, cells_ref, weight_ref, in_sems, out_sems, small_sems = refs[gx_count:]
+    window, payload_ref, owner_ref, cells_ref, weight_ref, in_sems, out_sems, small_sems = refs[
+        gx_count:
+    ]
     batches, nobs = cells_ref.shape
     held, _, cols = ens_ref.shape
     row_at = lax.axis_index("gx")
@@ -53,13 +54,9 @@
         rows = pl.ds(tile * tile_rows, tile_rows)
         return pltpu.make_async_copy(ens_ref.at[:, rows, :], window.at[tile], in_sems.at[tile])
 
-    def puts(slot):
-        upper = window.at[slot, :, pl.ds(0, first), :]
-        lower = window.at[row_at ^ slot, :, pl.ds(first, tile_rows - first), :]
-        return (
-            pltpu.make_async_copy(upper, blocks_ref.at[slot], out_sems.at[slot]),
-            pltpu.make_async_copy(lower, pieces[slot], out_sems.at[gx_count + slot]),
-        )
+    def put(tile):
+        other = window.at[tile, :, pl.ds(first, tile_rows - first), :]
+        return pltpu.make_async_copy(other, blocks_ref.at[tile], out_sems.at[tile])
 
     small = [
         pltpu.make_async_copy(source, target, small_sems.at[at])
@@ -71,12 +68,12 @@
         copy.start()
     for tile in range(gx_count):
         fetch(tile).start()
-    out_ref[...] = jnp.zeros_like(out_ref)
+    payload_ref[...] = jnp.zeros_like(payload_ref)
     for copy in small:
         copy.wait()
     for at, (b, later) in enumerate(pairs_of(batches)):
         row = held * batches + at
-        out_ref[row : row + 1, :] = jnp.where(owner_ref[later] == me, weight_ref[b : b + 1, :], 0.0)
+        payload_ref[row : row + 1, :] = jnp.where(owner_ref[later] == me, weight_ref[b : b + 1, :], 0.0)
     hits = []
     for b in range(batches):
         cell = cells_ref[b : b + 1, :]
@@ -86,9 +83,10 @@
         hits.append((jnp.concatenate([row_hit] * 3, axis=0), col_hit))
     for tile in range(gx_count):
         fetch(tile).wait()
+    for tile in range(gx_count):
+        put(tile).start()
     for slot in range(gx_count):
-        for copy in puts(slot):
-            copy.start()
+        pieces[slot][:, :first, :] = window[row_at ^ slot, :, :first, :]
     for b in range(batches):
         row_hit, col_hit = hits[b]
         owner_row = owner_ref[b] // gy_count
@@ -104,10 +102,14 @@
             )
             picked = jnp.sum(jnp.where(col_hit, columns, 0.0), axis=0, keepdims=True)
             row = m * batches + b
-            out_ref[row : row + 1, :] = jnp.where(mine, picked, 0.0)
+            payload_ref[row : row + 1, :] = jnp.where(mine, picked, 0.0)
+    deep = payload_ref.shape[0] // held
     for slot in range(gx_count):
-        for copy in puts(slot):
-            copy.wait()
+        pieces[slot][:, first:, :] = jnp.zeros((held, deep, cols), F32)
+        for m in range(held):
+            pieces[slot][m, first:, :nobs] = payload_ref[m * deep : (m + 1) * deep, :]
+    for tile in range(gx_count):
+        put(tile).wait()
 
 
 def observed_at(owner_ref, cells_ref, b, tile_rows, tile_cols, gy_count, inverse):
@@ -144,28 +146,25 @@
     values_ref,
     errors_ref,
     weight_ref,
-    got_ref,
-    other_ref,
-    a_ref,
-    w_ref,
-    prior_ref,
-    *,
+    *refs,
     tile_rows,
     tile_cols,
     held,
+    gx_count,
     gy_count,
-    offsets,
     inverse,
 ):
     batches, nobs = cells_ref.shape
-    members = held * len(offsets)
-    weights = jnp.zeros(got_ref.shape[1:], F32)
+    members = held * gx_count
+    parts, (a_ref, w_ref, prior_ref) = refs[:gy_count], refs[gy_count:]
+    weights = jnp.zeros(parts[0].shape[1:], F32)
     row_at = lax.axis_index("gx")
-    half = got_ref.shape[0]
-    for slot, offset in enumerate(offsets):
-        part = got_ref[slot] if slot < half else other_ref[slot - half]
+    for slot in range(gx_count):
+        part = parts[0][slot]
+        for other in parts[1:]:
+            part = part + other[slot]
         weights = weights + part
-        source = held * (row_at ^ offset)
+        source = held * (row_at ^ slot)
         for m in range(held):
             for b in range(batches):
                 row = m * batches + b
@@ -221,18 +220,19 @@
 
 
 def update_body(a_ref, w_ref, x_ref, y_ref, *refs, first, tile_rows, parts, inverse):
-    sources, targets = refs[:parts], refs[parts : 2 * parts]
-    held, rows, cols = sources[0].shape
-    members = held * parts
+    sources, targets, scratch = refs[: parts[0]], refs[parts[0] : sum(parts)], refs[-1]
+    members, rows, cols = scratch.shape
     batches, nobs, _ = x_ref.shape
     row_at = lax.axis_index("gx")
     top = row_at * tile_rows + first + pl.program_id(0) * rows
-    if parts == 1:
-        from_ref, to_ref = sources[0], targets[0]
-    else:
-        from_ref = to_ref = refs[-1]
+    from_ref, to_ref = sources[0], targets[0]
+    if len(sources) > 1:
+        from_ref = scratch
+        held = members // len(sources)
         for slot, source in enumerate(sources):
             from_ref[pl.ds(held * (row_at ^ slot), held)] = source[...]
+    if len(targets) > 1:
+        to_ref = scratch
     states = [from_ref[:, r, :] for r in range(rows)]
     for b in range(batches):
         scaled = a_ref[b][:, : 3 * members]
@@ -255,51 +255,37 @@
             states[r] = state + (change[:members] + change[members:])
     for r in range(rows):
         to_ref[:, r, :] = states[r]
-    if parts > 1:
+    if len(targets) > 1:
+        held = members // len(targets)
         for slot, target in enumerate(targets):
             target[...] = to_ref[pl.ds(held * (row_at ^ slot), held)]
 
 
-def share(picked, gx_count, gy_count):
-    def swap(array, axis, count, step):
-        return lax.ppermute(array, axis, [(i, i ^ step) for i in range(count)])
-
-    got = [picked[None]]
-    offsets = [0]
-    for step in range(2, gx_count, 2):
-        got.append(swap(picked[None], "gx", gx_count, step))
-        offsets.append(step)
-    got = jnp.concatenate(got, axis=0)
-    others = []
-    for step in range(1, gy_count):
-        others.append(swap(got, "gy", gy_count, step))
-    for other in others:
-        got = got + other
-    other = swap(got, "gx", gx_count, 1)
-    return (got, other), offsets + [offset ^ 1 for offset in offsets]
-
-
 def whole(array):
     return pl.BlockSpec(array.shape, lambda i: (0,) * array.ndim)
 
 
-def update(sources, tables, first, tile_rows, inverse):
-    parts = len(sources)
-    held, depth, cols = sources[0].shape
-    members = held * parts
+def update(sources, tables, first, depth, tile_rows, parts, inverse):
+    held, _, cols = sources[0].shape
+    members = held * len(sources)
     rows = ROWS
     batches, nobs = tables[0].shape[:2]
     cells = depth * cols * batches * nobs
-    blocks = [pl.BlockSpec((held, rows, cols), lambda i: (0, i, 0))] * parts
+    out = members // parts
     return pl.pallas_call(
         functools.partial(
-            update_body, first=first, tile_rows=tile_rows, parts=parts, inverse=inverse
+            update_body,
+            first=first,
+            tile_rows=tile_rows,
+            parts=(len(sources), parts),
+            inverse=inverse,
         ),
         grid=(depth // rows,),
-        in_specs=[whole(table) for table in tables] + blocks,
-        out_specs=blocks,
-        out_shape=[jax.ShapeDtypeStruct((held, depth, cols), F32)] * parts,
-        scratch_shapes=[pltpu.VMEM((members, rows, cols), F32)] if parts > 1 else [],
+        in_specs=[whole(table) for table in tables]
+        + [pl.BlockSpec((held, rows, cols), lambda i: (0, i, 0))] * len(sources),
+        out_specs=[pl.BlockSpec((out, rows, cols), lambda i: (0, i, 0))] * parts,
+        out_shape=[jax.ShapeDtypeStruct((out, depth, cols), F32)] * parts,
+        scratch_shapes=[pltpu.VMEM((members, rows, cols), F32)],
         cost_estimate=pl.CostEstimate(
             flops=cells * members * 10,
             bytes_accessed=8 * members * depth * cols,
@@ -343,7 +329,8 @@
     inverse = 1.0 / (all_rows // 4)
     weight = tile_weight[:, :, 0, 0]
     payload = held * batches + len(pairs_of(batches))
-    payload = -(-payload // 8) * 8
+    deep = -(-payload // (8 * held)) * 8
+    payload = held * deep
     in_smem = pl.BlockSpec(memory_space=SMEM)
     in_vmem = pl.BlockSpec(memory_space=VMEM)
     in_hbm = pl.BlockSpec(memory_space=pltpu.MemorySpace.HBM)
@@ -351,31 +338,29 @@
 
     first = tile_rows * FIRST_EIGHTHS // 8
     rest = tile_rows - first
-    picked, blocks, *pieces = pl.pallas_call(
+    blocks, *pieces = pl.pallas_call(
         functools.partial(
             pick_body, tile_rows=tile_rows, first=first, gx_count=gx_count, gy_count=gy_count
         ),
         in_specs=[in_hbm] * 4,
-        out_specs=[in_vmem] + [in_hbm] * (1 + gx_count),
-        out_shape=[
-            jax.ShapeDtypeStruct((payload, nobs), F32),
-            jax.ShapeDtypeStruct((gx_count, held, first, tile_cols), F32),
-        ]
-        + [jax.ShapeDtypeStruct((held, rest, tile_cols), F32)] * gx_count,
+        out_specs=[in_hbm] + [in_vmem] * gx_count,
+        out_shape=[jax.ShapeDtypeStruct((gx_count, held, rest, tile_cols), F32)]
+        + [jax.ShapeDtypeStruct((held, first + deep, tile_cols), F32)] * gx_count,
         scratch_shapes=[
             pltpu.VMEM((gx_count, held, tile_rows, tile_cols), F32),
+            pltpu.VMEM((payload, nobs), F32),
             pltpu.SMEM((batches,), jnp.int32),
             pltpu.VMEM((batches, nobs), jnp.int32),
             pltpu.VMEM((batches, nobs), F32),
             pltpu.SemaphoreType.DMA((gx_count,)),
-            pltpu.SemaphoreType.DMA((2 * gx_count,)),
+            pltpu.SemaphoreType.DMA((gx_count,)),
             pltpu.SemaphoreType.DMA((3,)),
         ],
         name="pick",
     )(owner_device, obs_cells, weight, ensemble)
-    state = lax.all_to_all(blocks, "gx", split_axis=0, concat_axis=0, tiled=True)
     for slot in range(1, gx_count):
         pieces[slot] = lax.ppermute(pieces[slot], "gx", [(i, i ^ slot) for i in range(gx_count)])
+    state = lax.all_to_all(blocks, "gx", split_axis=0, concat_axis=0, tiled=True)
     places = pl.pallas_call(
         functools.partial(tables_body, **geometry),
         in_specs=[in_smem, in_vmem],
@@ -387,11 +372,13 @@
         compiler_params=LIGHT,
         name="tables",
     )(owner_device, obs_cells)
-    got, offsets = share(picked, gx_count, gy_count)
+    got = [jnp.stack([piece[:, first:, :nobs].reshape(payload, nobs) for piece in pieces])]
+    for step in range(1, gy_count):
+        got.append(lax.ppermute(got[0], "gy", [(i, i ^ step) for i in range(gy_count)]))
     wide = -(-3 * members // nobs) * nobs
     chain = pl.pallas_call(
-        functools.partial(chain_body, held=held, offsets=offsets, **geometry),
-        in_specs=[in_smem] + [in_vmem] * 6,
+        functools.partial(chain_body, held=held, gx_count=gx_count, **geometry),
+        in_specs=[in_smem] + [in_vmem] * (4 + gy_count),
         out_specs=[in_vmem] * 2,
         out_shape=[
             jax.ShapeDtypeStruct((batches, nobs, wide), BF16),
@@ -404,7 +391,7 @@
     factors = chain(owner_device, obs_cells, obs_values, obs_error, weight, *got)
     tables = [*factors, *places]
 
-    (upper,) = update([state.reshape(members, first, tile_cols)], tables, 0, tile_rows, inverse)
+    (upper,) = update(pieces, tables, 0, first, tile_rows, 1, inverse)
     upper = lax.all_to_all(
         upper.reshape(gx_count, held, first, tile_cols),
         "gx",
@@ -412,7 +399,8 @@
         concat_axis=0,
         tiled=True,
     )
-    lower = [*update(pieces, tables, first, tile_rows, inverse)]
+    state = state.reshape(members, rest, tile_cols)
+    lower = [*update([state], tables, first, rest, tile_rows, gx_count, inverse)]
     for slot in range(1, gx_count):
         lower[slot] = lax.ppermute(
             lower[slot], "gx", [(i, i ^ slot) for i in range(gx_count)]

time: 95.1 us -> 85.3 us (0.90)
  waiting for transfers between devices: 27.7 us -> 22.4 us
  starting transfers between devices: 44.9 us -> 41 us
    ppermute x7 -> x3, waiting for transfers between devices: 12.3 us -> 3.17 us  [local(): lax.ppermute(got[0], 'gy', [(i, i ^ step) for i in range(gy_count)])]
    ppermute x7 -> x3, starting transfers between devices: 8.19 us -> 1.92 us  [local(): lax.ppermute(got[0], 'gy', [(i, i ^ step) for i in range(gy_count)])]
    ppermute x7, starting transfers between devices: 14.1 us -> 16.8 us  [local(): lax.ppermute(pieces[slot], 'gx', [(i, i ^ slot) for i in range(gx_count)])]
    ppermute x7, waiting for transfers between devices: 6.15 us -> 8.42 us  [local(): lax.ppermute(lower[slot], 'gx', [(i, i ^ slot) for i in range(gx_count)])]
    ppermute x7, waiting for transfers between devices: 9.18 us -> 10.8 us  [local(): lax.ppermute(pieces[slot], 'gx', [(i, i ^ slot) for i in range(gx_count)])]
  transfers between devices with their start and end apart: 23 -> 19, of which waited for: 9 -> 6; matrix products, arithmetic and copies ran while one was open for 0% -> 0% of each run, Pallas kernels for 12% -> 20%
where the time goes in v5:
time: 85.3 us; the launch traced here: 84.8 us
  starting transfers between devices  41 us (48%)
  waiting for transfers between devices  22.4 us (26%)
  Pallas kernels  21.1 us (25%)
    ppermute x7, starting transfers between devices, local(): lax.ppermute(pieces[slot], 'gx', [(i, i ^ slot) for i in range(gx_count)])  16.8 us
    pallas_call x2, Pallas kernels, update(): pl.pallas_call(functools.partial(update_body, first=first, tile_rows=tile...  13.5 us
    ppermute x7, starting transfers between devices, local(): lax.ppermute(lower[slot], 'gx', [(i, i ^ slot) for i in range(gx_count)])  11.3 us
    ppermute x7, waiting for transfers between devices, local(): lax.ppermute(pieces[slot], 'gx', [(i, i ^ slot) for i in range(gx_count)])  10.8 us
    ppermute x7, waiting for transfers between devices, local(): lax.ppermute(lower[slot], 'gx', [(i, i ^ slot) for i in range(gx_count)])  8.42 us
    all_to_all x1, starting transfers between devices, local(): lax.all_to_all(blocks, 'gx', split_axis=0, concat_axis=0, tiled=True)  7.43 us
    all_to_all x1, starting transfers between devices, local(): lax.all_to_all(upper.reshape(gx_count, held, first, tile_cols), 'gx', spl...  3.57 us
    pallas_call x1, Pallas kernels, local(): pl.pallas_call(functools.partial(pick_body, tile_rows=tile_rows, first=fi...  3.45 us
  transfers between devices with their start and end apart: 19, of which 6 were waited for; matrix products, arithmetic and copies ran while one was open for 0% of the time, Pallas kernels for 20%

profile of v5, /device:TPU:0, one launch (start us, length us, event | category | flops | bytes accessed | tf_op | source)
XLA Modules:
  0.0 84.8 jit_solution(9896937443194505056)
XLA Ops:
  0.0 3.4 %pick.1 = (f32[8,2,40,256]{3,2,1,0:T(8,128)}, f32[2,32,256]{2,1,0:T(8,128)}, f32[2,32,256]{2,1,0:T(8,128)}, f32[2,32,256]{2,1,0:T(8,128)}, f32[2,32,256]{2,1,0:T...) custom-call(s32[4]{0:T(128)} %owner_ref.3, ...), custom_call_target="tpu_custom_call" | custom-call | tf_op jit(solution)/shard_map/pick/pallas_call | solution.py:341
  3.5 7.4 %all-to-all-start.1 = ((f32[8,2,40,256]{3,2,1,0:T(8,128)}), f32[8,2,40,256]{3,2,1,0:T(8,128)S(1)}, u32[]{:S(2)}, u32[]{:S(2)}) async-start(f32[8,2,40,256]{3,2,1,0:T(8,128)} %get-tuple-element.38), calls=%async_computation.1 | async-start | bytes 1310720 | tf_op jit(solution)/shard_map/all_to_all | solution.py:363
  11.0 2.0 %collective-permute-start = (f32[2,32,256]{2,1,0:T(8,128)S(1)}, f32[2,32,256]{2,1,0:T(8,128)S(1)}, u32[]{:S(2)}, u32[]{:S(2)}) collective-permute-start(f32[2,32,256]{2,1,0:T(8,128)S(1)} %copy-done.12), channel_id=1, source_target_pairs={{0,4},{4,0},{8,12},{12,8},{16,20},{20,16},{24,28},{28,24},{1,5},{5... | collective-permute-start | bytes 196616 | tf_op jit(solution)/shard_map/ppermute | solution.py:362
  13.0 1.5 %collective-permute-start.1 = (f32[2,32,256]{2,1,0:T(8,128)S(1)}, f32[2,32,256]{2,1,0:T(8,128)S(1)}, u32[]{:S(2)}, u32[]{:S(2)}) collective-permute-start(f32[2,32,256]{2,1,0:T(8,128)S(1)} %copy-done.11), channel_id=1, source_target_pairs={{0,8},{4,12},{8,0},{12,4},{16,24},{20,28},{24,16},{28,20},{1,9},{5... | collective-permute-start | bytes 196616 | tf_op jit(solution)/shard_map/ppermute | solution.py:362
  14.5 2.8 %collective-permute-start.3 = (f32[2,32,256]{2,1,0:T(8,128)S(1)}, f32[2,32,256]{2,1,0:T(8,128)S(1)}, u32[]{:S(2)}, u32[]{:S(2)}) collective-permute-start(f32[2,32,256]{2,1,0:T(8,128)S(1)} %copy-done.9), channel_id=1, source_target_pairs={{0,16},{4,20},{8,24},{12,28},{16,0},{20,4},{24,8},{28,12},{1,17},{... | collective-permute-start | bytes 196616 | tf_op jit(solution)/shard_map/ppermute | solution.py:362
  17.4 1.5 %collective-permute-start.4 = (f32[2,32,256]{2,1,0:T(8,128)S(1)}, f32[2,32,256]{2,1,0:T(8,128)S(1)}, u32[]{:S(2)}, u32[]{:S(2)}) collective-permute-start(f32[2,32,256]{2,1,0:T(8,128)S(1)} %copy-done.8), channel_id=1, source_target_pairs={{0,20},{4,16},{8,28},{12,24},{16,4},{20,0},{24,12},{28,8},{1,21},{... | collective-permute-start | bytes 196616 | tf_op jit(solution)/shard_map/ppermute | solution.py:362
  18.9 4.1 %collective-permute-start.5 = (f32[2,32,256]{2,1,0:T(8,128)S(1)}, f32[2,32,256]{2,1,0:T(8,128)S(1)}, u32[]{:S(2)}, u32[]{:S(2)}) collective-permute-start(f32[2,32,256]{2,1,0:T(8,128)S(1)} %copy-done.7), channel_id=1, source_target_pairs={{0,24},{4,28},{8,16},{12,20},{16,8},{20,12},{24,0},{28,4},{1,25},{... | collective-permute-start | bytes 196616 | tf_op jit(solution)/shard_map/ppermute | solution.py:362
  23.0 1.2 %collective-permute-done.1.refs_2_ = f32[2,32,256]{2,1,0:T(8,128)S(1)} collective-permute-done((f32[2,32,256]{2,1,0:T(8,128)S(1)}, f32[2,32,256]{2,1,0:T(8,128)S(1)}, u32[]{:S(2)}, u32[]{:S(2)}) %collective-permute-start.1) | collective-permute-done | bytes 65568 | tf_op jit(solution)/shard_map/ppermute | solution.py:362
  24.2 4.8 %collective-permute-start.6 = (f32[2,32,256]{2,1,0:T(8,128)S(1)}, f32[2,32,256]{2,1,0:T(8,128)S(1)}, u32[]{:S(2)}, u32[]{:S(2)}) collective-permute-start(f32[2,32,256]{2,1,0:T(8,128)S(1)} %copy-done.6), channel_id=1, source_target_pairs={{0,28},{4,24},{8,20},{12,16},{16,12},{20,8},{24,4},{28,0},{1,29},{... | collective-permute-start | bytes 196616 | tf_op jit(solution)/shard_map/ppermute | solution.py:362
  29.0 7.7 %collective-permute-done.3.refs_4_ = f32[2,32,256]{2,1,0:T(8,128)S(1)} collective-permute-done((f32[2,32,256]{2,1,0:T(8,128)S(1)}, f32[2,32,256]{2,1,0:T(8,128)S(1)}, u32[]{:S(2)}, u32[]{:S(2)}) %collective-permute-start.3) | collective-permute-done | bytes 65568 | tf_op jit(solution)/shard_map/ppermute | solution.py:362
  36.7 1.9 %collective-permute-done.4.refs_5_ = f32[2,32,256]{2,1,0:T(8,128)S(1)} collective-permute-done((f32[2,32,256]{2,1,0:T(8,128)S(1)}, f32[2,32,256]{2,1,0:T(8,128)S(1)}, u32[]{:S(2)}, u32[]{:S(2)}) %collective-permute-start.4) | collective-permute-done | bytes 65568 | tf_op jit(solution)/shard_map/ppermute | solution.py:362
  38.8 1.6 %collective-permute-start.8 = (f32[8,16,128]{2,1,0:T(8,128)S(1)}, f32[8,16,128]{2,1,0:T(8,128)S(1)}, u32[]{:S(2)}, u32[]{:S(2)}) collective-permute-start(f32[8,16,128]{2,1,0:T(8,128)S(1)} %constant_dynamic-update-slice_fusion.refs_0_), channel_id=1, source_target_pairs={{0,2},{1,3},{2,0},{3,1},{4,6},{5,7},{6,4},{7,5},{8,10},{9,11},{10,... | collective-permute-start | bytes 196616 | tf_op jit(solution)/shard_map/ppermute | solution.py:377
  41.4 1.7 %collective-permute-done.9.refs_3_ = f32[8,16,128]{2,1,0:T(8,128)S(1)} collective-permute-done((f32[8,16,128]{2,1,0:T(8,128)S(1)}, f32[8,16,128]{2,1,0:T(8,128)S(1)}, u32[]{:S(2)}, u32[]{:S(2)}) %collective-permute-start.9) | collective-permute-done | bytes 65568 | tf_op jit(solution)/shard_map/ppermute | solution.py:377
  43.1 1.5 %collective-permute-done.8.refs_2_ = f32[8,16,128]{2,1,0:T(8,128)S(1)} collective-permute-done((f32[8,16,128]{2,1,0:T(8,128)S(1)}, f32[8,16,128]{2,1,0:T(8,128)S(1)}, u32[]{:S(2)}, u32[]{:S(2)}) %collective-permute-start.8) | collective-permute-done | bytes 65568 | tf_op jit(solution)/shard_map/ppermute | solution.py:377
  44.6 2.3 %chain.1 = (bf16[4,128,128]{2,1,0:T(8,128)(2,1)S(1)}, bf16[4,32,256]{2,1,0:T(8,128)(2,1)S(1)}) custom-call(s32[4]{0:T(128)S(1)} %copy-done.2, s32[4,128]{1,0:T(4,128)S(1)} %copy-done, f32[4,128]{1,0:T(4,128)S(1)} %copy-done.3, f32[4,128]{1,0:T(4,128)S(1)} %copy-done.4, f32[4,128]{1,0:T(4,128)S(1)} %bitcast.35, ...), custom_call_target="tpu_custom_call" | custom-call | tf_op jit(solution)/shard_map/chain/pallas_call | solution.py:391
  46.9 5.5 %update.2 = f32[16,24,256]{2,1,0:T(8,128)} custom-call(bf16[4,128,128]{2,1,0:T(8,128)(2,1)S(1)} %get-tuple-element.34.a_ref, bf16[4,32,256]{2,1,0:T(8,128)(2,1)S(1)} %get-tuple-element.35.w_ref, f32[4,128,128]{2,1,0:T(8,128)S(1)} %get-tuple-element.36.x_ref, f32[4,128,256]{2,1,0:T(8,128)S(1)} %get-tuple-element.37.y_ref, f32[2,32,256]{2,1,0:T(8,128)S(1)} %copy-done.5, ...), custom_call_target="tpu_custom_call" | custom-call | flops 503316480 | bytes 786432 | tf_op jit(solution)/shard_map/update/pallas_call | solution.py:275
  52.4 3.6 %all-to-all-start = ((f32[8,2,24,256]{3,2,1,0:T(8,128)}), f32[8,2,24,256]{3,2,1,0:T(8,128)S(1)}, u32[]{:S(2)}, u32[]{:S(2)}) async-start(f32[8,2,24,256]{3,2,1,0:T(8,128)} %bitcast.9), calls=%async_computation | async-start | bytes 786432 | tf_op jit(solution)/shard_map/all_to_all | solution.py:395
  56.0 8.0 %update.3 = (f32[2,40,256]{2,1,0:T(8,128)S(1)}, f32[2,40,256]{2,1,0:T(8,128)S(1)}, f32[2,40,256]{2,1,0:T(8,128)S(1)}, f32[2,40,256]{2,1,0:T(8,128)S(1)}, f32[2,4...) custom-call(bf16[4,128,128]{2,1,0:T(8,128)(2,1)S(1)} %get-tuple-element.3, ...), custom_call_target="tpu_custom_call" | custom-call | flops 838860800 | bytes 1310720 | tf_op jit(solution)/shard_map/update/pallas_call | solution.py:275
  63.9 2.1 %collective-permute-start.10 = (f32[2,40,256]{2,1,0:T(8,128)S(1)}, f32[2,40,256]{2,1,0:T(8,128)S(1)}, u32[]{:S(2)}, u32[]{:S(2)}) collective-permute-start(f32[2,40,256]{2,1,0:T(8,128)S(1)} %get-tuple-element.40), channel_id=1, source_target_pairs={{0,4},{4,0},{8,12},{12,8},{16,20},{20,16},{24,28},{28,24},{1,5},{5... | collective-permute-start | bytes 245768 | tf_op jit(solution)/shard_map/ppermute | solution.py:405
  66.0 1.5 %collective-permute-start.11 = (f32[2,40,256]{2,1,0:T(8,128)S(1)}, f32[2,40,256]{2,1,0:T(8,128)S(1)}, u32[]{:S(2)}, u32[]{:S(2)}) collective-permute-start(f32[2,40,256]{2,1,0:T(8,128)S(1)} %get-tuple-element.41), channel_id=1, source_target_pairs={{0,8},{4,12},{8,0},{12,4},{16,24},{20,28},{24,16},{28,20},{1,9},{5... | collective-permute-start | bytes 245768 | tf_op jit(solution)/shard_map/ppermute | solution.py:405
  67.6 2.8 %collective-permute-start.13 = (f32[2,40,256]{2,1,0:T(8,128)S(1)}, f32[2,40,256]{2,1,0:T(8,128)S(1)}, u32[]{:S(2)}, u32[]{:S(2)}) collective-permute-start(f32[2,40,256]{2,1,0:T(8,128)S(1)} %get-tuple-element.43), channel_id=1, source_target_pairs={{0,16},{4,20},{8,24},{12,28},{16,0},{20,4},{24,8},{28,12},{1,17},{... | collective-permute-start | bytes 245768 | tf_op jit(solution)/shard_map/ppermute | solution.py:405
  70.4 1.5 %collective-permute-start.14 = (f32[2,40,256]{2,1,0:T(8,128)S(1)}, f32[2,40,256]{2,1,0:T(8,128)S(1)}, u32[]{:S(2)}, u32[]{:S(2)}) collective-permute-start(f32[2,40,256]{2,1,0:T(8,128)S(1)} %get-tuple-element.44), channel_id=1, source_target_pairs={{0,20},{4,16},{8,28},{12,24},{16,4},{20,0},{24,12},{28,8},{1,21},{... | collective-permute-start | bytes 245768 | tf_op jit(solution)/shard_map/ppermute | solution.py:405
  71.9 3.3 %collective-permute-start.15 = (f32[2,40,256]{2,1,0:T(8,128)S(1)}, f32[2,40,256]{2,1,0:T(8,128)S(1)}, u32[]{:S(2)}, u32[]{:S(2)}) collective-permute-start(f32[2,40,256]{2,1,0:T(8,128)S(1)} %get-tuple-element.45), channel_id=1, source_target_pairs={{0,24},{4,28},{8,16},{12,20},{16,8},{20,12},{24,0},{28,4},{1,25},{... | collective-permute-start | bytes 245768 | tf_op jit(solution)/shard_map/ppermute | solution.py:405
  75.3 8.4 %collective-permute-done.14.refs_5_ = f32[2,40,256]{2,1,0:T(8,128)S(1)} collective-permute-done((f32[2,40,256]{2,1,0:T(8,128)S(1)}, f32[2,40,256]{2,1,0:T(8,128)S(1)}, u32[]{:S(2)}, u32[]{:S(2)}) %collective-permute-start.14) | collective-permute-done | bytes 81952 | tf_op jit(solution)/shard_map/ppermute | solution.py:405
  (54 shorter events, 2.6 us)
Async XLA Ops:
  3.5 11.1 %copy-start.9 = (f32[2,32,256]{2,1,0:T(8,128)S(1)}, f32[2,32,256]{2,1,0:T(8,128)}, u32[]{:S(2)}) copy-start(f32[2,32,256]{2,1,0:T(8,128)} %get-tuple-element.30) | copy-start | bytes 196612
  3.5 13.9 %copy-start.8 = (f32[2,32,256]{2,1,0:T(8,128)S(1)}, f32[2,32,256]{2,1,0:T(8,128)}, u32[]{:S(2)}) copy-start(f32[2,32,256]{2,1,0:T(8,128)} %get-tuple-element.31) | copy-start | bytes 196612
  3.5 15.3 %copy-start.5 = (f32[2,32,256]{2,1,0:T(8,128)S(1)}, f32[2,32,256]{2,1,0:T(8,128)}, u32[]{:S(2)}) copy-start(f32[2,32,256]{2,1,0:T(8,128)} %get-tuple-element.26.refs_0_) | copy-start | bytes 196612
  3.5 15.3 %copy-start.7 = (f32[2,32,256]{2,1,0:T(8,128)S(1)}, f32[2,32,256]{2,1,0:T(8,128)}, u32[]{:S(2)}) copy-start(f32[2,32,256]{2,1,0:T(8,128)} %get-tuple-element.32) | copy-start | bytes 196612
  3.5 20.7 %copy-start.6 = (f32[2,32,256]{2,1,0:T(8,128)S(1)}, f32[2,32,256]{2,1,0:T(8,128)}, u32[]{:S(2)}) copy-start(f32[2,32,256]{2,1,0:T(8,128)} %get-tuple-element.33) | copy-start | bytes 196612
  3.5 48.9 %all-to-all-start.1 = ((f32[8,2,40,256]{3,2,1,0:T(8,128)}), f32[8,2,40,256]{3,2,1,0:T(8,128)S(1)}, u32[]{:S(2)}, u32[]{:S(2)}) async-start(f32[8,2,40,256]{3,2,1,0:T(8,128)} %get-tuple-element.38), calls=%async_computation.1 | async-start | bytes 1310720 | tf_op jit(solution)/shard_map/all_to_all | solution.py:363
  11.0 7.9 %collective-permute-start = (f32[2,32,256]{2,1,0:T(8,128)S(1)}, f32[2,32,256]{2,1,0:T(8,128)S(1)}, u32[]{:S(2)}, u32[]{:S(2)}) collective-permute-start(f32[2,32,256]{2,1,0:T(8,128)S(1)} %copy-done.12), channel_id=1, source_target_pairs={{0,4},{4,0},{8,12},{12,8},{16,20},{20,16},{24,28},{28,24},{1,5},{5... | collective-permute-start | bytes 196616 | tf_op jit(solution)/shard_map/ppermute | solution.py:362
  13.0 11.2 %collective-permute-start.1 = (f32[2,32,256]{2,1,0:T(8,128)S(1)}, f32[2,32,256]{2,1,0:T(8,128)S(1)}, u32[]{:S(2)}, u32[]{:S(2)}) collective-permute-start(f32[2,32,256]{2,1,0:T(8,128)S(1)} %copy-done.11), channel_id=1, source_target_pairs={{0,8},{4,12},{8,0},{12,4},{16,24},{20,28},{24,16},{28,20},{1,9},{5... | collective-permute-start | bytes 196616 | tf_op jit(solution)/shard_map/ppermute | solution.py:362
  14.5 14.5 %collective-permute-start.2 = (f32[2,32,256]{2,1,0:T(8,128)S(1)}, f32[2,32,256]{2,1,0:T(8,128)S(1)}, u32[]{:S(2)}, u32[]{:S(2)}) collective-permute-start(f32[2,32,256]{2,1,0:T(8,128)S(1)} %copy-done.10), channel_id=1, source_target_pairs={{0,12},{4,8},{8,4},{12,0},{16,28},{20,24},{24,20},{28,16},{1,13},{... | collective-permute-start | bytes 196616 | tf_op jit(solution)/shard_map/ppermute | solution.py:362
  14.5 22.2 %collective-permute-start.3 = (f32[2,32,256]{2,1,0:T(8,128)S(1)}, f32[2,32,256]{2,1,0:T(8,128)S(1)}, u32[]{:S(2)}, u32[]{:S(2)}) collective-permute-start(f32[2,32,256]{2,1,0:T(8,128)S(1)} %copy-done.9), channel_id=1, source_target_pairs={{0,16},{4,20},{8,24},{12,28},{16,0},{20,4},{24,8},{28,12},{1,17},{... | collective-permute-start | bytes 196616 | tf_op jit(solution)/shard_map/ppermute | solution.py:362
  17.4 21.2 %collective-permute-start.4 = (f32[2,32,256]{2,1,0:T(8,128)S(1)}, f32[2,32,256]{2,1,0:T(8,128)S(1)}, u32[]{:S(2)}, u32[]{:S(2)}) collective-permute-start(f32[2,32,256]{2,1,0:T(8,128)S(1)} %copy-done.8), channel_id=1, source_target_pairs={{0,20},{4,16},{8,28},{12,24},{16,4},{20,0},{24,12},{28,8},{1,21},{... | collective-permute-start | bytes 196616 | tf_op jit(solution)/shard_map/ppermute | solution.py:362
  18.9 19.7 %collective-permute-start.5 = (f32[2,32,256]{2,1,0:T(8,128)S(1)}, f32[2,32,256]{2,1,0:T(8,128)S(1)}, u32[]{:S(2)}, u32[]{:S(2)}) collective-permute-start(f32[2,32,256]{2,1,0:T(8,128)S(1)} %copy-done.7), channel_id=1, source_target_pairs={{0,24},{4,28},{8,16},{12,20},{16,8},{20,12},{24,0},{28,4},{1,25},{... | collective-permute-start | bytes 196616 | tf_op jit(solution)/shard_map/ppermute | solution.py:362
  24.2 14.4 %collective-permute-start.6 = (f32[2,32,256]{2,1,0:T(8,128)S(1)}, f32[2,32,256]{2,1,0:T(8,128)S(1)}, u32[]{:S(2)}, u32[]{:S(2)}) collective-permute-start(f32[2,32,256]{2,1,0:T(8,128)S(1)} %copy-done.6), channel_id=1, source_target_pairs={{0,28},{4,24},{8,20},{12,16},{16,12},{20,8},{24,4},{28,0},{1,29},{... | collective-permute-start | bytes 196616 | tf_op jit(solution)/shard_map/ppermute | solution.py:362
  38.7 4.4 %collective-permute-start.9 = (f32[8,16,128]{2,1,0:T(8,128)S(1)}, f32[8,16,128]{2,1,0:T(8,128)S(1)}, u32[]{:S(2)}, u32[]{:S(2)}) collective-permute-start(f32[8,16,128]{2,1,0:T(8,128)S(1)} %constant_dynamic-update-slice_fusion.refs_0_), channel_id=1, source_target_pairs={{0,3},{1,2},{2,1},{3,0},{4,7},{5,6},{6,5},{7,4},{8,11},{9,10},{10,... | collective-permute-start | bytes 196616 | tf_op jit(solution)/shard_map/ppermute | solution.py:377
  38.8 5.8 %collective-permute-start.8 = (f32[8,16,128]{2,1,0:T(8,128)S(1)}, f32[8,16,128]{2,1,0:T(8,128)S(1)}, u32[]{:S(2)}, u32[]{:S(2)}) collective-permute-start(f32[8,16,128]{2,1,0:T(8,128)S(1)} %constant_dynamic-update-slice_fusion.refs_0_), channel_id=1, source_target_pairs={{0,2},{1,3},{2,0},{3,1},{4,6},{5,7},{6,4},{7,5},{8,10},{9,11},{10,... | collective-permute-start | bytes 196616 | tf_op jit(solution)/shard_map/ppermute | solution.py:377
  40.3 4.2 %collective-permute-start.7 = (f32[8,16,128]{2,1,0:T(8,128)S(1)}, f32[8,16,128]{2,1,0:T(8,128)S(1)}, u32[]{:S(2)}, u32[]{:S(2)}) collective-permute-start(f32[8,16,128]{2,1,0:T(8,128)S(1)} %constant_dynamic-update-slice_fusion.refs_0_), channel_id=1, source_target_pairs={{0,1},{1,0},{2,3},{3,2},{4,5},{5,4},{6,7},{7,6},{8,9},{9,8},{10,11... | collective-permute-start | bytes 196616 | tf_op jit(solution)/shard_map/ppermute | solution.py:377
  52.4 22.9 %all-to-all-start = ((f32[8,2,24,256]{3,2,1,0:T(8,128)}), f32[8,2,24,256]{3,2,1,0:T(8,128)S(1)}, u32[]{:S(2)}, u32[]{:S(2)}) async-start(f32[8,2,24,256]{3,2,1,0:T(8,128)} %bitcast.9), calls=%async_computation | async-start | bytes 786432 | tf_op jit(solution)/shard_map/all_to_all | solution.py:395
  63.9 7.9 %collective-permute-start.10 = (f32[2,40,256]{2,1,0:T(8,128)S(1)}, f32[2,40,256]{2,1,0:T(8,128)S(1)}, u32[]{:S(2)}, u32[]{:S(2)}) collective-permute-start(f32[2,40,256]{2,1,0:T(8,128)S(1)} %get-tuple-element.40), channel_id=1, source_target_pairs={{0,4},{4,0},{8,12},{12,8},{16,20},{20,16},{24,28},{28,24},{1,5},{5... | collective-permute-start | bytes 245768 | tf_op jit(solution)/shard_map/ppermute | solution.py:405
  66.0 9.1 %collective-permute-start.11 = (f32[2,40,256]{2,1,0:T(8,128)S(1)}, f32[2,40,256]{2,1,0:T(8,128)S(1)}, u32[]{:S(2)}, u32[]{:S(2)}) collective-permute-start(f32[2,40,256]{2,1,0:T(8,128)S(1)} %get-tuple-element.41), channel_id=1, source_target_pairs={{0,8},{4,12},{8,0},{12,4},{16,24},{20,28},{24,16},{28,20},{1,9},{5... | collective-permute-start | bytes 245768 | tf_op jit(solution)/shard_map/ppermute | solution.py:405
  67.5 7.8 %collective-permute-start.12 = (f32[2,40,256]{2,1,0:T(8,128)S(1)}, f32[2,40,256]{2,1,0:T(8,128)S(1)}, u32[]{:S(2)}, u32[]{:S(2)}) collective-permute-start(f32[2,40,256]{2,1,0:T(8,128)S(1)} %get-tuple-element.42), channel_id=1, source_target_pairs={{0,12},{4,8},{8,4},{12,0},{16,28},{20,24},{24,20},{28,16},{1,13},{... | collective-permute-start | bytes 245768 | tf_op jit(solution)/shard_map/ppermute | solution.py:405
  67.6 7.7 %collective-permute-start.13 = (f32[2,40,256]{2,1,0:T(8,128)S(1)}, f32[2,40,256]{2,1,0:T(8,128)S(1)}, u32[]{:S(2)}, u32[]{:S(2)}) collective-permute-start(f32[2,40,256]{2,1,0:T(8,128)S(1)} %get-tuple-element.43), channel_id=1, source_target_pairs={{0,16},{4,20},{8,24},{12,28},{16,0},{20,4},{24,8},{28,12},{1,17},{... | collective-permute-start | bytes 245768 | tf_op jit(solution)/shard_map/ppermute | solution.py:405
  70.4 13.3 %collective-permute-start.14 = (f32[2,40,256]{2,1,0:T(8,128)S(1)}, f32[2,40,256]{2,1,0:T(8,128)S(1)}, u32[]{:S(2)}, u32[]{:S(2)}) collective-permute-start(f32[2,40,256]{2,1,0:T(8,128)S(1)} %get-tuple-element.44), channel_id=1, source_target_pairs={{0,20},{4,16},{8,28},{12,24},{16,4},{20,0},{24,12},{28,8},{1,21},{... | collective-permute-start | bytes 245768 | tf_op jit(solution)/shard_map/ppermute | solution.py:405
  71.9 11.8 %collective-permute-start.15 = (f32[2,40,256]{2,1,0:T(8,128)S(1)}, f32[2,40,256]{2,1,0:T(8,128)S(1)}, u32[]{:S(2)}, u32[]{:S(2)}) collective-permute-start(f32[2,40,256]{2,1,0:T(8,128)S(1)} %get-tuple-element.45), channel_id=1, source_target_pairs={{0,24},{4,28},{8,16},{12,20},{16,8},{20,12},{24,0},{28,4},{1,25},{... | collective-permute-start | bytes 245768 | tf_op jit(solution)/shard_map/ppermute | solution.py:405
  75.2 8.5 %collective-permute-start.16 = (f32[2,40,256]{2,1,0:T(8,128)S(1)}, f32[2,40,256]{2,1,0:T(8,128)S(1)}, u32[]{:S(2)}, u32[]{:S(2)}) collective-permute-start(f32[2,40,256]{2,1,0:T(8,128)S(1)} %get-tuple-element.46), channel_id=1, source_target_pairs={{0,28},{4,24},{8,20},{12,16},{16,12},{20,8},{24,4},{28,0},{1,29},{... | collective-permute-start | bytes 245768 | tf_op jit(solution)/shard_map/ppermute | solution.py:405
  (8 other events, 49.7 us)

commit v6 on v5

--- a/solution.py
+++ b/solution.py
@@ -85,8 +85,13 @@
         fetch(tile).wait()
     for tile in range(gx_count):
         put(tile).start()
+    folds = cols // nobs
     for slot in range(gx_count):
-        pieces[slot][:, :first, :] = window[row_at ^ slot, :, :first, :]
+        for m in range(held):
+            for fold in range(folds):
+                at = (m * folds + fold) * first
+                lanes = slice(fold * nobs, (fold + 1) * nobs)
+                pieces[slot][at : at + first, :] = window[row_at ^ slot, m, :first, lanes]
     for b in range(batches):
         row_hit, col_hit = hits[b]
         owner_row = owner_ref[b] // gy_count
@@ -103,11 +108,8 @@
             picked = jnp.sum(jnp.where(col_hit, columns, 0.0), axis=0, keepdims=True)
             row = m * batches + b
             payload_ref[row : row + 1, :] = jnp.where(mine, picked, 0.0)
-    deep = payload_ref.shape[0] // held
     for slot in range(gx_count):
-        pieces[slot][:, first:, :] = jnp.zeros((held, deep, cols), F32)
-        for m in range(held):
-            pieces[slot][m, first:, :nobs] = payload_ref[m * deep : (m + 1) * deep, :]
+        pieces[slot][held * folds * first :, :] = payload_ref[...]
     for tile in range(gx_count):
         put(tile).wait()
 
@@ -124,37 +126,38 @@
 
 
 def tables_body(
-    owner_ref, cells_ref, x_ref, y_ref, *, tile_rows, tile_cols, gy_count, inverse
+    owner_ref, cells_ref, x_ref, y_ref, taper_ref, *, tile_rows, tile_cols, gy_count, inverse
 ):
     batches, nobs = cells_ref.shape
     left = lax.axis_index("gy") * tile_cols
-    for b in range(batches):
-        _, _, down_x, down_y = observed_at(
-            owner_ref, cells_ref, b, tile_rows, tile_cols, gy_count, inverse
-        )
+    places = [
+        observed_at(owner_ref, cells_ref, b, tile_rows, tile_cols, gy_count, inverse)
+        for b in range(batches)
+    ]
+    for b, (_, _, down_x, down_y) in enumerate(places):
         x_ref[b] = down_x
         for piece in range(tile_cols // nobs):
             lanes = slice(piece * nobs, (piece + 1) * nobs)
             grid = lax.broadcasted_iota(jnp.int32, (nobs, nobs), 1) + (left + piece * nobs)
             away = down_y - grid.astype(F32) * inverse
             y_ref[b, :, lanes] = away * away
+    for at, (b, later) in enumerate(pairs_of(batches)):
+        dx = places[b][2] - places[later][0]
+        dy = places[b][3] - places[later][1]
+        taper_ref[at] = pl.reciprocal(1.0 + (dx * dx + dy * dy))
+
+
+def factor_rows(increment):
+    high, low = split_two(increment)
+    return jnp.concatenate(
+        [jnp.concatenate([high, high], axis=1), jnp.concatenate([low, low], axis=1)], axis=0
+    )
 
 
 def chain_body(
-    owner_ref,
-    cells_ref,
-    values_ref,
-    errors_ref,
-    weight_ref,
-    *refs,
-    tile_rows,
-    tile_cols,
-    held,
-    gx_count,
-    gy_count,
-    inverse,
+    values_ref, errors_ref, weight_ref, taper_ref, *refs, held, gx_count, gy_count
 ):
-    batches, nobs = cells_ref.shape
+    batches, nobs = values_ref.shape
     members = held * gx_count
     parts, (a_ref, w_ref, prior_ref) = refs[:gy_count], refs[gy_count:]
     weights = jnp.zeros(parts[0].shape[1:], F32)
@@ -169,41 +172,12 @@
             for b in range(batches):
                 row = m * batches + b
                 prior_ref[b, pl.ds(source + m, 1), :] = part[row : row + 1, :]
-    pair_weight = {
-        pair: weights[held * batches + at : held * batches + at + 1, :]
-        for at, pair in enumerate(pairs_of(batches))
-    }
-    places = [
-        observed_at(owner_ref, cells_ref, b, tile_rows, tile_cols, gy_count, inverse)
-        for b in range(batches)
-    ]
     for b in range(batches):
         prior = prior_ref[b]
         average = jnp.mean(prior, axis=0, keepdims=True)
         anomaly = prior - average
         spread = jnp.sum(anomaly * anomaly, axis=0, keepdims=True) / (members - 1) + EPSILON
-        noise = errors_ref[b : b + 1, :]
-        post_var = 1.0 / (1.0 / spread + 1.0 / noise)
-        post_mean = post_var * (average / spread + values_ref[b : b + 1, :] / noise)
-        increment = post_mean - average + (jnp.sqrt(post_var / spread) - 1.0) * anomaly
-        for later in range(b + 1, batches):
-            there = prior_ref[later]
-            deviation = there - jnp.mean(there, axis=0, keepdims=True)
-            scaled = anomaly * (pair_weight[b, later] / spread / (members - 1))
-            covariance = lax.dot_general(
-                scaled,
-                deviation,
-                (((0,), (0,)), ((), ())),
-                precision=lax.Precision.HIGHEST,
-                preferred_element_type=F32,
-            )
-            dx = places[b][2] - places[later][0]
-            dy = places[b][3] - places[later][1]
-            gain = covariance / (1.0 + (dx * dx + dy * dy))
-            prior_ref[later] = there + jnp.dot(
-                increment, gain, precision=lax.Precision.HIGHEST, preferred_element_type=F32
-            )
-        scaled = anomaly * (weight_ref[b : b + 1, :] / spread / (members - 1))
+        scaled = anomaly / (spread * (members - 1))
         high, low = split_two(scaled)
         stacked = jnp.concatenate([high, high, low], axis=0).astype(F32)
         wide = a_ref.shape[2]
@@ -211,15 +185,37 @@
             stacked = jnp.concatenate(
                 [stacked, jnp.zeros((wide - stacked.shape[0], nobs), F32)], axis=0
             )
-        a_ref[b] = jnp.transpose(stacked).astype(BF16)
-        high, low = split_two(increment)
-        w_ref[b, :members, :nobs] = high
-        w_ref[b, :members, nobs:] = high
-        w_ref[b, members:, :nobs] = low
-        w_ref[b, members:, nobs:] = low
-
-
-def update_body(a_ref, w_ref, x_ref, y_ref, *refs, first, tile_rows, parts, inverse):
+        upright = jnp.transpose(stacked).astype(BF16)
+        a_ref[b] = upright
+        noise = errors_ref[b : b + 1, :]
+        post_var = 1.0 / (1.0 / spread + 1.0 / noise)
+        post_mean = post_var * (average / spread + values_ref[b : b + 1, :] / noise)
+        increment = post_mean - average + (jnp.sqrt(post_var / spread) - 1.0) * anomaly
+        w_ref[b] = factor_rows(increment * weight_ref[b : b + 1, :])
+        for at, (earlier, later) in enumerate(pairs_of(batches)):
+            if earlier != b:
+                continue
+            there = prior_ref[later]
+            deviation = there - jnp.mean(there, axis=0, keepdims=True)
+            high, low = split_two(deviation)
+            covariance = jnp.dot(
+                upright[:, : 3 * members],
+                jnp.concatenate([high, low, high], axis=0),
+                preferred_element_type=F32,
+            )
+            high, low = split_two(covariance * taper_ref[at])
+            row = held * batches + at
+            change = jnp.dot(
+                factor_rows(increment * weights[row : row + 1, :]),
+                jnp.concatenate([high, low], axis=0),
+                preferred_element_type=F32,
+            )
+            prior_ref[later] = there + (change[:members] + change[members:])
+
+
+def update_body(
+    a_ref, w_ref, x_ref, y_ref, *refs, first, depth, tile_rows, parts, inverse
+):
     sources, targets, scratch = refs[: parts[0]], refs[parts[0] : sum(parts)], refs[-1]
     members, rows, cols = scratch.shape
     batches, nobs, _ = x_ref.shape
@@ -229,8 +225,15 @@
     if len(sources) > 1:
         from_ref = scratch
         held = members // len(sources)
+        folds = cols // nobs
         for slot, source in enumerate(sources):
-            from_ref[pl.ds(held * (row_at ^ slot), held)] = source[...]
+            for m in range(held):
+                for fold in range(folds):
+                    at = (m * folds + fold) * depth + pl.program_id(0) * rows
+                    lanes = slice(fold * nobs, (fold + 1) * nobs)
+                    from_ref[held * (row_at ^ slot) + m, :, lanes] = source[
+                        pl.ds(pl.multiple_of(at, rows), rows), :
+                    ]
     if len(targets) > 1:
         to_ref = scratch
     states = [from_ref[:, r, :] for r in range(rows)]
@@ -265,10 +268,8 @@
     return pl.BlockSpec(array.shape, lambda i: (0,) * array.ndim)
 
 
-def update(sources, tables, first, depth, tile_rows, parts, inverse):
-    held, _, cols = sources[0].shape
-    members = held * len(sources)
-    rows = ROWS
+def update(sources, tables, first, depth, tile_rows, tile_cols, members, parts, inverse):
+    rows, cols = ROWS, tile_cols
     batches, nobs = tables[0].shape[:2]
     cells = depth * cols * batches * nobs
     out = members // parts
@@ -276,13 +277,18 @@
         functools.partial(
             update_body,
             first=first,
+            depth=depth,
             tile_rows=tile_rows,
             parts=(len(sources), parts),
             inverse=inverse,
         ),
         grid=(depth // rows,),
         in_specs=[whole(table) for table in tables]
-        + [pl.BlockSpec((held, rows, cols), lambda i: (0, i, 0))] * len(sources),
+        + (
+            [whole(source) for source in sources]
+            if len(sources) > 1
+            else [pl.BlockSpec((members, rows, cols), lambda i: (0, i, 0))]
+        ),
         out_specs=[pl.BlockSpec((out, rows, cols), lambda i: (0, i, 0))] * parts,
         out_shape=[jax.ShapeDtypeStruct((out, depth, cols), F32)] * parts,
         scratch_shapes=[pltpu.VMEM((members, rows, cols), F32)],
@@ -326,18 +332,18 @@
     members = held * gx_count
     tile_rows = all_rows // gx_count
     batches, nobs = obs_cells.shape
+    first = tile_rows * FIRST_EIGHTHS // 8
+    rest = tile_rows - first
     inverse = 1.0 / (all_rows // 4)
     weight = tile_weight[:, :, 0, 0]
     payload = held * batches + len(pairs_of(batches))
-    deep = -(-payload // (8 * held)) * 8
-    payload = held * deep
+    payload = -(-payload // 8) * 8
+    state_rows = held * (tile_cols // nobs) * first
     in_smem = pl.BlockSpec(memory_space=SMEM)
     in_vmem = pl.BlockSpec(memory_space=VMEM)
     in_hbm = pl.BlockSpec(memory_space=pltpu.MemorySpace.HBM)
     geometry = dict(tile_rows=tile_rows, tile_cols=tile_cols, gy_count=gy_count, inverse=inverse)
 
-    first = tile_rows * FIRST_EIGHTHS // 8
-    rest = tile_rows - first
     blocks, *pieces = pl.pallas_call(
         functools.partial(
             pick_body, tile_rows=tile_rows, first=first, gx_count=gx_count, gy_count=gy_count
@@ -345,7 +351,7 @@
         in_specs=[in_hbm] * 4,
         out_specs=[in_hbm] + [in_vmem] * gx_count,
         out_shape=[jax.ShapeDtypeStruct((gx_count, held, rest, tile_cols), F32)]
-        + [jax.ShapeDtypeStruct((held, first + deep, tile_cols), F32)] * gx_count,
+        + [jax.ShapeDtypeStruct((state_rows + payload, nobs), F32)] * gx_count,
         scratch_shapes=[
             pltpu.VMEM((gx_count, held, tile_rows, tile_cols), F32),
             pltpu.VMEM((payload, nobs), F32),
@@ -361,24 +367,25 @@
     for slot in range(1, gx_count):
         pieces[slot] = lax.ppermute(pieces[slot], "gx", [(i, i ^ slot) for i in range(gx_count)])
     state = lax.all_to_all(blocks, "gx", split_axis=0, concat_axis=0, tiled=True)
-    places = pl.pallas_call(
+    *places, tapers = pl.pallas_call(
         functools.partial(tables_body, **geometry),
         in_specs=[in_smem, in_vmem],
-        out_specs=[in_vmem] * 2,
+        out_specs=[in_vmem] * 3,
         out_shape=[
             jax.ShapeDtypeStruct((batches, nobs, nobs), F32),
             jax.ShapeDtypeStruct((batches, nobs, tile_cols), F32),
+            jax.ShapeDtypeStruct((len(pairs_of(batches)), nobs, nobs), F32),
         ],
         compiler_params=LIGHT,
         name="tables",
     )(owner_device, obs_cells)
-    got = [jnp.stack([piece[:, first:, :nobs].reshape(payload, nobs) for piece in pieces])]
+    got = [jnp.stack([piece[state_rows:] for piece in pieces])]
     for step in range(1, gy_count):
         got.append(lax.ppermute(got[0], "gy", [(i, i ^ step) for i in range(gy_count)]))
     wide = -(-3 * members // nobs) * nobs
     chain = pl.pallas_call(
-        functools.partial(chain_body, held=held, gx_count=gx_count, **geometry),
-        in_specs=[in_smem] + [in_vmem] * (4 + gy_count),
+        functools.partial(chain_body, held=held, gx_count=gx_count, gy_count=gy_count),
+        in_specs=[in_vmem] * (4 + gy_count),
         out_specs=[in_vmem] * 2,
         out_shape=[
             jax.ShapeDtypeStruct((batches, nobs, wide), BF16),
@@ -388,10 +395,11 @@
         compiler_params=LIGHT,
         name="chain",
     )
-    factors = chain(owner_device, obs_cells, obs_values, obs_error, weight, *got)
+    factors = chain(obs_values, obs_error, weight, tapers, *got)
     tables = [*factors, *places]
 
-    (upper,) = update(pieces, tables, 0, first, tile_rows, 1, inverse)
+    shape = (tile_rows, tile_cols, members)
+    (upper,) = update(pieces, tables, 0, first, *shape, 1, inverse)
     upper = lax.all_to_all(
         upper.reshape(gx_count, held, first, tile_cols),
         "gx",
@@ -400,7 +408,7 @@
         tiled=True,
     )
     state = state.reshape(members, rest, tile_cols)
-    lower = [*update([state], tables, first, rest, tile_rows, gx_count, inverse)]
+    lower = [*update([state], tables, first, rest, *shape, gx_count, inverse)]
     for slot in range(1, gx_count):
         lower[slot] = lax.ppermute(
             lower[slot], "gx", [(i, i ^ slot) for i in range(gx_count)]

time: 85.3 us -> 83.3 us (0.977)
  starting transfers between devices: 41 us -> 40 us
  transfers between devices with their start and end apart: 19 -> 19, of which waited for: 6 -> 6; matrix products, arithmetic and copies ran while one was open for 0% -> 0% of each run, Pallas kernels for 20% -> 19%
where the time goes in v6:
time: 83.3 us; the launch traced here: 82.8 us
  starting transfers between devices  40 us (48%)
  waiting for transfers between devices  22.2 us (27%)
  Pallas kernels  20.4 us (24%)
    ppermute x7, starting transfers between devices, local(): lax.ppermute(pieces[slot], 'gx', [(i, i ^ slot) for i in range(gx_count)])  16 us
    pallas_call x2, Pallas kernels, update(): pl.pallas_call(functools.partial(update_body, first=first, depth=depth, t...  13.8 us
    ppermute x7, starting transfers between devices, local(): lax.ppermute(lower[slot], 'gx', [(i, i ^ slot) for i in range(gx_count)])  11.2 us
    ppermute x7, waiting for transfers between devices, local(): lax.ppermute(pieces[slot], 'gx', [(i, i ^ slot) for i in range(gx_count)])  10.6 us
    ppermute x7, waiting for transfers between devices, local(): lax.ppermute(lower[slot], 'gx', [(i, i ^ slot) for i in range(gx_count)])  8.43 us
    all_to_all x1, starting transfers between devices, local(): lax.all_to_all(blocks, 'gx', split_axis=0, concat_axis=0, tiled=True)  7.43 us
    all_to_all x1, starting transfers between devices, local(): lax.all_to_all(upper.reshape(gx_count, held, first, tile_cols), 'gx', spl...  3.45 us
    pallas_call x1, Pallas kernels, local(): pl.pallas_call(functools.partial(pick_body, tile_rows=tile_rows, first=fi...  3.44 us
  transfers between devices with their start and end apart: 19, of which 6 were waited for; matrix products, arithmetic and copies ran while one was open for 0% of the time, Pallas kernels for 19%

profile of v6, /device:TPU:0, one launch (start us, length us, event | category | flops | bytes accessed | tf_op | source)
XLA Modules:
  0.0 82.8 jit_solution(3146599673847410399)
XLA Ops:
  0.0 3.4 %pick.1 = (f32[8,2,40,256]{3,2,1,0:T(8,128)}, f32[112,128]{1,0:T(8,128)}, f32[112,128]{1,0:T(8,128)}, f32[112,128]{1,0:T(8,128)}, f32[112,128]{1,0:T(8,128)}, /*...) custom-call(s32[4]{0:T(128)} %owner_in.1, s32[4,128]{1,0:T(4,128)} %cells_in.1, ...), custom_call_target="tpu_custom_call" | custom-call | tf_op jit(solution)/shard_map/pick/pallas_call | solution.py:347
  3.5 7.4 %all-to-all-start.1 = ((f32[8,2,40,256]{3,2,1,0:T(8,128)}), f32[8,2,40,256]{3,2,1,0:T(8,128)S(1)}, u32[]{:S(2)}, u32[]{:S(2)}) async-start(f32[8,2,40,256]{3,2,1,0:T(8,128)} %get-tuple-element.40), calls=%async_computation.1 | async-start | bytes 1310720 | tf_op jit(solution)/shard_map/all_to_all | solution.py:369
  11.0 2.0 %collective-permute-start = (f32[112,128]{1,0:T(8,128)S(1)}, f32[112,128]{1,0:T(8,128)S(1)}, u32[]{:S(2)}, u32[]{:S(2)}) collective-permute-start(f32[112,128]{1,0:T(8,128)S(1)} %copy-done.12), channel_id=1, source_target_pairs={{0,4},{4,0},{8,12},{12,8},{16,20},{20,16},{24,28},{28,24},{1,5},{5... | collective-permute-start | bytes 172040 | tf_op jit(solution)/shard_map/ppermute | solution.py:368
  13.0 1.5 %collective-permute-start.1 = (f32[112,128]{1,0:T(8,128)S(1)}, f32[112,128]{1,0:T(8,128)S(1)}, u32[]{:S(2)}, u32[]{:S(2)}) collective-permute-start(f32[112,128]{1,0:T(8,128)S(1)} %copy-done.11), channel_id=1, source_target_pairs={{0,8},{4,12},{8,0},{12,4},{16,24},{20,28},{24,16},{28,20},{1,9},{5... | collective-permute-start | bytes 172040 | tf_op jit(solution)/shard_map/ppermute | solution.py:368
  14.5 2.8 %collective-permute-start.3 = (f32[112,128]{1,0:T(8,128)S(1)}, f32[112,128]{1,0:T(8,128)S(1)}, u32[]{:S(2)}, u32[]{:S(2)}) collective-permute-start(f32[112,128]{1,0:T(8,128)S(1)} %copy-done.9), channel_id=1, source_target_pairs={{0,16},{4,20},{8,24},{12,28},{16,0},{20,4},{24,8},{28,12},{1,17},{... | collective-permute-start | bytes 172040 | tf_op jit(solution)/shard_map/ppermute | solution.py:368
  17.4 1.5 %collective-permute-start.4 = (f32[112,128]{1,0:T(8,128)S(1)}, f32[112,128]{1,0:T(8,128)S(1)}, u32[]{:S(2)}, u32[]{:S(2)}) collective-permute-start(f32[112,128]{1,0:T(8,128)S(1)} %copy-done.8), channel_id=1, source_target_pairs={{0,20},{4,16},{8,28},{12,24},{16,4},{20,0},{24,12},{28,8},{1,21},{... | collective-permute-start | bytes 172040 | tf_op jit(solution)/shard_map/ppermute | solution.py:368
  18.9 3.3 %collective-permute-start.5 = (f32[112,128]{1,0:T(8,128)S(1)}, f32[112,128]{1,0:T(8,128)S(1)}, u32[]{:S(2)}, u32[]{:S(2)}) collective-permute-start(f32[112,128]{1,0:T(8,128)S(1)} %copy-done.7), channel_id=1, source_target_pairs={{0,24},{4,28},{8,16},{12,20},{16,8},{20,12},{24,0},{28,4},{1,25},{... | collective-permute-start | bytes 172040 | tf_op jit(solution)/shard_map/ppermute | solution.py:368
  22.2 1.8 %collective-permute-done.1.refs_2_ = f32[112,128]{1,0:T(8,128)S(1)} collective-permute-done((f32[112,128]{1,0:T(8,128)S(1)}, f32[112,128]{1,0:T(8,128)S(1)}, u32[]{:S(2)}, u32[]{:S(2)}) %collective-permute-start.1) | collective-permute-done | bytes 57376 | tf_op jit(solution)/shard_map/ppermute | solution.py:368
  24.0 4.8 %collective-permute-start.6 = (f32[112,128]{1,0:T(8,128)S(1)}, f32[112,128]{1,0:T(8,128)S(1)}, u32[]{:S(2)}, u32[]{:S(2)}) collective-permute-start(f32[112,128]{1,0:T(8,128)S(1)} %copy-done.6), channel_id=1, source_target_pairs={{0,28},{4,24},{8,20},{12,16},{16,12},{20,8},{24,4},{28,0},{1,29},{... | collective-permute-start | bytes 172040 | tf_op jit(solution)/shard_map/ppermute | solution.py:368
  28.8 7.0 %collective-permute-done.3.refs_4_ = f32[112,128]{1,0:T(8,128)S(1)} collective-permute-done((f32[112,128]{1,0:T(8,128)S(1)}, f32[112,128]{1,0:T(8,128)S(1)}, u32[]{:S(2)}, u32[]{:S(2)}) %collective-permute-start.3) | collective-permute-done | bytes 57376 | tf_op jit(solution)/shard_map/ppermute | solution.py:368
  35.8 1.7 %collective-permute-done.4.refs_5_ = f32[112,128]{1,0:T(8,128)S(1)} collective-permute-done((f32[112,128]{1,0:T(8,128)S(1)}, f32[112,128]{1,0:T(8,128)S(1)}, u32[]{:S(2)}, u32[]{:S(2)}) %collective-permute-start.4) | collective-permute-done | bytes 57376 | tf_op jit(solution)/shard_map/ppermute | solution.py:368
  37.7 1.6 %collective-permute-start.8 = (f32[8,16,128]{2,1,0:T(8,128)S(1)}, f32[8,16,128]{2,1,0:T(8,128)S(1)}, u32[]{:S(2)}, u32[]{:S(2)}) collective-permute-start(f32[8,16,128]{2,1,0:T(8,128)S(1)} %constant_dynamic-update-slice_fusion.refs_0_), channel_id=1, source_target_pairs={{0,2},{1,3},{2,0},{3,1},{4,6},{5,7},{6,4},{7,5},{8,10},{9,11},{10,... | collective-permute-start | bytes 196616 | tf_op jit(solution)/shard_map/ppermute | solution.py:384
  40.3 1.7 %collective-permute-done.9.refs_3_ = f32[8,16,128]{2,1,0:T(8,128)S(1)} collective-permute-done((f32[8,16,128]{2,1,0:T(8,128)S(1)}, f32[8,16,128]{2,1,0:T(8,128)S(1)}, u32[]{:S(2)}, u32[]{:S(2)}) %collective-permute-start.9) | collective-permute-done | bytes 65568 | tf_op jit(solution)/shard_map/ppermute | solution.py:384
  42.0 1.5 %collective-permute-done.8.refs_2_ = f32[8,16,128]{2,1,0:T(8,128)S(1)} collective-permute-done((f32[8,16,128]{2,1,0:T(8,128)S(1)}, f32[8,16,128]{2,1,0:T(8,128)S(1)}, u32[]{:S(2)}, u32[]{:S(2)}) %collective-permute-start.8) | collective-permute-done | bytes 65568 | tf_op jit(solution)/shard_map/ppermute | solution.py:384
  43.5 1.3 %chain.1 = (bf16[4,128,128]{2,1,0:T(8,128)(2,1)S(1)}, bf16[4,32,256]{2,1,0:T(8,128)(2,1)S(1)}) custom-call(f32[4,128]{1,0:T(4,128)S(1)} %copy-done.2, f32[4,128]{1,0:T(4,128)S(1)} %copy-done.3, f32[4,128]{1,0:T(4,128)S(1)} %bitcast.35, f32[6,128,128]{2,1,0:T(8,128)S(1)} %get-tuple-element.27.taper_ref, ...), custom_call_target="tpu_custom_call" | custom-call | tf_op jit(solution)/shard_map/chain/pallas_call | solution.py:398
  44.8 5.5 %update.2 = f32[16,24,256]{2,1,0:T(8,128)} custom-call(bf16[4,128,128]{2,1,0:T(8,128)(2,1)S(1)} %get-tuple-element.36.a_ref, bf16[4,32,256]{2,1,0:T(8,128)(2,1)S(1)} %get-tuple-element.37.w_ref, f32[4,128,128]{2,1,0:T(8,128)S(1)} %get-tuple-element.38.x_ref, f32[4,128,256]{2,1,0:T(8,128)S(1)} %get-tuple-element.39.y_ref, f32[112,128]{1,0:T(8,128)S(1)} %copy-done.5, ...), custom_call_target="tpu_custom_call" | custom-call | flops 503316480 | bytes 786432 | tf_op jit(solution)/shard_map/update/pallas_call | solution.py:276
  50.3 3.5 %all-to-all-start = ((f32[8,2,24,256]{3,2,1,0:T(8,128)}), f32[8,2,24,256]{3,2,1,0:T(8,128)S(1)}, u32[]{:S(2)}, u32[]{:S(2)}) async-start(f32[8,2,24,256]{3,2,1,0:T(8,128)} %bitcast.9), calls=%async_computation | async-start | bytes 786432 | tf_op jit(solution)/shard_map/all_to_all | solution.py:403
  53.8 8.3 %update.3 = (f32[2,40,256]{2,1,0:T(8,128)S(1)}, f32[2,40,256]{2,1,0:T(8,128)S(1)}, f32[2,40,256]{2,1,0:T(8,128)S(1)}, f32[2,40,256]{2,1,0:T(8,128)S(1)}, f32[2,4...) custom-call(bf16[4,128,128]{2,1,0:T(8,128)(2,1)S(1)} %get-tuple-element.3, ...), custom_call_target="tpu_custom_call" | custom-call | flops 838860800 | bytes 1310720 | tf_op jit(solution)/shard_map/update/pallas_call | solution.py:276
  62.1 2.0 %collective-permute-start.10 = (f32[2,40,256]{2,1,0:T(8,128)S(1)}, f32[2,40,256]{2,1,0:T(8,128)S(1)}, u32[]{:S(2)}, u32[]{:S(2)}) collective-permute-start(f32[2,40,256]{2,1,0:T(8,128)S(1)} %get-tuple-element.42), channel_id=1, source_target_pairs={{0,4},{4,0},{8,12},{12,8},{16,20},{20,16},{24,28},{28,24},{1,5},{5... | collective-permute-start | bytes 245768 | tf_op jit(solution)/shard_map/ppermute | solution.py:413
  64.0 1.5 %collective-permute-start.11 = (f32[2,40,256]{2,1,0:T(8,128)S(1)}, f32[2,40,256]{2,1,0:T(8,128)S(1)}, u32[]{:S(2)}, u32[]{:S(2)}) collective-permute-start(f32[2,40,256]{2,1,0:T(8,128)S(1)} %get-tuple-element.43), channel_id=1, source_target_pairs={{0,8},{4,12},{8,0},{12,4},{16,24},{20,28},{24,16},{28,20},{1,9},{5... | collective-permute-start | bytes 245768 | tf_op jit(solution)/shard_map/ppermute | solution.py:413
  65.6 2.8 %collective-permute-start.13 = (f32[2,40,256]{2,1,0:T(8,128)S(1)}, f32[2,40,256]{2,1,0:T(8,128)S(1)}, u32[]{:S(2)}, u32[]{:S(2)}) collective-permute-start(f32[2,40,256]{2,1,0:T(8,128)S(1)} %get-tuple-element.45), channel_id=1, source_target_pairs={{0,16},{4,20},{8,24},{12,28},{16,0},{20,4},{24,8},{28,12},{1,17},{... | collective-permute-start | bytes 245768 | tf_op jit(solution)/shard_map/ppermute | solution.py:413
  68.5 1.4 %collective-permute-start.14 = (f32[2,40,256]{2,1,0:T(8,128)S(1)}, f32[2,40,256]{2,1,0:T(8,128)S(1)}, u32[]{:S(2)}, u32[]{:S(2)}) collective-permute-start(f32[2,40,256]{2,1,0:T(8,128)S(1)} %get-tuple-element.46), channel_id=1, source_target_pairs={{0,20},{4,16},{8,28},{12,24},{16,4},{20,0},{24,12},{28,8},{1,21},{... | collective-permute-start | bytes 245768 | tf_op jit(solution)/shard_map/ppermute | solution.py:413
  69.9 3.3 %collective-permute-start.15 = (f32[2,40,256]{2,1,0:T(8,128)S(1)}, f32[2,40,256]{2,1,0:T(8,128)S(1)}, u32[]{:S(2)}, u32[]{:S(2)}) collective-permute-start(f32[2,40,256]{2,1,0:T(8,128)S(1)} %get-tuple-element.47), channel_id=1, source_target_pairs={{0,24},{4,28},{8,16},{12,20},{16,8},{20,12},{24,0},{28,4},{1,25},{... | collective-permute-start | bytes 245768 | tf_op jit(solution)/shard_map/ppermute | solution.py:413
  73.3 8.4 %collective-permute-done.14.refs_5_ = f32[2,40,256]{2,1,0:T(8,128)S(1)} collective-permute-done((f32[2,40,256]{2,1,0:T(8,128)S(1)}, f32[2,40,256]{2,1,0:T(8,128)S(1)}, u32[]{:S(2)}, u32[]{:S(2)}) %collective-permute-start.14) | collective-permute-done | bytes 81952 | tf_op jit(solution)/shard_map/ppermute | solution.py:413
  (54 shorter events, 2.5 us)
Async XLA Ops:
  3.5 11.0 %copy-start.9 = (f32[112,128]{1,0:T(8,128)S(1)}, f32[112,128]{1,0:T(8,128)}, u32[]{:S(2)}) copy-start(f32[112,128]{1,0:T(8,128)} %get-tuple-element.32) | copy-start | bytes 172036
  3.5 13.9 %copy-start.8 = (f32[112,128]{1,0:T(8,128)S(1)}, f32[112,128]{1,0:T(8,128)}, u32[]{:S(2)}) copy-start(f32[112,128]{1,0:T(8,128)} %get-tuple-element.33) | copy-start | bytes 172036
  3.5 15.3 %copy-start.5 = (f32[112,128]{1,0:T(8,128)S(1)}, f32[112,128]{1,0:T(8,128)}, u32[]{:S(2)}) copy-start(f32[112,128]{1,0:T(8,128)} %get-tuple-element.28.refs_0_) | copy-start | bytes 172036
  3.5 15.3 %copy-start.7 = (f32[112,128]{1,0:T(8,128)S(1)}, f32[112,128]{1,0:T(8,128)}, u32[]{:S(2)}) copy-start(f32[112,128]{1,0:T(8,128)} %get-tuple-element.34) | copy-start | bytes 172036
  3.5 20.5 %copy-start.6 = (f32[112,128]{1,0:T(8,128)S(1)}, f32[112,128]{1,0:T(8,128)}, u32[]{:S(2)}) copy-start(f32[112,128]{1,0:T(8,128)} %get-tuple-element.35) | copy-start | bytes 172036
  3.5 46.8 %all-to-all-start.1 = ((f32[8,2,40,256]{3,2,1,0:T(8,128)}), f32[8,2,40,256]{3,2,1,0:T(8,128)S(1)}, u32[]{:S(2)}, u32[]{:S(2)}) async-start(f32[8,2,40,256]{3,2,1,0:T(8,128)} %get-tuple-element.40), calls=%async_computation.1 | async-start | bytes 1310720 | tf_op jit(solution)/shard_map/all_to_all | solution.py:369
  11.0 7.9 %collective-permute-start = (f32[112,128]{1,0:T(8,128)S(1)}, f32[112,128]{1,0:T(8,128)S(1)}, u32[]{:S(2)}, u32[]{:S(2)}) collective-permute-start(f32[112,128]{1,0:T(8,128)S(1)} %copy-done.12), channel_id=1, source_target_pairs={{0,4},{4,0},{8,12},{12,8},{16,20},{20,16},{24,28},{28,24},{1,5},{5... | collective-permute-start | bytes 172040 | tf_op jit(solution)/shard_map/ppermute | solution.py:368
  13.0 11.0 %collective-permute-start.1 = (f32[112,128]{1,0:T(8,128)S(1)}, f32[112,128]{1,0:T(8,128)S(1)}, u32[]{:S(2)}, u32[]{:S(2)}) collective-permute-start(f32[112,128]{1,0:T(8,128)S(1)} %copy-done.11), channel_id=1, source_target_pairs={{0,8},{4,12},{8,0},{12,4},{16,24},{20,28},{24,16},{28,20},{1,9},{5... | collective-permute-start | bytes 172040 | tf_op jit(solution)/shard_map/ppermute | solution.py:368
  14.4 14.3 %collective-permute-start.2 = (f32[112,128]{1,0:T(8,128)S(1)}, f32[112,128]{1,0:T(8,128)S(1)}, u32[]{:S(2)}, u32[]{:S(2)}) collective-permute-start(f32[112,128]{1,0:T(8,128)S(1)} %copy-done.10), channel_id=1, source_target_pairs={{0,12},{4,8},{8,4},{12,0},{16,28},{20,24},{24,20},{28,16},{1,13},{... | collective-permute-start | bytes 172040 | tf_op jit(solution)/shard_map/ppermute | solution.py:368
  14.5 21.3 %collective-permute-start.3 = (f32[112,128]{1,0:T(8,128)S(1)}, f32[112,128]{1,0:T(8,128)S(1)}, u32[]{:S(2)}, u32[]{:S(2)}) collective-permute-start(f32[112,128]{1,0:T(8,128)S(1)} %copy-done.9), channel_id=1, source_target_pairs={{0,16},{4,20},{8,24},{12,28},{16,0},{20,4},{24,8},{28,12},{1,17},{... | collective-permute-start | bytes 172040 | tf_op jit(solution)/shard_map/ppermute | solution.py:368
  17.4 20.1 %collective-permute-start.4 = (f32[112,128]{1,0:T(8,128)S(1)}, f32[112,128]{1,0:T(8,128)S(1)}, u32[]{:S(2)}, u32[]{:S(2)}) collective-permute-start(f32[112,128]{1,0:T(8,128)S(1)} %copy-done.8), channel_id=1, source_target_pairs={{0,20},{4,16},{8,28},{12,24},{16,4},{20,0},{24,12},{28,8},{1,21},{... | collective-permute-start | bytes 172040 | tf_op jit(solution)/shard_map/ppermute | solution.py:368
  18.9 18.7 %collective-permute-start.5 = (f32[112,128]{1,0:T(8,128)S(1)}, f32[112,128]{1,0:T(8,128)S(1)}, u32[]{:S(2)}, u32[]{:S(2)}) collective-permute-start(f32[112,128]{1,0:T(8,128)S(1)} %copy-done.7), channel_id=1, source_target_pairs={{0,24},{4,28},{8,16},{12,20},{16,8},{20,12},{24,0},{28,4},{1,25},{... | collective-permute-start | bytes 172040 | tf_op jit(solution)/shard_map/ppermute | solution.py:368
  24.0 13.5 %collective-permute-start.6 = (f32[112,128]{1,0:T(8,128)S(1)}, f32[112,128]{1,0:T(8,128)S(1)}, u32[]{:S(2)}, u32[]{:S(2)}) collective-permute-start(f32[112,128]{1,0:T(8,128)S(1)} %copy-done.6), channel_id=1, source_target_pairs={{0,28},{4,24},{8,20},{12,16},{16,12},{20,8},{24,4},{28,0},{1,29},{... | collective-permute-start | bytes 172040 | tf_op jit(solution)/shard_map/ppermute | solution.py:368
  37.6 4.4 %collective-permute-start.9 = (f32[8,16,128]{2,1,0:T(8,128)S(1)}, f32[8,16,128]{2,1,0:T(8,128)S(1)}, u32[]{:S(2)}, u32[]{:S(2)}) collective-permute-start(f32[8,16,128]{2,1,0:T(8,128)S(1)} %constant_dynamic-update-slice_fusion.refs_0_), channel_id=1, source_target_pairs={{0,3},{1,2},{2,1},{3,0},{4,7},{5,6},{6,5},{7,4},{8,11},{9,10},{10,... | collective-permute-start | bytes 196616 | tf_op jit(solution)/shard_map/ppermute | solution.py:384
  37.7 5.8 %collective-permute-start.8 = (f32[8,16,128]{2,1,0:T(8,128)S(1)}, f32[8,16,128]{2,1,0:T(8,128)S(1)}, u32[]{:S(2)}, u32[]{:S(2)}) collective-permute-start(f32[8,16,128]{2,1,0:T(8,128)S(1)} %constant_dynamic-update-slice_fusion.refs_0_), channel_id=1, source_target_pairs={{0,2},{1,3},{2,0},{3,1},{4,6},{5,7},{6,4},{7,5},{8,10},{9,11},{10,... | collective-permute-start | bytes 196616 | tf_op jit(solution)/shard_map/ppermute | solution.py:384
  39.3 4.2 %collective-permute-start.7 = (f32[8,16,128]{2,1,0:T(8,128)S(1)}, f32[8,16,128]{2,1,0:T(8,128)S(1)}, u32[]{:S(2)}, u32[]{:S(2)}) collective-permute-start(f32[8,16,128]{2,1,0:T(8,128)S(1)} %constant_dynamic-update-slice_fusion.refs_0_), channel_id=1, source_target_pairs={{0,1},{1,0},{2,3},{3,2},{4,5},{5,4},{6,7},{7,6},{8,9},{9,8},{10,11... | collective-permute-start | bytes 196616 | tf_op jit(solution)/shard_map/ppermute | solution.py:384
  50.3 23.0 %all-to-all-start = ((f32[8,2,24,256]{3,2,1,0:T(8,128)}), f32[8,2,24,256]{3,2,1,0:T(8,128)S(1)}, u32[]{:S(2)}, u32[]{:S(2)}) async-start(f32[8,2,24,256]{3,2,1,0:T(8,128)} %bitcast.9), calls=%async_computation | async-start | bytes 786432 | tf_op jit(solution)/shard_map/all_to_all | solution.py:403
  62.1 7.8 %collective-permute-start.10 = (f32[2,40,256]{2,1,0:T(8,128)S(1)}, f32[2,40,256]{2,1,0:T(8,128)S(1)}, u32[]{:S(2)}, u32[]{:S(2)}) collective-permute-start(f32[2,40,256]{2,1,0:T(8,128)S(1)} %get-tuple-element.42), channel_id=1, source_target_pairs={{0,4},{4,0},{8,12},{12,8},{16,20},{20,16},{24,28},{28,24},{1,5},{5... | collective-permute-start | bytes 245768 | tf_op jit(solution)/shard_map/ppermute | solution.py:413
  64.0 9.2 %collective-permute-start.11 = (f32[2,40,256]{2,1,0:T(8,128)S(1)}, f32[2,40,256]{2,1,0:T(8,128)S(1)}, u32[]{:S(2)}, u32[]{:S(2)}) collective-permute-start(f32[2,40,256]{2,1,0:T(8,128)S(1)} %get-tuple-element.43), channel_id=1, source_target_pairs={{0,8},{4,12},{8,0},{12,4},{16,24},{20,28},{24,16},{28,20},{1,9},{5... | collective-permute-start | bytes 245768 | tf_op jit(solution)/shard_map/ppermute | solution.py:413
  65.5 7.8 %collective-permute-start.12 = (f32[2,40,256]{2,1,0:T(8,128)S(1)}, f32[2,40,256]{2,1,0:T(8,128)S(1)}, u32[]{:S(2)}, u32[]{:S(2)}) collective-permute-start(f32[2,40,256]{2,1,0:T(8,128)S(1)} %get-tuple-element.44), channel_id=1, source_target_pairs={{0,12},{4,8},{8,4},{12,0},{16,28},{20,24},{24,20},{28,16},{1,13},{... | collective-permute-start | bytes 245768 | tf_op jit(solution)/shard_map/ppermute | solution.py:413
  65.6 7.7 %collective-permute-start.13 = (f32[2,40,256]{2,1,0:T(8,128)S(1)}, f32[2,40,256]{2,1,0:T(8,128)S(1)}, u32[]{:S(2)}, u32[]{:S(2)}) collective-permute-start(f32[2,40,256]{2,1,0:T(8,128)S(1)} %get-tuple-element.45), channel_id=1, source_target_pairs={{0,16},{4,20},{8,24},{12,28},{16,0},{20,4},{24,8},{28,12},{1,17},{... | collective-permute-start | bytes 245768 | tf_op jit(solution)/shard_map/ppermute | solution.py:413
  68.5 13.3 %collective-permute-start.14 = (f32[2,40,256]{2,1,0:T(8,128)S(1)}, f32[2,40,256]{2,1,0:T(8,128)S(1)}, u32[]{:S(2)}, u32[]{:S(2)}) collective-permute-start(f32[2,40,256]{2,1,0:T(8,128)S(1)} %get-tuple-element.46), channel_id=1, source_target_pairs={{0,20},{4,16},{8,28},{12,24},{16,4},{20,0},{24,12},{28,8},{1,21},{... | collective-permute-start | bytes 245768 | tf_op jit(solution)/shard_map/ppermute | solution.py:413
  69.9 11.8 %collective-permute-start.15 = (f32[2,40,256]{2,1,0:T(8,128)S(1)}, f32[2,40,256]{2,1,0:T(8,128)S(1)}, u32[]{:S(2)}, u32[]{:S(2)}) collective-permute-start(f32[2,40,256]{2,1,0:T(8,128)S(1)} %get-tuple-element.47), channel_id=1, source_target_pairs={{0,24},{4,28},{8,16},{12,20},{16,8},{20,12},{24,0},{28,4},{1,25},{... | collective-permute-start | bytes 245768 | tf_op jit(solution)/shard_map/ppermute | solution.py:413
  73.2 8.5 %collective-permute-start.16 = (f32[2,40,256]{2,1,0:T(8,128)S(1)}, f32[2,40,256]{2,1,0:T(8,128)S(1)}, u32[]{:S(2)}, u32[]{:S(2)}) collective-permute-start(f32[2,40,256]{2,1,0:T(8,128)S(1)} %get-tuple-element.48), channel_id=1, source_target_pairs={{0,28},{4,24},{8,20},{12,16},{16,12},{20,8},{24,4},{28,0},{1,29},{... | collective-permute-start | bytes 245768 | tf_op jit(solution)/shard_map/ppermute | solution.py:413
  (8 other events, 49.7 us)
